TPU v7x, 256 devices: a whole 4x4x8 slice. The times are simulated.
256 devices in a mesh: layer: 2 (over core), prow: 4 (over x), pcol: 32 (over y, z).
Axes of the slice: x: 4, y: 4, z: 8, core: 2. Of those that a mesh axis runs over, the one named last changes fastest.
Arguments:
- right_sub: float32 [14, 64, 4096], P('layer', None, 'prow'), may hold values from -3 to 3
- right_root: float32 [64, 4096], P(None, 'prow'), may hold values from -3 to 3
- inverse_sub: bfloat16 [14, 4096, 4096], P('layer', 'prow', 'pcol'), as said below
- inverse_root: bfloat16 [4096, 4096], P('prow', 'pcol')
- factor_blocks: bfloat16 [34, 4096, 2048], P('layer', 'pcol', 'prow'), may hold values from -0.046875 to 0.046875
- block_lists: int32 [34, 8], P('layer', 'prow'), may hold values from 0 to 15, all different within a row
Outputs:
- solution_sub: float32 [14, 64, 4096], P('layer', None, 'prow')
- solution_root: float32 [64, 4096], P(None, 'prow')
Inputs may be any that keep to these rules, and one draw needn't show every extreme that they name: `block_lists`: each row names 8 different block rows of its ancestor. inverse_sub and inverse_root are upper triangular (the transpose of a lower-triangular inverse, zero below the diagonal) and well conditioned.
All inputs are finite; a program needn't handle non-finite values.
Results may differ from a plain program's by a relative error of at most 0.009.
Values may be sent and summed in bfloat16 or wider, within the bound.
No kernel may reach another device: no remote copies, remote signals or barrier semaphores. Data moves between devices by JAX's collectives and lax.ppermute only.
A program may use at most 128 MiB of HBM per device.

v0:
```python
import jax
import jax.numpy as jnp
from jax import lax
from jax.sharding import PartitionSpec as P

W = 256
NB = 16
NODES = 7
M = 4096


def tree_pairs():
    listing = []
    for node_index in range(NODES):
        ancestry = []
        walker = node_index
        while walker > 0:
            walker = (walker - 1) // 2
            ancestry.append(walker)
        listing.append((node_index, -1))
        for above in reversed(ancestry):
            listing.append((node_index, above))
    return listing


def level_range(level_now):
    return (2 ** (level_now - 1) - 1, 2**level_now - 1)


def spread_blocks(update, selector):
    rows_count = update.shape[0]
    blocked = update.reshape(rows_count, selector.shape[0], W)
    spread = jnp.einsum("rkw,kn->rnw", blocked, selector, precision=lax.Precision.HIGHEST)
    return spread.reshape(rows_count, NB * W)


def pick_blocks(values, selector):
    rows_count = values.shape[0]
    blocked = values.reshape(rows_count, NB, W)
    picked = jnp.einsum(
        "rnw,kn->rkw", blocked, selector.astype(jnp.bfloat16), preferred_element_type=jnp.float32
    )
    return picked.astype(jnp.bfloat16).reshape(rows_count, selector.shape[0] * W)


def forward_solve(residual, inverse):
    partial_terms = jnp.einsum(
        "nrm,nmc->nrc", residual.astype(jnp.bfloat16), inverse, preferred_element_type=jnp.float32
    )
    return lax.psum(partial_terms, "prow")


def backward_solve(target, inverse):
    partial_terms = jnp.einsum(
        "nrc,nmc->nrm", target.astype(jnp.bfloat16), inverse, preferred_element_type=jnp.float32
    )
    return lax.psum(partial_terms, "pcol")


def combine_rows(pending):
    share = lax.psum_scatter(pending, "prow", scatter_dimension=2, tiled=True)
    return lax.psum(share, "pcol")


def collect_rows(values):
    return lax.all_gather(values, "prow", axis=2, tiled=True)


def per_device(right_sub, right_root, inverse_sub, inverse_root, factor_blocks, block_lists):
    listing = tree_pairs()
    rhs_count = right_sub.shape[1]
    selectors = (block_lists[:, :, None] == jnp.arange(NB, dtype=jnp.int32)[None, None, :]).astype(
        jnp.float32
    )
    pending = jnp.zeros((NODES, rhs_count, M), jnp.float32)
    pending_root = jnp.zeros((rhs_count, M), jnp.float32)
    forward_parts = {}
    for level_now in (3, 2, 1):
        first_node, last_node = level_range(level_now)
        if level_now == 3:
            residual = right_sub[first_node:last_node]
        else:
            residual = right_sub[first_node:last_node] - combine_rows(pending[first_node:last_node])
        solved = forward_solve(residual, inverse_sub[first_node:last_node])
        forward_parts[level_now] = solved
        rounded = solved.astype(jnp.bfloat16)
        for pair_index, (owner, above) in enumerate(listing):
            if first_node <= owner < last_node:
                update = jnp.dot(
                    rounded[owner - first_node],
                    factor_blocks[pair_index],
                    preferred_element_type=jnp.float32,
                )
                spread = spread_blocks(update, selectors[pair_index])
                if above < 0:
                    pending_root = pending_root + spread
                else:
                    pending = pending.at[above].add(spread)
    root_rows = combine_rows(pending_root[None])[0]
    root_total = lax.psum(root_rows, "layer")
    root_forward = forward_solve((right_root - root_total)[None], inverse_root[None])
    solution_root = backward_solve(root_forward, inverse_root[None])[0]
    full_values = {-1: collect_rows(solution_root.astype(jnp.bfloat16)[None])[0]}
    solution_parts = []
    for level_now in (1, 2, 3):
        first_node, last_node = level_range(level_now)
        terms = []
        for node_index in range(first_node, last_node):
            total = jnp.zeros((rhs_count, factor_blocks.shape[1]), jnp.float32)
            for pair_index, (owner, above) in enumerate(listing):
                if owner == node_index:
                    picked = pick_blocks(full_values[above], selectors[pair_index])
                    total = total + jnp.einsum(
                        "rk,ck->rc",
                        picked,
                        factor_blocks[pair_index],
                        preferred_element_type=jnp.float32,
                    )
            terms.append(total)
        lowered = lax.psum(jnp.stack(terms), "prow")
        solution = backward_solve(
            forward_parts[level_now] - lowered, inverse_sub[first_node:last_node]
        )
        solution_parts.append(solution)
        if level_now < 3:
            gathered = collect_rows(solution.astype(jnp.bfloat16))
            for node_index in range(first_node, last_node):
                full_values[node_index] = gathered[node_index - first_node]
    return (jnp.concatenate(solution_parts, 0), solution_root)


def solution(mesh):
    in_specs = (
        P("layer", None, "prow"),
        P(None, "prow"),
        P("layer", "prow", "pcol"),
        P("prow", "pcol"),
        P("layer", "pcol", "prow"),
        P("layer", "prow"),
    )
    out_specs = (P("layer", None, "prow"), P(None, "prow"))
    return jax.shard_map(
        per_device, mesh=mesh, in_specs=in_specs, out_specs=out_specs, check_vma=False
    )
```

profile of v0, /device:TPU:32, one launch (start us, length us, event | category | flops | bytes accessed | tf_op | source)
XLA Modules:
  0.0 1537.5 jit_solution(3919149610758943151)
XLA Ops:
  7.2 2.7 fusion.16
  12.1 47.7 %all-reduce.14.cloned.1.call-done = f32[4,64,128]{2,1,0:T(8,128)} async-done(((f32[4,64,128]{2,1,0:T(8,128)}), f32[4,64,128]{2,1,0:T(8,128)}) %all-reduce.14.cloned.1.call-update) | async-done | bytes 131088 | tf_op jit(solution)/shard_map/psum | solution.py:50
  67.9 2.4 add.210
  73.6 2.4 reshape.516
  79.3 2.4 reshape.517
  90.9 2.4 reshape.519
  96.6 2.4 reshape.520
  112.7 2.9 copy-done.1
  117.2 32.8 %reduce-scatter.4.cloned.1.call-done = f32[2,64,1024]{2,1,0:T(8,128)} async-done(((f32[2,64,4096]{2,1,0:T(8,128)}), f32[2,64,1024]{2,1,0:T(8,128)}) %reduce-scatter.4.cloned.1.call-update) | async-done | bytes 524304 | tf_op jit(solution)/shard_map/reduce_scatter | solution.py:61
  150.9 148.9 %all-reduce.16.cloned.1.call-done = f32[2,64,1024]{2,1,0:T(8,128)} async-done(((f32[2,64,1024]{2,1,0:T(8,128)}), f32[2,64,1024]{2,1,0:T(8,128)}) %all-reduce.16.cloned.1.call-update) | async-done | bytes 524304 | tf_op jit(solution)/shard_map/psum | solution.py:62
  303.1 43.4 %all-reduce.18.cloned.1.call-done = f32[2,64,128]{2,1,0:T(8,128)} async-done(((f32[2,64,128]{2,1,0:T(8,128)}), f32[2,64,128]{2,1,0:T(8,128)}) %all-reduce.18.cloned.1.call-update) | async-done | bytes 65552 | tf_op jit(solution)/shard_map/psum | solution.py:50
  352.9 3.0 fusion.7
  360.8 21.8 %reduce-scatter.6.cloned.1.call-done = f32[1,64,1024]{2,1,0:T(8,128)} async-done(((f32[1,64,4096]{2,1,0:T(8,128)}), f32[1,64,1024]{2,1,0:T(8,128)}) %reduce-scatter.6.cloned.1.call-update) | async-done | bytes 262160 | tf_op jit(solution)/shard_map/reduce_scatter | solution.py:61
  382.7 2.5 convolution_add_fusion.1
  385.2 144.1 %all-reduce.20.cloned.1.call-done = f32[1,64,1024]{2,1,0:T(8,128)} async-done(((f32[1,64,1024]{2,1,0:T(8,128)}), f32[1,64,1024]{2,1,0:T(8,128)}) %all-reduce.20.cloned.1.call-update) | async-done | bytes 262160 | tf_op jit(solution)/shard_map/psum | solution.py:62
  530.6 17.0 %psum.109 = f32[1,64,128]{2,1,0:T(8,128)S(1)} all-reduce(f32[1,64,128]{2,1,0:T(8,128)S(1)} %convolution_bitcast_fusion.14), channel_id=1, replica_groups=mesh['layer'=2,'prow'=4,'pcol'=32] {'prow'}, use_global_device_ids=true, to_apply=%region_6.0 | all-reduce | flops 8192 | bytes 65536 | tf_op jit(solution)/shard_map/psum | solution.py:50
  552.4 22.5 %reduce-scatter.8.cloned.1.call-done = f32[1,64,1024]{2,1,0:T(8,128)} async-done(((f32[1,64,4096]{2,1,0:T(8,128)}), f32[1,64,1024]{2,1,0:T(8,128)}) %reduce-scatter.8.cloned.1.call-update) | async-done | bytes 262160 | tf_op jit(solution)/shard_map/reduce_scatter | solution.py:61
  575.0 146.5 %all-reduce.22.cloned.1.call-done = f32[64,1024]{1,0:T(8,128)} async-done(((f32[64,1024]{1,0:T(8,128)}), f32[64,1024]{1,0:T(8,128)}) %all-reduce.22.cloned.1.call-update) | async-done | bytes 262160 | tf_op jit(solution)/shard_map/psum | solution.py:62
  721.5 29.5 %all-reduce.24.cloned.1.call-done = f32[64,1024]{1,0:T(8,128)} async-done(((f32[64,1024]{1,0:T(8,128)}), f32[64,1024]{1,0:T(8,128)}) %all-reduce.24.cloned.1.call-update) | async-done | bytes 262160 | tf_op jit(solution)/shard_map/psum | solution.py:100
  752.3 17.0 %psum.112 = bf16[1,64,128]{2,1,0:T(8,128)(2,1)S(1)} all-reduce(f32[1,64,128]{2,1,0:T(8,128)S(1)} %convolution_bitcast_fusion.13), channel_id=1, replica_groups=mesh['layer'=2,'prow'=4,'pcol'=32] {'prow'}, use_global_device_ids=true, to_apply=%region_10.0 | all-reduce | flops 8192 | bytes 49152 | tf_op jit(solution)/shard_map/psum | solution.py:50
  770.3 143.0 %all-reduce.26.cloned.1.call-done = f32[1,64,1024]{2,1,0:T(8,128)} async-done(((f32[1,64,1024]{2,1,0:T(8,128)}), f32[1,64,1024]{2,1,0:T(8,128)}) %all-reduce.26.cloned.1.call-update) | async-done | bytes 262160 | tf_op jit(solution)/shard_map/psum | solution.py:57
  914.3 13.1 all_gather.9
  928.9 16.7 %psum.114 = f32[1,64,128]{2,1,0:T(8,128)S(1)} all-reduce(f32[1,64,128]{2,1,0:T(8,128)S(1)} %convolution_bitcast_fusion.12), channel_id=1, replica_groups=mesh['layer'=2,'prow'=4,'pcol'=32] {'prow'}, use_global_device_ids=true, to_apply=%region_12.0 | all-reduce | flops 8192 | bytes 65536 | tf_op jit(solution)/shard_map/psum | solution.py:120
  948.4 139.0 %all-reduce.28.cloned.1.call-done = f32[1,64,1024]{2,1,0:T(8,128)} async-done(((f32[1,64,1024]{2,1,0:T(8,128)}), f32[1,64,1024]{2,1,0:T(8,128)}) %all-reduce.28.cloned.1.call-update) | async-done | bytes 262160 | tf_op jit(solution)/shard_map/psum | solution.py:57
  1088.4 13.1 all_gather.10
  1103.2 43.1 %all-reduce.30.cloned.1.call-done = f32[2,64,128]{2,1,0:T(8,128)} async-done(((f32[2,64,128]{2,1,0:T(8,128)}), f32[2,64,128]{2,1,0:T(8,128)}) %all-reduce.30.cloned.1.call-update) | async-done | bytes 65552 | tf_op jit(solution)/shard_map/psum | solution.py:120
  1149.2 148.1 %all-reduce.32.cloned.1.call-done = f32[2,64,1024]{2,1,0:T(8,128)} async-done(((f32[2,64,1024]{2,1,0:T(8,128)}), f32[2,64,1024]{2,1,0:T(8,128)}) %all-reduce.32.cloned.1.call-update) | async-done | bytes 524304 | tf_op jit(solution)/shard_map/psum | solution.py:57
  1300.5 23.7 %all-gather.2.cloned.1.call-done = bf16[2,64,4096]{2,1,0:T(8,128)(2,1)} async-done(((bf16[2,64,1024]{2,1,0:T(8,128)(2,1)}), bf16[2,64,4096]{2,1,0:T(8,128)(2,1)}) %all-gather.2.cloned.1.call-update) | async-done | bytes 1048592 | tf_op jit(solution)/shard_map/all_gather | solution.py:66
  1328.0 46.7 %all-reduce.34.cloned.1.call-done = f32[4,64,128]{2,1,0:T(8,128)} async-done(((f32[4,64,128]{2,1,0:T(8,128)}), f32[4,64,128]{2,1,0:T(8,128)}) %all-reduce.34.cloned.1.call-update) | async-done | bytes 131088 | tf_op jit(solution)/shard_map/psum | solution.py:120
  1374.8 2.8 fusion.14
  1377.6 150.1 %all-reduce.36.cloned.1.call-done = f32[4,64,1024]{2,1,0:T(8,128)} async-done(((f32[4,64,1024]{2,1,0:T(8,128)}), f32[4,64,1024]{2,1,0:T(8,128)}) %all-reduce.36.cloned.1.call-update) | async-done | bytes 1048592 | tf_op jit(solution)/shard_map/psum | solution.py:57
  1527.7 2.6 pad_maximum_fusion
  (222 shorter events, 86.4 us)
Async XLA Ops:
  7.2 743.9 %copy-start = (bf16[1024,128]{1,0:T(8,128)(2,1)S(1)}, bf16[1024,128]{1,0:T(8,128)(2,1)}, u32[]{:S(2)}) copy-start(bf16[1024,128]{1,0:T(8,128)(2,1)} %param.29) | copy-start | bytes 786436
  7.2 52.6 %all-reduce.14.cloned.1.call-start = ((), (), s32[]{:S(2)}) async-start(), calls=%async_computation.3 | async-start | bytes 262144 | tf_op jit(solution)/shard_map/psum | solution.py:50
  9.9 140.1 %reduce-scatter.4.cloned.1.call-start = ((), (), s32[]{:S(2)}) async-start(), calls=%async_computation.4 | async-start | bytes 2621440 | tf_op jit(solution)/shard_map/reduce_scatter | solution.py:61
  12.1 53.5 %copy-start.31 = (pred[17,2,16]{2,1,0:T(4,128)(4,1)}, pred[17,2,16]{2,1,0:T(4,128)(4,1)S(1)}, u32[]{:S(2)}) copy-start(pred[17,2,16]{2,1,0:T(4,128)(4,1)S(1)} %get-tuple-element.123) | copy-start | bytes 1636
  117.1 32.9 %copy-start.13 = (bf16[4,64,128]{2,1,0:T(8,128)(2,1)S(1)}, bf16[4,64,128]{2,1,0:T(8,128)(2,1)}, u32[]{:S(2)}) copy-start(bf16[4,64,128]{2,1,0:T(8,128)(2,1)} %copy-done.12) | copy-start | bytes 196612
  117.1 33.0 %copy-start.23 = (bf16[1,128,512]{2,1,0:T(8,128)(2,1)S(1)}, bf16[1,128,512]{2,1,0:T(8,128)(2,1)}, u32[]{:S(2)}) copy-start(bf16[1,128,512]{2,1,0:T(8,128)(2,1)} %get-tuple-element.129) | copy-start | bytes 393220
  117.1 185.1 %copy-start.22 = (bf16[1,128,512]{2,1,0:T(8,128)(2,1)S(1)}, bf16[1,128,512]{2,1,0:T(8,128)(2,1)}, u32[]{:S(2)}) copy-start(bf16[1,128,512]{2,1,0:T(8,128)(2,1)} %get-tuple-element.128) | copy-start | bytes 393220
  117.1 230.8 %copy-start.21 = (bf16[1,128,512]{2,1,0:T(8,128)(2,1)S(1)}, bf16[1,128,512]{2,1,0:T(8,128)(2,1)}, u32[]{:S(2)}) copy-start(bf16[1,128,512]{2,1,0:T(8,128)(2,1)} %get-tuple-element.124) | copy-start | bytes 393220
  117.1 230.9 %copy-start.32 = (pred[17,2,16]{2,1,0:T(4,128)(4,1)S(1)}, pred[17,2,16]{2,1,0:T(4,128)(4,1)}, u32[]{:S(2)}) copy-start(pred[17,2,16]{2,1,0:T(4,128)(4,1)} %copy-done.31) | copy-start | bytes 1636
  117.2 182.6 %all-reduce.16.cloned.1.call-start = ((), (), s32[]{:S(2)}) async-start(), calls=%async_computation.5 | async-start | bytes 1048576 | tf_op jit(solution)/shard_map/psum | solution.py:62
  150.0 196.4 %all-reduce.18.cloned.1.call-start = ((), (), s32[]{:S(2)}) async-start(), calls=%async_computation.6 | async-start | bytes 131072 | tf_op jit(solution)/shard_map/psum | solution.py:50
  302.0 80.6 %reduce-scatter.6.cloned.1.call-start = ((), (), s32[]{:S(2)}) async-start(), calls=%async_computation.7 | async-start | bytes 1310720 | tf_op jit(solution)/shard_map/reduce_scatter | solution.py:61
  352.9 3.3 copy-start.19
  352.9 3.4 copy-start.24
  356.0 173.4 %all-reduce.20.cloned.1.call-start = ((), (), s32[]{:S(2)}) async-start(), calls=%async_computation.8 | async-start | bytes 524288 | tf_op jit(solution)/shard_map/psum | solution.py:62
  382.6 192.3 %reduce-scatter.8.cloned.1.call-start = ((), (), s32[]{:S(2)}) async-start(), calls=%async_computation.9 | async-start | bytes 1310720 | tf_op jit(solution)/shard_map/reduce_scatter | solution.py:61
  552.4 375.1 %copy-start.33 = (bf16[17,2,16]{2,1,0:T(2,128)(2,1)S(1)}, bf16[17,2,16]{2,1,0:T(2,128)(2,1)}, u32[]{:S(2)}) copy-start(bf16[17,2,16]{2,1,0:T(2,128)(2,1)} %get-tuple-element.122) | copy-start | bytes 3268
  552.4 169.1 %all-reduce.22.cloned.1.call-start = ((), (), s32[]{:S(2)}) async-start(), calls=%async_computation.10 | async-start | bytes 524288 | tf_op jit(solution)/shard_map/psum | solution.py:62
  575.0 176.1 %all-reduce.24.cloned.1.call-start = ((), (), s32[]{:S(2)}) async-start(), calls=%async_computation.11 | async-start | bytes 524288 | tf_op jit(solution)/shard_map/psum | solution.py:100
  721.5 191.8 %all-reduce.26.cloned.1.call-start = ((), (), s32[]{:S(2)}) async-start(), calls=%async_computation.12 | async-start | bytes 524288 | tf_op jit(solution)/shard_map/psum | solution.py:57
  770.2 317.2 %all-reduce.28.cloned.1.call-start = ((), (), s32[]{:S(2)}) async-start(), calls=%async_computation.13 | async-start | bytes 524288 | tf_op jit(solution)/shard_map/psum | solution.py:57
  927.5 18.2 %copy-start.29 = (f32[1,64,128]{2,1,0:T(8,128)S(1)}, f32[1,64,128]{2,1,0:T(8,128)}, u32[]{:S(2)}) copy-start(f32[1,64,128]{2,1,0:T(8,128)} %copy-done.28) | copy-start | bytes 98308
  947.5 198.8 %all-reduce.30.cloned.1.call-start = ((), (), s32[]{:S(2)}) async-start(), calls=%async_computation.14 | async-start | bytes 131072 | tf_op jit(solution)/shard_map/psum | solution.py:120
  948.4 198.0 %copy-start.30 = (f32[2,64,128]{2,1,0:T(8,128)S(1)}, f32[2,64,128]{2,1,0:T(8,128)}, u32[]{:S(2)}) copy-start(f32[2,64,128]{2,1,0:T(8,128)} %all-reduce.18.cloned.1.call-done) | copy-start | bytes 196612
  1103.0 194.3 %all-reduce.32.cloned.1.call-start = ((), (), s32[]{:S(2)}) async-start(), calls=%async_computation.15 | async-start | bytes 1048576 | tf_op jit(solution)/shard_map/psum | solution.py:57
  1148.5 175.6 %all-gather.2.cloned.1.call-start = ((), (), s32[]{:S(2)}) async-start(), calls=%async_computation.16 | async-start | bytes 1310720 | tf_op jit(solution)/shard_map/all_gather | solution.py:66
  1299.1 75.7 %all-reduce.34.cloned.1.call-start = ((), (), s32[]{:S(2)}) async-start(), calls=%async_computation.17 | async-start | bytes 262144 | tf_op jit(solution)/shard_map/psum | solution.py:120
  1326.0 48.8 %copy-start.16 = (f32[4,64,128]{2,1,0:T(8,128)S(1)}, f32[4,64,128]{2,1,0:T(8,128)}, u32[]{:S(2)}) copy-start(f32[4,64,128]{2,1,0:T(8,128)} %all-reduce.14.cloned.1.call-done) | copy-start | bytes 393220
  1326.9 200.7 %copy-start.10 = (f32[2,64,1024]{2,1,0:T(8,128)S(1)}, f32[2,64,1024]{2,1,0:T(8,128)}, u32[]{:S(2)}) copy-start(f32[2,64,1024]{2,1,0:T(8,128)} %all-reduce.32.cloned.1.call-done) | copy-start | bytes 1572868
  1327.0 200.7 %copy-start.11 = (f32[1,64,1024]{2,1,0:T(8,128)S(1)}, f32[1,64,1024]{2,1,0:T(8,128)}, u32[]{:S(2)}) copy-start(f32[1,64,1024]{2,1,0:T(8,128)} %all-reduce.28.cloned.1.call-done) | copy-start | bytes 786436
  1328.0 199.7 %all-reduce.36.cloned.1.call-start = ((), (), s32[]{:S(2)}) async-start(), calls=%async_computation.18 | async-start | bytes 2097152 | tf_op jit(solution)/shard_map/psum | solution.py:57
  1377.5 152.8 %copy-start.15 = (f32[1,64,1024]{2,1,0:T(8,128)S(1)}, f32[1,64,1024]{2,1,0:T(8,128)}, u32[]{:S(2)}) copy-start(f32[1,64,1024]{2,1,0:T(8,128)} %all-reduce.26.cloned.1.call-done) | copy-start | bytes 786436
  (19 other events, 30.3 us)
Sparse Core Ops, SparseCore 0:
  10.9 48.8 all-reduce.13
  117.3 32.6 reduce-scatter.3
  153.4 146.3 all-reduce.15
  302.6 43.7 all-reduce.17
  356.1 26.4 reduce-scatter.5
  386.3 142.9 all-reduce.19
  552.5 22.3 reduce-scatter.7
  578.4 143.0 all-reduce.21
  724.1 26.9 all-reduce.23
  770.3 142.9 all-reduce.25
  947.6 139.6 all-reduce.27
  1103.1 43.1 all-reduce.29
  1150.3 146.9 all-reduce.31
  1299.7 24.4 all-gather.1
  1328.1 46.6 all-reduce.33
  1378.6 148.9 all-reduce.35
where the time goes:
time: 1540 us
  waiting for transfers between devices  1330 us (86%)
  blocking collectives  76.9 us (5%)
  matrix products  60.7 us (4%)
  local copies, waits for them, and re-layouts  38.6 us (3%)
    psum x4, waiting for transfers between devices, backward_solve(): return lax.psum(partial_terms, 'pcol')  580 us
    psum x3, waiting for transfers between devices, combine_rows(): return lax.psum(share, 'pcol')  439 us
    psum x2, waiting for transfers between devices, forward_solve(): return lax.psum(partial_terms, 'prow')  91 us
    psum x2, waiting for transfers between devices, per_device(): lowered = lax.psum(jnp.stack(terms), 'prow')  89.8 us
    reduce_scatter x3, waiting for transfers between devices, combine_rows(): share = lax.psum_scatter(pending, 'prow', scatter_dimension=2, tiled=True)  77.1 us
    psum x2, blocking collectives, forward_solve(): return lax.psum(partial_terms, 'prow')  34 us
  transfers between devices with their start and end apart: 16, of which 16 were waited for; matrix products, arithmetic and copies ran while one was open for 1% of the time, Pallas kernels for 0%

commit v1 on v0

v1 whole, which is shorter than its diff:
```python
import jax
import jax.numpy as jnp
from jax import lax
from jax.experimental import pallas as pl
from jax.experimental.pallas import tpu as pltpu
from jax.sharding import PartitionSpec as P

NX = 4
NP = 32
RX = 16
BF = jnp.bfloat16
F32 = jnp.float32
LIMIT = 56 * 1024 * 1024

SMEM = pl.BlockSpec(memory_space=pltpu.SMEM)


def params():
    return pltpu.CompilerParams(vmem_limit_bytes=LIMIT)


def shift(value, distance):
    return lax.ppermute(value, "prow", [(i, (i + distance) % NX) for i in range(NX)])


def around(value):
    return [value] + [shift(value, distance) for distance in range(1, NX)]


def after(value, *earlier):
    return lax.optimization_barrier((value, *earlier))[0]


def exchange(value):
    return lax.all_to_all(value, "pcol", 0, 0, tiled=True)


def reduce_columns(parts):
    return jnp.sum(exchange(parts).astype(F32), axis=0)


def gather_columns(chunk):
    chunk = chunk.astype(BF)
    return exchange(jnp.broadcast_to(chunk[None], (NP,) + chunk.shape))


def dot(left, right):
    return lax.dot_general(left, right, (((1,), (0,)), ((), ())), preferred_element_type=F32)


def dot_t(left, right):
    return lax.dot_general(left, right, (((1,), (1,)), ((), ())), preferred_element_type=F32)


def row_start(x, distance):
    return pl.multiple_of(lax.rem(x + distance, NX) * RX, RX)


def source(x, distance):
    return lax.rem(x + (NX - distance), NX)


def leaf_update_kernel(x_ref, own, r1, r2, r3, factor, fwd, *rest):
    crit, other, total = rest[0:4], rest[4:8], rest[8]
    x = x_ref[0]
    total[...] = (own[...].astype(F32) + r1[...].astype(F32)) + (
        r2[...].astype(F32) + r3[...].astype(F32)
    )
    for n in range(4):
        fwd[n] = total[n, pl.ds(row_start(x, 0), RX), :]
        left = jnp.concatenate(
            [total[n, pl.ds(row_start(x, d), RX), :] for d in range(NX)], axis=0
        ).astype(BF)
        for i in range(3):
            update = dot(left, factor[3 * n + i]).astype(BF)
            for d in range(NX):
                piece = update[RX * d : RX * (d + 1)]
                if i == 2:
                    crit[d][n] = piece
                else:
                    other[d][2 * n + i] = piece


def leaf_update(x, own, received, factor):
    out = (
        [jax.ShapeDtypeStruct((4, RX, 128), F32)]
        + [jax.ShapeDtypeStruct((4, RX, 512), BF)] * 4
        + [jax.ShapeDtypeStruct((8, RX, 512), BF)] * 4
    )
    result = pl.pallas_call(
        leaf_update_kernel,
        out_shape=out,
        in_specs=[SMEM] + [pl.BlockSpec(memory_space=pltpu.VMEM)] * 5,
        scratch_shapes=[pltpu.VMEM((4, 64, 128), F32)],
        compiler_params=params(),
        name="leaf_update",
    )(x, own, *received, factor)
    return result[0], result[1:5], result[5:9]


def add_update(acc, lists, distance, pair, update, *lead):
    for j in range(2):
        block = lists[distance][pair, j]
        for h in range(2):
            index = (2 * block + h, *lead)
            tile = update[:, 256 * j + 128 * h : 256 * j + 128 * (h + 1)]
            acc[index] = acc[index] + tile.astype(F32)


def leaf_spread_kernel(l0, l1, l2, l3, c0, c1, c2, c3, out, acc):
    lists = (l0, l1, l2, l3)
    acc[...] = jnp.zeros(acc.shape, F32)
    for d, crit in enumerate((c0, c1, c2, c3)):
        for n in range(4):
            add_update(acc, lists, d, 5 + 3 * n + 2, crit[n], n // 2)
    out[...] = acc[...].astype(BF)


def leaf_spread(lists, crit):
    return pl.pallas_call(
        leaf_spread_kernel,
        out_shape=jax.ShapeDtypeStruct((NP, 2, RX, 128), BF),
        in_specs=[SMEM] * 4 + [pl.BlockSpec(memory_space=pltpu.VMEM)] * 4,
        scratch_shapes=[pltpu.VMEM((NP, 2, RX, 128), F32)],
        compiler_params=params(),
        name="leaf_spread",
    )(*lists, *crit)


def solve_columns(x, values, inverses, which, *lead):
    total = None
    for d in range(NX):
        first = 8 * source(x, d)
        left = jnp.concatenate([values[(first + k, *lead)] for k in range(8)], axis=1)
        term = dot(left, inverses[d][which])
        total = term if total is None else total + term
    return total


def solve_rows(x, target, inverses, which, store):
    for d in range(NX):
        row = source(x, d)
        wide = dot_t(target, inverses[d][which]).astype(BF)
        for k in range(8):
            store(row, k, wide[:, 128 * k : 128 * (k + 1)])


def pick_product(lists, pair, local_pair, values, factors, *lead):
    total = None
    for d in range(NX):
        tiles = []
        for j in range(2):
            block = lists[d][pair, j]
            tiles += [values[(2 * block, *lead)], values[(2 * block + 1, *lead)]]
        term = dot_t(jnp.concatenate(tiles, axis=1), factors[d][local_pair])
        total = term if total is None else total + term
    return total


def middle_forward_kernel(x_ref, *refs):
    lists, values, inverses, factors, other = (
        refs[0:4], refs[4], refs[5:9], refs[9:13], refs[13:17],
    )
    fwd, out, acc_root, acc = refs[17:21]
    x = x_ref[0]
    acc[...] = jnp.zeros(acc.shape, F32)
    acc_root[...] = jnp.zeros(acc_root.shape, F32)
    for d in range(NX):
        for n in range(4):
            add_update(acc_root, lists, d, 5 + 3 * n, other[d][2 * n])
            add_update(acc, lists, d, 5 + 3 * n + 1, other[d][2 * n + 1])
    for m in range(2):
        solved = solve_columns(x, values, inverses, m, m)
        fwd[m] = solved
        rounded = solved.astype(BF)
        for d in range(NX):
            add_update(acc_root, lists, d, 1 + 2 * m, dot(rounded, factors[d][1 + 2 * m]))
            add_update(acc, lists, d, 2 + 2 * m, dot(rounded, factors[d][2 + 2 * m]))
    out[...] = acc[...].astype(BF)


def middle_forward(x, lists, values, inverses, factors, other):
    return pl.pallas_call(
        middle_forward_kernel,
        out_shape=[
            jax.ShapeDtypeStruct((2, RX, 128), F32),
            jax.ShapeDtypeStruct((NP, RX, 128), BF),
            jax.ShapeDtypeStruct((NP, RX, 128), F32),
        ],
        in_specs=[SMEM] * 5 + [pl.BlockSpec(memory_space=pltpu.VMEM)] * 13,
        scratch_shapes=[pltpu.VMEM((NP, RX, 128), F32)],
        compiler_params=params(),
        name="middle_forward",
    )(x, *lists, values, *inverses, *factors, *other)


def top_forward_kernel(x_ref, *refs):
    lists, values, inverses, factors, acc_in = refs[0:4], refs[4], refs[5:9], refs[9:13], refs[13]
    fwd, out, acc = refs[14:17]
    x = x_ref[0]
    acc[...] = acc_in[...]
    solved = solve_columns(x, values, inverses, 0)
    fwd[...] = solved
    rounded = solved.astype(BF)
    for d in range(NX):
        add_update(acc, lists, d, 0, dot(rounded, factors[d][0]))
    out[...] = acc[...].astype(BF)


FIRST_PAIR = pl.BlockSpec((1, 128, 512), lambda i: (0, 0, 0))


def top_forward(x, lists, values, inverses, factors, acc_root):
    return pl.pallas_call(
        top_forward_kernel,
        grid=(1,),
        out_shape=[
            jax.ShapeDtypeStruct((RX, 128), F32),
            jax.ShapeDtypeStruct((NP, RX, 128), BF),
        ],
        in_specs=[SMEM] * 5
        + [pl.BlockSpec((NP, RX, 128), lambda i: (0, 0, 0))]
        + [pl.BlockSpec((1, 1024, 128), lambda i: (0, 0, 0))] * 4
        + [FIRST_PAIR] * 4
        + [pl.BlockSpec((NP, RX, 128), lambda i: (0, 0, 0))],
        out_specs=[
            pl.BlockSpec((RX, 128), lambda i: (0, 0)),
            pl.BlockSpec((NP, RX, 128), lambda i: (0, 0, 0)),
        ],
        scratch_shapes=[pltpu.VMEM((NP, RX, 128), F32)],
        compiler_params=params(),
        name="top_forward",
    )(x, *lists, values, *inverses, *factors, acc_root)


def root_kernel(x_ref, values, i0, i1, i2, i3, out):
    x = x_ref[0]
    inverses = (i0, i1, i2, i3)
    rounded = solve_columns(x, values, inverses, 0).astype(BF)

    def store(row, k, tile):
        out[8 * row + k] = tile

    solve_rows(x, rounded, inverses, 0, store)


def root_solve(x, values, inverses):
    return pl.pallas_call(
        root_kernel,
        grid=(1,),
        out_shape=jax.ShapeDtypeStruct((NP, RX, 128), BF),
        in_specs=[SMEM]
        + [pl.BlockSpec((NP, RX, 128), lambda i: (0, 0, 0))]
        + [pl.BlockSpec((1, 1024, 128), lambda i: (1, 0, 0))] * 4,
        out_specs=pl.BlockSpec((NP, RX, 128), lambda i: (0, 0, 0)),
        compiler_params=params(),
        name="root_solve",
    )(x, values, *inverses)


def top_backward_kernel(x_ref, *refs):
    lists, root, fwd, inverses, factors, out = (
        refs[0:4], refs[4], refs[5], refs[6:10], refs[10:14], refs[14],
    )
    x = x_ref[0]
    target = (fwd[...] - pick_product(lists, 0, 0, root, factors)).astype(BF)

    def store(row, k, tile):
        out[8 * row + k] = tile

    solve_rows(x, target, inverses, 0, store)


def top_backward(x, lists, root, fwd, inverses, factors):
    return pl.pallas_call(
        top_backward_kernel,
        grid=(1,),
        out_shape=jax.ShapeDtypeStruct((NP, RX, 128), BF),
        in_specs=[SMEM] * 5
        + [pl.BlockSpec((NP, RX, 128), lambda i: (0, 0, 0)), pl.BlockSpec((RX, 128), lambda i: (0, 0))]
        + [pl.BlockSpec((1, 1024, 128), lambda i: (0, 0, 0))] * 4
        + [FIRST_PAIR] * 4,
        out_specs=pl.BlockSpec((NP, RX, 128), lambda i: (0, 0, 0)),
        compiler_params=params(),
        name="top_backward",
    )(x, *lists, root, fwd, *inverses, *factors)


def middle_backward_kernel(x_ref, *refs):
    lists, root, top, fwd, inverses, factors, out = (
        refs[0:4], refs[4], refs[5], refs[6], refs[7:11], refs[11:15], refs[15],
    )
    x = x_ref[0]
    for m in range(2):
        down = pick_product(lists, 1 + 2 * m, 1 + 2 * m, root, factors)
        down = down + pick_product(lists, 2 + 2 * m, 2 + 2 * m, top, factors)
        target = (fwd[m] - down).astype(BF)

        def store(row, k, tile, m=m):
            out[8 * row + k, m] = tile

        solve_rows(x, target, inverses, m, store)


def middle_backward(x, lists, root, top, fwd, inverses, factors):
    return pl.pallas_call(
        middle_backward_kernel,
        out_shape=jax.ShapeDtypeStruct((NP, 2, RX, 128), BF),
        in_specs=[SMEM] * 5 + [pl.BlockSpec(memory_space=pltpu.VMEM)] * 11,
        compiler_params=params(),
        name="middle_backward",
    )(x, *lists, root, top, fwd, *inverses, *factors)


def leaf_backward_kernel(x_ref, *refs):
    lists, root, top, middle, fwd, inverses, factors, out = (
        refs[0:4], refs[4], refs[5], refs[6], refs[7], refs[8:12], refs[12:16], refs[16],
    )
    x = x_ref[0]
    n = pl.program_id(0)
    first = 5 + 3 * n
    down = pick_product(lists, first, 0, root, factors)
    down = down + pick_product(lists, first + 1, 1, top, factors)
    down = down + pick_product(lists, first + 2, 2, middle, factors, n // 2)
    target = (fwd[0] - down).astype(BF)

    def store(row, k, tile):
        out[k, row] = tile

    solve_rows(x, target, inverses, 0, store)


def leaf_backward(x, lists, root, top, middle, fwd, inverses, factors):
    whole = lambda shape: pl.BlockSpec(shape, lambda n: (0,) * len(shape))
    return pl.pallas_call(
        leaf_backward_kernel,
        grid=(4,),
        out_shape=jax.ShapeDtypeStruct((NP, NX, RX, 128), BF),
        in_specs=[SMEM] * 5
        + [whole((NP, RX, 128)), whole((NP, RX, 128)), whole((NP, 2, RX, 128))]
        + [pl.BlockSpec((1, RX, 128), lambda n: (n, 0, 0))]
        + [pl.BlockSpec((1, 1024, 128), lambda n: (n, 0, 0))] * 4
        + [pl.BlockSpec((3, 128, 512), lambda n: (n, 0, 0))] * 4,
        out_specs=pl.BlockSpec((8, NX, RX, 128), lambda n: (n, 0, 0, 0)),
        compiler_params=params(),
        name="leaf_backward",
    )(x, *lists, root, top, middle, fwd, *inverses, *factors)


def finish_kernel(x_ref, e0, e1, e2, e3, leaves, out_sub, out_root):
    x = x_ref[0]
    for d, early in enumerate((e0, e1, e2, e3)):
        rows = pl.ds(pl.multiple_of(RX * source(x, d), RX), RX)
        for k in range(8):
            columns = slice(128 * k, 128 * (k + 1))
            out_root[rows, columns] = early[k, 0].astype(F32)
            for t in range(3):
                out_sub[t, rows, columns] = early[k, 1 + t].astype(F32)
    for t in range(4):
        for k in range(8):
            out_sub[3 + t, :, 128 * k : 128 * (k + 1)] = leaves[8 * t + k].astype(F32)


def finish(x, early, leaves):
    return pl.pallas_call(
        finish_kernel,
        out_shape=[
            jax.ShapeDtypeStruct((7, 64, 1024), F32),
            jax.ShapeDtypeStruct((64, 1024), F32),
        ],
        in_specs=[SMEM] + [pl.BlockSpec(memory_space=pltpu.VMEM)] * 5,
        compiler_params=params(),
        name="finish",
    )(x, *early, leaves)


def per_device(right_sub, right_root, inverse_sub, inverse_root, factor_blocks, block_lists):
    position = lax.axis_index("prow")
    column = lax.axis_index("pcol")
    x = position.astype(jnp.int32)[None]

    inverse_leaf = inverse_sub[3:7]
    factor_leaf = factor_blocks[5:17]
    own = jnp.einsum(
        "nrm,nmc->nrc", right_sub[3:7].astype(BF), inverse_leaf, preferred_element_type=F32
    ).astype(BF)
    received = around(own)
    lists = around(block_lists)

    def right_piece(d):
        row = RX * lax.rem(position + d, NX)
        start = 128 * lax.rem(column, 8)
        sub = lax.dynamic_slice(right_sub, (0, row, start), (3, RX, 128))
        root = lax.dynamic_slice(right_root, (row, start), (RX, 128))
        return jnp.concatenate([sub, root[None]], 0)

    right = right_piece(0)
    held = lax.rem(position + NX - column // 8, NX)
    for d in range(1, NX):
        right = jnp.where(held == d, shift(right_piece(d), d), right)

    fwd_leaf, crit, other = leaf_update(x, own, received[1:], factor_leaf)
    crit = [crit[0]] + [shift(crit[d], d) for d in range(1, NX)]
    other = [other[0]] + [shift(other[d], d) for d in range(1, NX)]

    inverse_middle = around(inverse_sub[1:3])
    factor_upper = around(factor_blocks[0:5])
    inverse_top = around(jnp.concatenate([inverse_sub[0:1], inverse_root[None]], 0))

    parts = leaf_spread(lists, crit)
    values = gather_columns(right[1:3] - reduce_columns(parts))
    inverse_leaf = around(after(inverse_leaf, values))
    factor_leaf = around(after(factor_leaf, values))

    fwd_middle, parts, acc_root = middle_forward(x, lists, values, inverse_middle, factor_upper, other)
    values = gather_columns(right[0] - reduce_columns(parts))
    fwd_top, parts = top_forward(x, lists, values, inverse_top, factor_upper, acc_root)
    total = reduce_columns(parts)
    total = total + lax.ppermute(total, "layer", [(0, 1), (1, 0)])
    values = gather_columns(right[3] - total)
    root = gather_columns(reduce_columns(root_solve(x, values, inverse_top)))
    top = gather_columns(
        reduce_columns(top_backward(x, lists, root, fwd_top, inverse_top, factor_upper))
    )
    middle = gather_columns(
        reduce_columns(
            middle_backward(x, lists, root, top, fwd_middle, inverse_middle, factor_upper)
        )
    )

    early = jnp.concatenate([root[:, None], top[:, None], middle], 1)
    pieces = []
    for d in range(NX):
        piece = lax.dynamic_slice_in_dim(early, 8 * lax.rem(position + d, NX), 8, 0)
        pieces.append(shift(piece, d) if d else piece)

    parts = leaf_backward(x, lists, root, top, middle, fwd_leaf, inverse_leaf, factor_leaf)
    chunk = reduce_columns(parts).astype(BF)
    chunk = lax.all_to_all(chunk, "prow", 0, 0, tiled=True).reshape(4 * RX, 128)
    leaves = gather_columns(chunk)
    return tuple(finish(x, pieces, leaves))


def solution(mesh):
    in_specs = (
        P("layer", None, "prow"),
        P(None, "prow"),
        P("layer", "prow", "pcol"),
        P("prow", "pcol"),
        P("layer", "pcol", "prow"),
        P("layer", "prow"),
    )
    out_specs = (P("layer", None, "prow"), P(None, "prow"))
    return jax.shard_map(
        per_device, mesh=mesh, in_specs=in_specs, out_specs=out_specs, check_vma=False
    )
```

time: 1540 us -> 412 us (0.27)
  waiting for transfers between devices: 1330 us -> 151 us
  starting transfers between devices: 0.83 us -> 102 us
  matrix products: 60.7 us -> 2.01 us
  Pallas kernels: 0 us -> 34.5 us
  blocking collectives: 76.9 us -> 99.9 us
  local copies, waits for them, and re-layouts: 38.6 us -> 18.1 us
    psum x12 -> x0, waiting for transfers between devices: 1230 us -> none  [the longest x4 580 us: backward_solve(): return lax.psum(partial_terms, 'pcol')]
    ppermute x0 -> x34, waiting for transfers between devices: none -> 119 us  [the longest x33 118 us: shift(): lax.ppermute(value, 'prow', [(i, (i + distance) % NX) for i in range(NX)])]
    all_to_all x0 -> x6, blocking collectives: none -> 99.9 us  [the longest x5 89.7 us: exchange(): return lax.all_to_all(value, 'pcol', 0, 0, tiled=True)]
    reduce_scatter x3 -> x0, waiting for transfers between devices: 77.1 us -> none  [combine_rows(): share = lax.psum_scatter(pending, 'prow', scatter_dimension=2, tiled=True)]
    all_to_all x0 -> x9, starting transfers between devices: none -> 59.2 us  [exchange(): return lax.all_to_all(value, 'pcol', 0, 0, tiled=True)]
    dot_general x76 -> x1, matrix products: 60.7 us -> 2.01 us  [per_device(): jnp.einsum('nrm,nmc->nrc', right_sub[3:7].astype(BF), inverse_leaf, prefe...]
    psum x3 -> x0, blocking collectives: 50.7 us -> none  [the longest x2 34 us: forward_solve(): return lax.psum(partial_terms, 'prow')]
    ppermute x0 -> x34, starting transfers between devices: none -> 43.1 us  [the longest x33 43 us: shift(): lax.ppermute(value, 'prow', [(i, (i + distance) % NX) for i in range(NX)])]
  transfers between devices with their start and end apart: 16 -> 43, of which waited for: 16 -> 20; matrix products, arithmetic and copies ran while one was open for 1% -> 3% of each run, Pallas kernels for 0% -> 3%
where the time goes in v1:
time: 412 us; the launch traced here: 411 us
  waiting for transfers between devices  151 us (37%)
  starting transfers between devices  102 us (25%)
  blocking collectives  99.9 us (24%)
  Pallas kernels  34.5 us (8%)
  local copies, waits for them, and re-layouts  18.1 us (4%)
    ppermute x33, waiting for transfers between devices, shift(): lax.ppermute(value, 'prow', [(i, (i + distance) % NX) for i in range(NX)])  118 us
    all_to_all x5, blocking collectives, exchange(): return lax.all_to_all(value, 'pcol', 0, 0, tiled=True)  89.7 us
    all_to_all x9, starting transfers between devices, exchange(): return lax.all_to_all(value, 'pcol', 0, 0, tiled=True)  59.2 us
    ppermute x33, starting transfers between devices, shift(): lax.ppermute(value, 'prow', [(i, (i + distance) % NX) for i in range(NX)])  43 us
    all_to_all x9, waiting for transfers between devices, exchange(): return lax.all_to_all(value, 'pcol', 0, 0, tiled=True)  32.3 us
    all_to_all x1, blocking collectives, per_device(): chunk = lax.all_to_all(chunk, 'prow', 0, 0, tiled=True).reshape(4 * RX, 128)  10.2 us
    pallas_call x1, Pallas kernels, leaf_backward(): pl.pallas_call(leaf_backward_kernel, grid=(4,), out_shape=jax.ShapeDtypeS...  9.01 us
  transfers between devices with their start and end apart: 43, of which 20 were waited for; matrix products, arithmetic and copies ran while one was open for 3% of the time, Pallas kernels for 3%

profile of v1, /device:TPU:32, one launch (start us, length us, event | category | flops | bytes accessed | tf_op | source)
XLA Modules:
  0.0 410.6 jit_solution(9218017140232916784)
XLA Ops:
  30.0 11.4 %all-to-all-start = ((bf16[32,2,16,128]{3,2,1,0:T(8,128)(2,1)}), bf16[32,2,16,128]{3,2,1,0:T(8,128)(2,1)S(1)}, u32[]{:S(2)}, u32[]{:S(2)}) async-start(bf16[32,2,16,128]{3,2,1,0:T(8,128)(2,1)} %leaf_spread.1), calls=%async_computation | async-start | bytes 524288 | tf_op jit(solution)/shard_map/all_to_all | solution.py:35
  41.9 4.4 %collective-permute-start.1 = (f32[4,16,128]{2,1,0:T(8,128)S(1)}, f32[4,16,128]{2,1,0:T(8,128)S(1)}, u32[]{:S(2)}, u32[]{:S(2)}) collective-permute-start(f32[4,16,128]{2,1,0:T(8,128)S(1)} %pad_maximum_fusion.3), channel_id=1, source_target_pairs={{0,64},{32,96},{64,0},{96,32},{1,65},{33,97},{65,1},{97,33},{2,66}... | collective-permute-start | bytes 98312 | tf_op jit(solution)/shard_map/ppermute | solution.py:23
  49.9 10.0 %collective-permute-done.1 = f32[4,16,128]{2,1,0:T(8,128)S(1)} collective-permute-done((f32[4,16,128]{2,1,0:T(8,128)S(1)}, f32[4,16,128]{2,1,0:T(8,128)S(1)}, u32[]{:S(2)}, u32[]{:S(2)}) %collective-permute-start.1) | collective-permute-done | bytes 32800 | tf_op jit(solution)/shard_map/ppermute | solution.py:23
  60.0 14.3 %collective-permute-done.18.refs_14_ = bf16[8,16,512]{2,1,0:T(8,128)(2,1)S(1)} collective-permute-done((bf16[8,16,512]{2,1,0:T(8,128)(2,1)S(1)}, bf16[8,16,512]{2,1,0:T(8,128)(2,1)S(1)}, u32[]{:S(2)}, u32[]{:S(2)}) %collective-permute-start.18) | collective-permute-done | bytes 131104 | tf_op jit(solution)/shard_map/ppermute | solution.py:23
  79.7 4.1 %collective-permute-start.14 = (bf16[2,1024,128]{2,1,0:T(8,128)(2,1)S(1)}, bf16[2,1024,128]{2,1,0:T(8,128)(2,1)}, u32[]{:S(2)}, u32[]{:S(2)}) collective-permute-start(bf16[2,1024,128]{2,1,0:T(8,128)(2,1)S(1)} %slice.34.refs_5_.refs_7_), channel_id=1, source_target_pairs={{0,96},{32,0},{64,32},{96,64},{1,97},{33,1},{65,33},{97,65},{2,98}... | collective-permute-start | bytes 1572872 | tf_op jit(solution)/shard_map/ppermute | solution.py:23
  84.6 9.8 %all-to-all-start.1 = ((bf16[32,2,16,128]{3,2,1,0:T(8,128)(2,1)}), bf16[32,2,16,128]{3,2,1,0:T(8,128)(2,1)S(1)}, u32[]{:S(2)}, u32[]{:S(2)}) async-start(bf16[32,2,16,128]{3,2,1,0:T(8,128)(2,1)} %broadcast_in_dim.74), calls=%async_computation.1 | async-start | bytes 524288 | tf_op jit(solution)/shard_map/all_to_all | solution.py:35
  94.4 6.3 %collective-permute-done.13.refs_7_.refs_9_ = bf16[2,1024,128]{2,1,0:T(8,128)(2,1)} collective-permute-done((bf16[2,1024,128]{2,1,0:T(8,128)(2,1)S(1)}, bf16[2,1024,128]{2,1,0:T(8,128)(2,1)}, u32[]{:S(2)}, u32[]{:S(2)}) %collective-permute-start.13) | collective-permute-done | bytes 524320 | tf_op jit(solution)/shard_map/ppermute | solution.py:23
  100.7 20.6 %collective-permute-done.14.refs_8_.refs_10_ = bf16[2,1024,128]{2,1,0:T(8,128)(2,1)} collective-permute-done((bf16[2,1024,128]{2,1,0:T(8,128)(2,1)S(1)}, bf16[2,1024,128]{2,1,0:T(8,128)(2,1)}, u32[]{:S(2)}, u32[]{:S(2)}) %collective-permute-start.14) | collective-permute-done | bytes 524320 | tf_op jit(solution)/shard_map/ppermute | solution.py:23
  122.7 4.2 %middle_forward.1 = (f32[2,16,128]{2,1,0:T(8,128)}, bf16[32,16,128]{2,1,0:T(8,128)(2,1)}, f32[32,16,128]{2,1,0:T(8,128)}) custom-call(s32[1]{0:T(128)} %bitcast.x_ref, s32[17,2]{1,0:T(8,128)} %copy-done.21, s32[17,2]{1,0:T(8,128)} %copy-done.24, s32[17,2]{1,0:T(8,128)} %copy-done.25, s32[17,2]{1,0:T(8,128)} %copy-done.26, ...), custom_call_target="tpu_custom_call" | custom-call | tf_op jit(solution)/shard_map/middle_forward/pallas_call | solution.py:183
  126.9 9.9 %all-to-all-start.2 = ((bf16[32,16,128]{2,1,0:T(8,128)(2,1)}), bf16[32,16,128]{2,1,0:T(8,128)(2,1)S(1)}, u32[]{:S(2)}, u32[]{:S(2)}) async-start(bf16[32,16,128]{2,1,0:T(8,128)(2,1)} %get-tuple-element.26), calls=%async_computation.2 | async-start | bytes 262144 | tf_op jit(solution)/shard_map/all_to_all | solution.py:35
  142.0 4.6 %all-to-all-done.2 = bf16[32,16,128]{2,1,0:T(8,128)(2,1)S(1)} async-done(((bf16[32,16,128]{2,1,0:T(8,128)(2,1)}), bf16[32,16,128]{2,1,0:T(8,128)(2,1)S(1)}, u32[]{:S(2)}, u32[]{:S(2)}) %all-to-all-start.2) | async-done | bytes 131104 | tf_op jit(solution)/shard_map/all_to_all | solution.py:35
  147.3 5.2 %all-to-all-start.3 = ((bf16[32,16,128]{2,1,0:T(8,128)(2,1)}), bf16[32,16,128]{2,1,0:T(8,128)(2,1)S(1)}, u32[]{:S(2)}, u32[]{:S(2)}) async-start(bf16[32,16,128]{2,1,0:T(8,128)(2,1)} %broadcast_in_dim.76), calls=%async_computation.3 | async-start | bytes 262144 | tf_op jit(solution)/shard_map/all_to_all | solution.py:35
  152.5 9.3 %collective-permute-done.22.refs_7_.i2.refs_8_ = bf16[2,1024,128]{2,1,0:T(8,128)(2,1)S(1)} collective-permute-done((bf16[2,1024,128]{2,1,0:T(8,128)(2,1)S(1)}, bf16[2,1024,128]{2,1,0:T(8,128)(2,1)S(1)}, u32[]{:S(2)}, u32[]{:S(2)}) %collective-permute-start.22) | collective-permute-done | bytes 524320 | tf_op jit(solution)/shard_map/ppermute | solution.py:23
  165.5 19.4 %all_to_all.75 = bf16[32,16,128]{2,1,0:T(8,128)(2,1)S(1)} all-to-all(bf16[32,16,128]{2,1,0:T(8,128)(2,1)} %get-tuple-element.28), channel_id=1, replica_groups=mesh['layer'=2,'prow'=4,'pcol'=32] {'pcol'}, dimensions={0} | all-to-all | bytes 262144 | tf_op jit(solution)/shard_map/all_to_all | solution.py:35
  186.9 4.5 %all-to-all-start.5 = ((bf16[32,16,128]{2,1,0:T(8,128)(2,1)}), bf16[32,16,128]{2,1,0:T(8,128)(2,1)S(1)}, u32[]{:S(2)}, u32[]{:S(2)}) async-start(bf16[32,16,128]{2,1,0:T(8,128)(2,1)} %broadcast_in_dim.78), calls=%async_computation.5 | async-start | bytes 262144 | tf_op jit(solution)/shard_map/all_to_all | solution.py:35
  192.9 9.0 %all-to-all-done.5.values = bf16[32,16,128]{2,1,0:T(8,128)(2,1)S(1)} async-done(((bf16[32,16,128]{2,1,0:T(8,128)(2,1)}), bf16[32,16,128]{2,1,0:T(8,128)(2,1)S(1)}, u32[]{:S(2)}, u32[]{:S(2)}) %all-to-all-start.5) | async-done | bytes 131104 | tf_op jit(solution)/shard_map/all_to_all | solution.py:35
  205.0 14.0 %all_to_all.76 = bf16[32,16,128]{2,1,0:T(8,128)(2,1)S(1)} all-to-all(bf16[32,16,128]{2,1,0:T(8,128)(2,1)} %root_solve.1), channel_id=1, replica_groups=mesh['layer'=2,'prow'=4,'pcol'=32] {'pcol'}, dimensions={0} | all-to-all | bytes 262144 | tf_op jit(solution)/shard_map/all_to_all | solution.py:35
  219.8 4.7 %all-to-all-start.7 = ((bf16[32,16,128]{2,1,0:T(8,128)(2,1)}), bf16[32,16,128]{2,1,0:T(8,128)(2,1)S(1)}, u32[]{:S(2)}, u32[]{:S(2)}) async-start(bf16[32,16,128]{2,1,0:T(8,128)(2,1)} %broadcast_in_dim.79), calls=%async_computation.7 | async-start | bytes 262144 | tf_op jit(solution)/shard_map/all_to_all | solution.py:35
  228.1 6.2 %all-to-all-done.7.refs_4_ = bf16[32,16,128]{2,1,0:T(8,128)(2,1)S(1)} async-done(((bf16[32,16,128]{2,1,0:T(8,128)(2,1)}), bf16[32,16,128]{2,1,0:T(8,128)(2,1)S(1)}, u32[]{:S(2)}, u32[]{:S(2)}) %all-to-all-start.7) | async-done | bytes 131104 | tf_op jit(solution)/shard_map/all_to_all | solution.py:35
  238.1 14.3 %all_to_all.77 = bf16[32,16,128]{2,1,0:T(8,128)(2,1)S(1)} all-to-all(bf16[32,16,128]{2,1,0:T(8,128)(2,1)} %top_backward.1), channel_id=1, replica_groups=mesh['layer'=2,'prow'=4,'pcol'=32] {'pcol'}, dimensions={0} | all-to-all | bytes 262144 | tf_op jit(solution)/shard_map/all_to_all | solution.py:35
  253.1 4.4 %all-to-all-start.9 = ((bf16[32,16,128]{2,1,0:T(8,128)(2,1)}), bf16[32,16,128]{2,1,0:T(8,128)(2,1)S(1)}, u32[]{:S(2)}, u32[]{:S(2)}) async-start(bf16[32,16,128]{2,1,0:T(8,128)(2,1)} %broadcast_in_dim.81), calls=%async_computation.9 | async-start | bytes 262144 | tf_op jit(solution)/shard_map/all_to_all | solution.py:35
  261.4 5.8 %all-to-all-done.9.refs_5_ = bf16[32,16,128]{2,1,0:T(8,128)(2,1)S(1)} async-done(((bf16[32,16,128]{2,1,0:T(8,128)(2,1)}), bf16[32,16,128]{2,1,0:T(8,128)(2,1)S(1)}, u32[]{:S(2)}, u32[]{:S(2)}) %all-to-all-start.9) | async-done | bytes 131104 | tf_op jit(solution)/shard_map/all_to_all | solution.py:35
  267.9 5.0 %middle_backward.1 = bf16[32,2,16,128]{3,2,1,0:T(8,128)(2,1)} custom-call(s32[1]{0:T(128)} %bitcast.x_ref, s32[17,2]{1,0:T(8,128)} %copy-done.21, s32[17,2]{1,0:T(8,128)} %copy-done.24, s32[17,2]{1,0:T(8,128)} %copy-done.25, s32[17,2]{1,0:T(8,128)} %copy-done.26, bf16[32,16,128]{2,1,0:T(8,128)(2,1)} %copy-done.12, bf16[32,16,128]{2,1,0:T(8,128)(2,1)} %copy-done.17, ...), custom_call_target="tpu_custom_call" | custom-call | tf_op jit(solution)/shard_map/middle_backward/pallas_call | solution.py:306
  272.8 15.4 %all_to_all.78 = bf16[32,2,16,128]{3,2,1,0:T(8,128)(2,1)S(1)} all-to-all(bf16[32,2,16,128]{3,2,1,0:T(8,128)(2,1)} %middle_backward.1), channel_id=1, replica_groups=mesh['layer'=2,'prow'=4,'pcol'=32] {'pcol'}, dimensions={0} | all-to-all | bytes 524288 | tf_op jit(solution)/shard_map/all_to_all | solution.py:35
  289.1 4.5 %all-to-all-start.11 = ((bf16[32,2,16,128]{3,2,1,0:T(8,128)(2,1)}), bf16[32,2,16,128]{3,2,1,0:T(8,128)(2,1)S(1)}, u32[]{:S(2)}, u32[]{:S(2)}) async-start(bf16[32,2,16,128]{3,2,1,0:T(8,128)(2,1)} %broadcast_in_dim.83), calls=%async_computation.11 | async-start | bytes 524288 | tf_op jit(solution)/shard_map/all_to_all | solution.py:35
  293.6 22.7 %collective-permute-done.29.refs_10_ = bf16[4,1024,128]{2,1,0:T(8,128)(2,1)} collective-permute-done((bf16[4,1024,128]{2,1,0:T(8,128)(2,1)S(1)}, bf16[4,1024,128]{2,1,0:T(8,128)(2,1)}, u32[]{:S(2)}, u32[]{:S(2)}) %collective-permute-start.29) | collective-permute-done | bytes 1048608 | tf_op jit(solution)/shard_map/ppermute | solution.py:23
  316.2 22.9 %collective-permute-done.30.refs_11_ = bf16[4,1024,128]{2,1,0:T(8,128)(2,1)} collective-permute-done((bf16[4,1024,128]{2,1,0:T(8,128)(2,1)S(1)}, bf16[4,1024,128]{2,1,0:T(8,128)(2,1)}, u32[]{:S(2)}, u32[]{:S(2)}) %collective-permute-start.30) | collective-permute-done | bytes 1048608 | tf_op jit(solution)/shard_map/ppermute | solution.py:23
  339.8 9.0 %leaf_backward.1 = bf16[32,4,16,128]{3,2,1,0:T(8,128)(2,1)} custom-call(s32[1]{0:T(128)} %bitcast.x_ref, s32[17,2]{1,0:T(8,128)} %copy-done.21, s32[17,2]{1,0:T(8,128)} %copy-done.24, s32[17,2]{1,0:T(8,128)} %copy-done.25, s32[17,2]{1,0:T(8,128)} %copy-done.26, bf16[32,16,128]{2,1,0:T(8,128)(2,1)} %copy-done.12, bf16[32,16,128]{2,1,0:T(8,128)(2,1)} %copy-done.17, ...), custom_call_target="tpu_custom_call" | custom-call | tf_op jit(solution)/shard_map/leaf_backward/pallas_call | solution.py:335
  348.9 26.6 %all_to_all.79 = bf16[32,4,16,128]{3,2,1,0:T(8,128)(2,1)S(1)} all-to-all(bf16[32,4,16,128]{3,2,1,0:T(8,128)(2,1)} %leaf_backward.1), channel_id=1, replica_groups=mesh['layer'=2,'prow'=4,'pcol'=32] {'pcol'}, dimensions={0} | all-to-all | bytes 1048576 | tf_op jit(solution)/shard_map/all_to_all | solution.py:35
  375.5 10.2 %all_to_all.80 = bf16[4,16,128]{2,1,0:T(8,128)(2,1)S(1)} all-to-all(bf16[4,16,128]{2,1,0:T(8,128)(2,1)S(1)} %reduce_sum.84), channel_id=1, replica_groups=mesh['layer'=2,'prow'=4,'pcol'=32] {'prow'}, dimensions={0} | all-to-all | bytes 32768 | tf_op jit(solution)/shard_map/all_to_all | solution.py:439
  386.7 4.8 %all-to-all-start.14 = ((bf16[32,64,128]{2,1,0:T(8,128)(2,1)}), bf16[32,64,128]{2,1,0:T(8,128)(2,1)S(1)}, u32[]{:S(2)}, u32[]{:S(2)}) async-start(bf16[32,64,128]{2,1,0:T(8,128)(2,1)} %broadcast_in_dim.85), calls=%async_computation.14 | async-start | bytes 1048576 | tf_op jit(solution)/shard_map/all_to_all | solution.py:35
  400.8 6.2 %all-to-all-done.14.leaves = bf16[32,64,128]{2,1,0:T(8,128)(2,1)S(1)} async-done(((bf16[32,64,128]{2,1,0:T(8,128)(2,1)}), bf16[32,64,128]{2,1,0:T(8,128)(2,1)S(1)}, u32[]{:S(2)}, u32[]{:S(2)}) %all-to-all-start.14) | async-done | bytes 524320 | tf_op jit(solution)/shard_map/all_to_all | solution.py:35
  (191 shorter events, 85.6 us)
Async XLA Ops:
  8.5 12.7 %collective-permute-start.3 = (s32[17,2]{1,0:T(8,128)S(1)}, s32[17,2]{1,0:T(8,128)S(1)}, u32[]{:S(2)}, u32[]{:S(2)}) collective-permute-start(s32[17,2]{1,0:T(8,128)S(1)} %copy.13.l0.refs_0_), channel_id=1, source_target_pairs={{0,32},{32,64},{64,96},{96,0},{1,33},{33,65},{65,97},{97,1},{2,34}... | collective-permute-start | bytes 416 | tf_op jit(solution)/shard_map/ppermute | solution.py:23
  9.1 14.3 %collective-permute-start.4 = (s32[17,2]{1,0:T(8,128)S(1)}, s32[17,2]{1,0:T(8,128)S(1)}, u32[]{:S(2)}, u32[]{:S(2)}) collective-permute-start(s32[17,2]{1,0:T(8,128)S(1)} %copy.13.l0.refs_0_), channel_id=1, source_target_pairs={{0,64},{32,96},{64,0},{96,32},{1,65},{33,97},{65,1},{97,33},{2,66}... | collective-permute-start | bytes 416 | tf_op jit(solution)/shard_map/ppermute | solution.py:23
  12.3 11.1 %collective-permute-start.5 = (s32[17,2]{1,0:T(8,128)S(1)}, s32[17,2]{1,0:T(8,128)S(1)}, u32[]{:S(2)}, u32[]{:S(2)}) collective-permute-start(s32[17,2]{1,0:T(8,128)S(1)} %copy.13.l0.refs_0_), channel_id=1, source_target_pairs={{0,96},{32,0},{64,32},{96,64},{1,97},{33,1},{65,33},{97,65},{2,98}... | collective-permute-start | bytes 416 | tf_op jit(solution)/shard_map/ppermute | solution.py:23
  30.0 30.0 %all-to-all-start = ((bf16[32,2,16,128]{3,2,1,0:T(8,128)(2,1)}), bf16[32,2,16,128]{3,2,1,0:T(8,128)(2,1)S(1)}, u32[]{:S(2)}, u32[]{:S(2)}) async-start(bf16[32,2,16,128]{3,2,1,0:T(8,128)(2,1)} %leaf_spread.1), calls=%async_computation | async-start | bytes 524288 | tf_op jit(solution)/shard_map/all_to_all | solution.py:35
  41.7 38.0 %collective-permute-start.12 = (bf16[2,1024,128]{2,1,0:T(8,128)(2,1)S(1)}, bf16[2,1024,128]{2,1,0:T(8,128)(2,1)}, u32[]{:S(2)}, u32[]{:S(2)}) collective-permute-start(bf16[2,1024,128]{2,1,0:T(8,128)(2,1)S(1)} %slice.34.refs_5_.refs_7_), channel_id=1, source_target_pairs={{0,32},{32,64},{64,96},{96,0},{1,33},{33,65},{65,97},{97,1},{2,34}... | collective-permute-start | bytes 1572872 | tf_op jit(solution)/shard_map/ppermute | solution.py:23
  41.9 17.9 %collective-permute-start.1 = (f32[4,16,128]{2,1,0:T(8,128)S(1)}, f32[4,16,128]{2,1,0:T(8,128)S(1)}, u32[]{:S(2)}, u32[]{:S(2)}) collective-permute-start(f32[4,16,128]{2,1,0:T(8,128)S(1)} %pad_maximum_fusion.3), channel_id=1, source_target_pairs={{0,64},{32,96},{64,0},{96,32},{1,65},{33,97},{65,1},{97,33},{2,66}... | collective-permute-start | bytes 98312 | tf_op jit(solution)/shard_map/ppermute | solution.py:23
  46.3 13.5 %collective-permute-start = (f32[4,16,128]{2,1,0:T(8,128)S(1)}, f32[4,16,128]{2,1,0:T(8,128)S(1)}, u32[]{:S(2)}, u32[]{:S(2)}) collective-permute-start(f32[4,16,128]{2,1,0:T(8,128)S(1)} %pad_maximum_fusion.2), channel_id=1, source_target_pairs={{0,96},{32,0},{64,32},{96,64},{1,97},{33,1},{65,33},{97,65},{2,98}... | collective-permute-start | bytes 98312 | tf_op jit(solution)/shard_map/ppermute | solution.py:23
  47.4 73.9 %collective-permute-start.15 = (bf16[5,128,512]{2,1,0:T(8,128)(2,1)S(1)}, bf16[5,128,512]{2,1,0:T(8,128)(2,1)S(1)}, u32[]{:S(2)}, u32[]{:S(2)}) collective-permute-start(bf16[5,128,512]{2,1,0:T(8,128)(2,1)S(1)} %slice.35.refs_9_.refs_10_.refs_11_), channel_id=1, source_target_pairs={{0,32},{32,64},{64,96},{96,0},{1,33},{33,65},{65,97},{97,1},{2,34}... | collective-permute-start | bytes 1966088 | tf_op jit(solution)/shard_map/ppermute | solution.py:23
  49.5 24.8 %collective-permute-start.18 = (bf16[8,16,512]{2,1,0:T(8,128)(2,1)S(1)}, bf16[8,16,512]{2,1,0:T(8,128)(2,1)S(1)}, u32[]{:S(2)}, u32[]{:S(2)}) collective-permute-start(bf16[8,16,512]{2,1,0:T(8,128)(2,1)S(1)} %copy-done.43), channel_id=1, source_target_pairs={{0,32},{32,64},{64,96},{96,0},{1,33},{33,65},{65,97},{97,1},{2,34}... | collective-permute-start | bytes 393224 | tf_op jit(solution)/shard_map/ppermute | solution.py:23
  59.8 19.3 %collective-permute-start.19 = (bf16[8,16,512]{2,1,0:T(8,128)(2,1)S(1)}, bf16[8,16,512]{2,1,0:T(8,128)(2,1)}, u32[]{:S(2)}, u32[]{:S(2)}) collective-permute-start(bf16[8,16,512]{2,1,0:T(8,128)(2,1)S(1)} %copy-done.42), channel_id=1, source_target_pairs={{0,64},{32,96},{64,0},{96,32},{1,65},{33,97},{65,1},{97,33},{2,66}... | collective-permute-start | bytes 393224 | tf_op jit(solution)/shard_map/ppermute | solution.py:23
  59.8 19.3 %collective-permute-start.20 = (bf16[8,16,512]{2,1,0:T(8,128)(2,1)}, bf16[8,16,512]{2,1,0:T(8,128)(2,1)S(1)}, u32[]{:S(2)}, u32[]{:S(2)}) collective-permute-start(bf16[8,16,512]{2,1,0:T(8,128)(2,1)} %get-tuple-element.25), channel_id=1, source_target_pairs={{0,96},{32,0},{64,32},{96,64},{1,97},{33,1},{65,33},{97,65},{2,98}... | collective-permute-start | bytes 393224 | tf_op jit(solution)/shard_map/ppermute | solution.py:23
  74.3 47.0 %collective-permute-start.16 = (bf16[5,128,512]{2,1,0:T(8,128)(2,1)S(1)}, bf16[5,128,512]{2,1,0:T(8,128)(2,1)S(1)}, u32[]{:S(2)}, u32[]{:S(2)}) collective-permute-start(bf16[5,128,512]{2,1,0:T(8,128)(2,1)S(1)} %slice.35.refs_9_.refs_10_.refs_11_), channel_id=1, source_target_pairs={{0,64},{32,96},{64,0},{96,32},{1,65},{33,97},{65,1},{97,33},{2,66}... | collective-permute-start | bytes 1966088 | tf_op jit(solution)/shard_map/ppermute | solution.py:23
  79.1 42.2 %collective-permute-start.17 = (bf16[5,128,512]{2,1,0:T(8,128)(2,1)S(1)}, bf16[5,128,512]{2,1,0:T(8,128)(2,1)S(1)}, u32[]{:S(2)}, u32[]{:S(2)}) collective-permute-start(bf16[5,128,512]{2,1,0:T(8,128)(2,1)S(1)} %slice.35.refs_9_.refs_10_.refs_11_), channel_id=1, source_target_pairs={{0,96},{32,0},{64,32},{96,64},{1,97},{33,1},{65,33},{97,65},{2,98}... | collective-permute-start | bytes 1966088 | tf_op jit(solution)/shard_map/ppermute | solution.py:23
  79.2 21.6 %collective-permute-start.13 = (bf16[2,1024,128]{2,1,0:T(8,128)(2,1)S(1)}, bf16[2,1024,128]{2,1,0:T(8,128)(2,1)}, u32[]{:S(2)}, u32[]{:S(2)}) collective-permute-start(bf16[2,1024,128]{2,1,0:T(8,128)(2,1)S(1)} %slice.34.refs_5_.refs_7_), channel_id=1, source_target_pairs={{0,64},{32,96},{64,0},{96,32},{1,65},{33,97},{65,1},{97,33},{2,66}... | collective-permute-start | bytes 1572872 | tf_op jit(solution)/shard_map/ppermute | solution.py:23
  79.7 41.6 %collective-permute-start.14 = (bf16[2,1024,128]{2,1,0:T(8,128)(2,1)S(1)}, bf16[2,1024,128]{2,1,0:T(8,128)(2,1)}, u32[]{:S(2)}, u32[]{:S(2)}) collective-permute-start(bf16[2,1024,128]{2,1,0:T(8,128)(2,1)S(1)} %slice.34.refs_5_.refs_7_), channel_id=1, source_target_pairs={{0,96},{32,0},{64,32},{96,64},{1,97},{33,1},{65,33},{97,65},{2,98}... | collective-permute-start | bytes 1572872 | tf_op jit(solution)/shard_map/ppermute | solution.py:23
  84.6 36.8 %all-to-all-start.1 = ((bf16[32,2,16,128]{3,2,1,0:T(8,128)(2,1)}), bf16[32,2,16,128]{3,2,1,0:T(8,128)(2,1)S(1)}, u32[]{:S(2)}, u32[]{:S(2)}) async-start(bf16[32,2,16,128]{3,2,1,0:T(8,128)(2,1)} %broadcast_in_dim.74), calls=%async_computation.1 | async-start | bytes 524288 | tf_op jit(solution)/shard_map/all_to_all | solution.py:35
  126.9 19.6 %all-to-all-start.2 = ((bf16[32,16,128]{2,1,0:T(8,128)(2,1)}), bf16[32,16,128]{2,1,0:T(8,128)(2,1)S(1)}, u32[]{:S(2)}, u32[]{:S(2)}) async-start(bf16[32,16,128]{2,1,0:T(8,128)(2,1)} %get-tuple-element.26), calls=%async_computation.2 | async-start | bytes 262144 | tf_op jit(solution)/shard_map/all_to_all | solution.py:35
  137.9 14.6 %collective-permute-start.21 = (bf16[2,1024,128]{2,1,0:T(8,128)(2,1)S(1)}, bf16[2,1024,128]{2,1,0:T(8,128)(2,1)S(1)}, u32[]{:S(2)}, u32[]{:S(2)}) collective-permute-start(bf16[2,1024,128]{2,1,0:T(8,128)(2,1)S(1)} %pad_maximum_fusion.refs_5_.i0.refs_6_), channel_id=1, source_target_pairs={{0,32},{32,64},{64,96},{96,0},{1,33},{33,65},{65,97},{97,1},{2,34}... | collective-permute-start | bytes 1572872 | tf_op jit(solution)/shard_map/ppermute | solution.py:23
  138.1 23.7 %collective-permute-start.22 = (bf16[2,1024,128]{2,1,0:T(8,128)(2,1)S(1)}, bf16[2,1024,128]{2,1,0:T(8,128)(2,1)S(1)}, u32[]{:S(2)}, u32[]{:S(2)}) collective-permute-start(bf16[2,1024,128]{2,1,0:T(8,128)(2,1)S(1)} %pad_maximum_fusion.refs_5_.i0.refs_6_), channel_id=1, source_target_pairs={{0,64},{32,96},{64,0},{96,32},{1,65},{33,97},{65,1},{97,33},{2,66}... | collective-permute-start | bytes 1572872 | tf_op jit(solution)/shard_map/ppermute | solution.py:23
  142.0 19.8 %collective-permute-start.23 = (bf16[2,1024,128]{2,1,0:T(8,128)(2,1)S(1)}, bf16[2,1024,128]{2,1,0:T(8,128)(2,1)S(1)}, u32[]{:S(2)}, u32[]{:S(2)}) collective-permute-start(bf16[2,1024,128]{2,1,0:T(8,128)(2,1)S(1)} %pad_maximum_fusion.refs_5_.i0.refs_6_), channel_id=1, source_target_pairs={{0,96},{32,0},{64,32},{96,64},{1,97},{33,1},{65,33},{97,65},{2,98}... | collective-permute-start | bytes 1572872 | tf_op jit(solution)/shard_map/ppermute | solution.py:23
  147.3 14.9 %all-to-all-start.3 = ((bf16[32,16,128]{2,1,0:T(8,128)(2,1)}), bf16[32,16,128]{2,1,0:T(8,128)(2,1)S(1)}, u32[]{:S(2)}, u32[]{:S(2)}) async-start(bf16[32,16,128]{2,1,0:T(8,128)(2,1)} %broadcast_in_dim.76), calls=%async_computation.3 | async-start | bytes 262144 | tf_op jit(solution)/shard_map/all_to_all | solution.py:35
  186.9 15.0 %all-to-all-start.5 = ((bf16[32,16,128]{2,1,0:T(8,128)(2,1)}), bf16[32,16,128]{2,1,0:T(8,128)(2,1)S(1)}, u32[]{:S(2)}, u32[]{:S(2)}) async-start(bf16[32,16,128]{2,1,0:T(8,128)(2,1)} %broadcast_in_dim.78), calls=%async_computation.5 | async-start | bytes 262144 | tf_op jit(solution)/shard_map/all_to_all | solution.py:35
  192.8 66.6 %collective-permute-start.28 = (bf16[4,1024,128]{2,1,0:T(8,128)(2,1)S(1)}, bf16[4,1024,128]{2,1,0:T(8,128)(2,1)}, u32[]{:S(2)}, u32[]{:S(2)}) collective-permute-start(bf16[4,1024,128]{2,1,0:T(8,128)(2,1)S(1)} %slice.32.refs_8_), channel_id=1, source_target_pairs={{0,32},{32,64},{64,96},{96,0},{1,33},{33,65},{65,97},{97,1},{2,34}... | collective-permute-start | bytes 3145736 | tf_op jit(solution)/shard_map/ppermute | solution.py:23
  219.8 14.5 %all-to-all-start.7 = ((bf16[32,16,128]{2,1,0:T(8,128)(2,1)}), bf16[32,16,128]{2,1,0:T(8,128)(2,1)S(1)}, u32[]{:S(2)}, u32[]{:S(2)}) async-start(bf16[32,16,128]{2,1,0:T(8,128)(2,1)} %broadcast_in_dim.79), calls=%async_computation.7 | async-start | bytes 262144 | tf_op jit(solution)/shard_map/all_to_all | solution.py:35
  224.5 114.6 %collective-permute-start.31 = (bf16[12,128,512]{2,1,0:T(8,128)(2,1)S(1)}, bf16[12,128,512]{2,1,0:T(8,128)(2,1)}, u32[]{:S(2)}, u32[]{:S(2)}) collective-permute-start(bf16[12,128,512]{2,1,0:T(8,128)(2,1)S(1)} %copy-done.1), channel_id=1, source_target_pairs={{0,32},{32,64},{64,96},{96,0},{1,33},{33,65},{65,97},{97,1},{2,34}... | collective-permute-start | bytes 4718600 | tf_op jit(solution)/shard_map/ppermute | solution.py:23
  224.6 114.5 %collective-permute-start.32 = (bf16[12,128,512]{2,1,0:T(8,128)(2,1)S(1)}, bf16[12,128,512]{2,1,0:T(8,128)(2,1)}, u32[]{:S(2)}, u32[]{:S(2)}) collective-permute-start(bf16[12,128,512]{2,1,0:T(8,128)(2,1)S(1)} %copy-done.1), channel_id=1, source_target_pairs={{0,64},{32,96},{64,0},{96,32},{1,65},{33,97},{65,1},{97,33},{2,66}... | collective-permute-start | bytes 4718600 | tf_op jit(solution)/shard_map/ppermute | solution.py:23
  228.1 111.0 %collective-permute-start.33 = (bf16[12,128,512]{2,1,0:T(8,128)(2,1)S(1)}, bf16[12,128,512]{2,1,0:T(8,128)(2,1)}, u32[]{:S(2)}, u32[]{:S(2)}) collective-permute-start(bf16[12,128,512]{2,1,0:T(8,128)(2,1)S(1)} %copy-done.1), channel_id=1, source_target_pairs={{0,96},{32,0},{64,32},{96,64},{1,97},{33,1},{65,33},{97,65},{2,98}... | collective-permute-start | bytes 4718600 | tf_op jit(solution)/shard_map/ppermute | solution.py:23
  253.1 14.2 %all-to-all-start.9 = ((bf16[32,16,128]{2,1,0:T(8,128)(2,1)}), bf16[32,16,128]{2,1,0:T(8,128)(2,1)S(1)}, u32[]{:S(2)}, u32[]{:S(2)}) async-start(bf16[32,16,128]{2,1,0:T(8,128)(2,1)} %broadcast_in_dim.81), calls=%async_computation.9 | async-start | bytes 262144 | tf_op jit(solution)/shard_map/all_to_all | solution.py:35
  257.5 58.8 %collective-permute-start.29 = (bf16[4,1024,128]{2,1,0:T(8,128)(2,1)S(1)}, bf16[4,1024,128]{2,1,0:T(8,128)(2,1)}, u32[]{:S(2)}, u32[]{:S(2)}) collective-permute-start(bf16[4,1024,128]{2,1,0:T(8,128)(2,1)S(1)} %slice.32.refs_8_), channel_id=1, source_target_pairs={{0,64},{32,96},{64,0},{96,32},{1,65},{33,97},{65,1},{97,33},{2,66}... | collective-permute-start | bytes 3145736 | tf_op jit(solution)/shard_map/ppermute | solution.py:23
  259.3 79.8 %collective-permute-start.30 = (bf16[4,1024,128]{2,1,0:T(8,128)(2,1)S(1)}, bf16[4,1024,128]{2,1,0:T(8,128)(2,1)}, u32[]{:S(2)}, u32[]{:S(2)}) collective-permute-start(bf16[4,1024,128]{2,1,0:T(8,128)(2,1)S(1)} %slice.32.refs_8_), channel_id=1, source_target_pairs={{0,96},{32,0},{64,32},{96,64},{1,97},{33,1},{65,33},{97,65},{2,98}... | collective-permute-start | bytes 3145736 | tf_op jit(solution)/shard_map/ppermute | solution.py:23
  289.1 50.1 %all-to-all-start.11 = ((bf16[32,2,16,128]{3,2,1,0:T(8,128)(2,1)}), bf16[32,2,16,128]{3,2,1,0:T(8,128)(2,1)S(1)}, u32[]{:S(2)}, u32[]{:S(2)}) async-start(bf16[32,2,16,128]{3,2,1,0:T(8,128)(2,1)} %broadcast_in_dim.83), calls=%async_computation.11 | async-start | bytes 524288 | tf_op jit(solution)/shard_map/all_to_all | solution.py:35
  386.7 20.4 %all-to-all-start.14 = ((bf16[32,64,128]{2,1,0:T(8,128)(2,1)}), bf16[32,64,128]{2,1,0:T(8,128)(2,1)S(1)}, u32[]{:S(2)}, u32[]{:S(2)}) async-start(bf16[32,64,128]{2,1,0:T(8,128)(2,1)} %broadcast_in_dim.85), calls=%async_computation.14 | async-start | bytes 1048576 | tf_op jit(solution)/shard_map/all_to_all | solution.py:35
  (56 other events, 775.3 us)

commit v2 on v1

v2 whole, which is shorter than its diff:
```python
import jax
import jax.numpy as jnp
from jax import lax
from jax.experimental import pallas as pl
from jax.experimental.pallas import tpu as pltpu
from jax.sharding import PartitionSpec as P

NX = 4
NP = 32
RX = 16
BF = jnp.bfloat16
F32 = jnp.float32
LIMIT = 56 * 1024 * 1024

SMEM = pl.BlockSpec(memory_space=pltpu.SMEM)


def params():
    return pltpu.CompilerParams(vmem_limit_bytes=LIMIT)


def shift(value, distance):
    return lax.ppermute(value, "prow", [(i, (i + distance) % NX) for i in range(NX)])


def around(value):
    return [value] + [shift(value, distance) for distance in range(1, NX)]


def after(value, *earlier):
    return lax.optimization_barrier((value, *earlier))[0]


def exchange(value):
    return lax.all_to_all(value, "pcol", 0, 0, tiled=True)


def reduce_columns(parts):
    return jnp.sum(exchange(parts).astype(F32), axis=0)


def gather_columns(chunk):
    chunk = chunk.astype(BF)
    return exchange(jnp.broadcast_to(chunk[None], (NP,) + chunk.shape))


def dot(left, right):
    return lax.dot_general(left, right, (((1,), (0,)), ((), ())), preferred_element_type=F32)


def dot_t(left, right):
    return lax.dot_general(left, right, (((1,), (1,)), ((), ())), preferred_element_type=F32)


def row_start(x, distance):
    return pl.multiple_of(lax.rem(x + distance, NX) * RX, RX)


def source(x, distance):
    return lax.rem(x + (NX - distance), NX)


def leaf_update_kernel(x_ref, own, r1, r2, r3, factor, fwd, *rest):
    crit, other, total = rest[0:4], rest[4:8], rest[8]
    x = x_ref[0]
    total[...] = (own[...].astype(F32) + r1[...].astype(F32)) + (
        r2[...].astype(F32) + r3[...].astype(F32)
    )
    for n in range(4):
        fwd[n] = total[n, pl.ds(row_start(x, 0), RX), :]
        left = jnp.concatenate(
            [total[n, pl.ds(row_start(x, d), RX), :] for d in range(NX)], axis=0
        ).astype(BF)
        for i in range(3):
            update = dot(left, factor[3 * n + i]).astype(BF)
            for d in range(NX):
                piece = update[RX * d : RX * (d + 1)]
                if i == 2:
                    crit[d][n] = piece
                else:
                    other[d][2 * n + i] = piece


def leaf_update(x, own, received, factor):
    out = (
        [jax.ShapeDtypeStruct((4, RX, 128), F32)]
        + [jax.ShapeDtypeStruct((4, RX, 512), BF)] * 4
        + [jax.ShapeDtypeStruct((8, RX, 512), BF)] * 4
    )
    result = pl.pallas_call(
        leaf_update_kernel,
        out_shape=out,
        in_specs=[SMEM] + [pl.BlockSpec(memory_space=pltpu.VMEM)] * 5,
        scratch_shapes=[pltpu.VMEM((4, 64, 128), F32)],
        compiler_params=params(),
        name="leaf_update",
    )(x, own, *received, factor)
    return result[0], result[1:5], result[5:9]


def listed(table, distance, pair, j):
    return table[(distance * 17 + pair) * 2 + j]


def add_update(acc, table, distance, pair, update, *lead):
    for j in range(2):
        block = listed(table, distance, pair, j)
        for h in range(2):
            index = (2 * block + h, *lead)
            tile = update[:, 256 * j + 128 * h : 256 * j + 128 * (h + 1)]
            acc[index] = acc[index] + tile.astype(F32)


def leaf_spread_kernel(lists, c0, c1, c2, c3, out, acc):
    acc[...] = jnp.zeros(acc.shape, F32)
    for d, crit in enumerate((c0, c1, c2, c3)):
        for n in range(4):
            add_update(acc, lists, d, 5 + 3 * n + 2, crit[n], n // 2)
    out[...] = acc[...].astype(BF)


def leaf_spread(lists, crit):
    return pl.pallas_call(
        leaf_spread_kernel,
        out_shape=jax.ShapeDtypeStruct((NP, 2, RX, 128), BF),
        in_specs=[SMEM] + [pl.BlockSpec(memory_space=pltpu.VMEM)] * 4,
        scratch_shapes=[pltpu.VMEM((NP, 2, RX, 128), F32)],
        compiler_params=params(),
        name="leaf_spread",
    )(lists, *crit)


def solve_columns(values, inverse, which, *lead):
    total = None
    for r in range(NX):
        left = jnp.concatenate([values[(8 * r + k, *lead)] for k in range(8)], axis=1)
        term = dot(left, inverse[r, which])
        total = term if total is None else total + term
    return total


def solve_rows(target, inverse, which, store):
    for r in range(NX):
        wide = dot_t(target, inverse[r, which]).astype(BF)
        for k in range(8):
            store(r, k, wide[:, 128 * k : 128 * (k + 1)])


def multiply_update(acc, x, table, pair, local_pair, rounded, factor, *lead):
    for r in range(NX):
        update = dot(rounded, factor[r, local_pair])
        add_update(acc, table, source(x, r), pair, update, *lead)


def pick_product(x, table, pair, local_pair, values, factor, *lead):
    total = None
    for r in range(NX):
        tiles = []
        for j in range(2):
            block = listed(table, source(x, r), pair, j)
            tiles += [values[(2 * block, *lead)], values[(2 * block + 1, *lead)]]
        term = dot_t(jnp.concatenate(tiles, axis=1), factor[r, local_pair])
        total = term if total is None else total + term
    return total


def whole(*shape):
    return pl.BlockSpec(shape, lambda n: (0,) * len(shape))


TILES = whole(NP, RX, 128)
TOP_INVERSE = whole(NX, 1, 1024, 128)
TOP_FACTOR = whole(NX, 1, 128, 512)
VMEM = pl.BlockSpec(memory_space=pltpu.VMEM)


def middle_forward_kernel(x_ref, table, values, inverse, factor, o0, o1, o2, o3, fwd, out, acc_root, acc):
    x = x_ref[0]
    acc[...] = jnp.zeros(acc.shape, F32)
    acc_root[...] = jnp.zeros(acc_root.shape, F32)
    for d, other in enumerate((o0, o1, o2, o3)):
        for n in range(4):
            add_update(acc_root, table, d, 5 + 3 * n, other[2 * n])
            add_update(acc, table, d, 5 + 3 * n + 1, other[2 * n + 1])
    for m in range(2):
        solved = solve_columns(values, inverse, m, m)
        fwd[m] = solved
        rounded = solved.astype(BF)
        multiply_update(acc_root, x, table, 1 + 2 * m, 1 + 2 * m, rounded, factor)
        multiply_update(acc, x, table, 2 + 2 * m, 2 + 2 * m, rounded, factor)
    out[...] = acc[...].astype(BF)


def middle_forward(x, table, values, inverse, factor, other):
    return pl.pallas_call(
        middle_forward_kernel,
        out_shape=[
            jax.ShapeDtypeStruct((2, RX, 128), F32),
            jax.ShapeDtypeStruct((NP, RX, 128), BF),
            jax.ShapeDtypeStruct((NP, RX, 128), F32),
        ],
        in_specs=[SMEM] * 2 + [VMEM] * 7,
        scratch_shapes=[pltpu.VMEM((NP, RX, 128), F32)],
        compiler_params=params(),
        name="middle_forward",
    )(x, table, values, inverse, factor, *other)


def top_forward_kernel(x_ref, table, values, inverse, factor, acc_in, fwd, out, acc):
    acc[...] = acc_in[...]
    solved = solve_columns(values, inverse, 0)
    fwd[...] = solved
    multiply_update(acc, x_ref[0], table, 0, 0, solved.astype(BF), factor)
    out[...] = acc[...].astype(BF)


def top_forward(x, table, values, inverse, factor, acc_root):
    return pl.pallas_call(
        top_forward_kernel,
        grid=(1,),
        out_shape=[
            jax.ShapeDtypeStruct((RX, 128), F32),
            jax.ShapeDtypeStruct((NP, RX, 128), BF),
        ],
        in_specs=[SMEM] * 2 + [TILES, TOP_INVERSE, TOP_FACTOR, TILES],
        out_specs=[whole(RX, 128), TILES],
        scratch_shapes=[pltpu.VMEM((NP, RX, 128), F32)],
        compiler_params=params(),
        name="top_forward",
    )(x, table, values, inverse, factor, acc_root)


def root_kernel(values, inverse, out):
    rounded = solve_columns(values, inverse, 0).astype(BF)

    def store(r, k, tile):
        out[8 * r + k] = tile

    solve_rows(rounded, inverse, 0, store)


def root_solve(values, inverse):
    return pl.pallas_call(
        root_kernel,
        grid=(1,),
        out_shape=jax.ShapeDtypeStruct((NP, RX, 128), BF),
        in_specs=[TILES, pl.BlockSpec((NX, 1, 1024, 128), lambda n: (0, 1, 0, 0))],
        out_specs=TILES,
        compiler_params=params(),
        name="root_solve",
    )(values, inverse)


def top_backward_kernel(x_ref, table, root, fwd, inverse, factor, out):
    down = pick_product(x_ref[0], table, 0, 0, root, factor)

    def store(r, k, tile):
        out[8 * r + k] = tile

    solve_rows((fwd[...] - down).astype(BF), inverse, 0, store)


def top_backward(x, table, root, fwd, inverse, factor):
    return pl.pallas_call(
        top_backward_kernel,
        grid=(1,),
        out_shape=jax.ShapeDtypeStruct((NP, RX, 128), BF),
        in_specs=[SMEM] * 2 + [TILES, whole(RX, 128), TOP_INVERSE, TOP_FACTOR],
        out_specs=TILES,
        compiler_params=params(),
        name="top_backward",
    )(x, table, root, fwd, inverse, factor)


def middle_backward_kernel(x_ref, table, root, top, fwd, inverse, factor, out):
    x = x_ref[0]
    for m in range(2):
        down = pick_product(x, table, 1 + 2 * m, 1 + 2 * m, root, factor)
        down = down + pick_product(x, table, 2 + 2 * m, 2 + 2 * m, top, factor)

        def store(r, k, tile, m=m):
            out[8 * r + k, m] = tile

        solve_rows((fwd[m] - down).astype(BF), inverse, m, store)


def middle_backward(x, table, root, top, fwd, inverse, factor):
    return pl.pallas_call(
        middle_backward_kernel,
        out_shape=jax.ShapeDtypeStruct((NP, 2, RX, 128), BF),
        in_specs=[SMEM] * 2 + [VMEM] * 5,
        compiler_params=params(),
        name="middle_backward",
    )(x, table, root, top, fwd, inverse, factor)


def leaf_backward_kernel(x_ref, table, root, top, middle, fwd, inverse, factor, out):
    x = x_ref[0]
    n = pl.program_id(0)
    first = 5 + 3 * n
    down = pick_product(x, table, first, 0, root, factor)
    down = down + pick_product(x, table, first + 1, 1, top, factor)
    down = down + pick_product(x, table, first + 2, 2, middle, factor, n // 2)

    def store(r, k, tile):
        out[k, r] = tile

    solve_rows((fwd[0] - down).astype(BF), inverse, 0, store)


def leaf_backward(x, table, root, top, middle, fwd, inverse, factor):
    return pl.pallas_call(
        leaf_backward_kernel,
        grid=(4,),
        out_shape=jax.ShapeDtypeStruct((NP, NX, RX, 128), BF),
        in_specs=[SMEM] * 2
        + [TILES, TILES, whole(NP, 2, RX, 128)]
        + [pl.BlockSpec((1, RX, 128), lambda n: (n, 0, 0))]
        + [pl.BlockSpec((NX, 1, 1024, 128), lambda n: (0, n, 0, 0))]
        + [pl.BlockSpec((NX, 3, 128, 512), lambda n: (0, n, 0, 0))],
        out_specs=pl.BlockSpec((8, NX, RX, 128), lambda n: (n, 0, 0, 0)),
        compiler_params=params(),
        name="leaf_backward",
    )(x, table, root, top, middle, fwd, inverse, factor)


def finish_kernel(x_ref, e0, e1, e2, e3, leaves, out_sub, out_root):
    x = x_ref[0]
    for d, early in enumerate((e0, e1, e2, e3)):
        rows = pl.ds(pl.multiple_of(RX * source(x, d), RX), RX)
        for k in range(8):
            columns = slice(128 * k, 128 * (k + 1))
            out_root[rows, columns] = early[k, 0].astype(F32)
            for t in range(3):
                out_sub[t, rows, columns] = early[k, 1 + t].astype(F32)
    for t in range(4):
        for k in range(8):
            out_sub[3 + t, :, 128 * k : 128 * (k + 1)] = leaves[8 * t + k].astype(F32)


def finish(x, early, leaves):
    return pl.pallas_call(
        finish_kernel,
        out_shape=[
            jax.ShapeDtypeStruct((7, 64, 1024), F32),
            jax.ShapeDtypeStruct((64, 1024), F32),
        ],
        in_specs=[SMEM] + [pl.BlockSpec(memory_space=pltpu.VMEM)] * 5,
        compiler_params=params(),
        name="finish",
    )(x, *early, leaves)


def gather_rows(value):
    return lax.all_gather(value, "prow")


def per_device(right_sub, right_root, inverse_sub, inverse_root, factor_blocks, block_lists):
    position = lax.axis_index("prow")
    column = lax.axis_index("pcol")
    x = position.astype(jnp.int32)[None]

    inverse_middle = gather_rows(inverse_sub[1:3])
    factor_upper = gather_rows(factor_blocks[0:5])
    inverse_top = gather_rows(jnp.concatenate([inverse_sub[0:1], inverse_root[None]], 0))
    inverse_leaf = gather_rows(inverse_sub[3:7])
    factor_leaf = gather_rows(factor_blocks[5:17])

    own = jnp.einsum(
        "nrm,nmc->nrc", right_sub[3:7].astype(BF), inverse_sub[3:7], preferred_element_type=F32
    ).astype(BF)
    received = around(own)
    table = jnp.concatenate([value.reshape(-1) for value in around(block_lists)])

    def right_piece(d):
        row = RX * lax.rem(position + d, NX)
        start = 128 * lax.rem(column, 8)
        sub = lax.dynamic_slice(right_sub, (0, row, start), (3, RX, 128))
        root = lax.dynamic_slice(right_root, (row, start), (RX, 128))
        return jnp.concatenate([sub, root[None]], 0)

    right = right_piece(0)
    held = lax.rem(position + NX - column // 8, NX)
    for d in range(1, NX):
        right = jnp.where(held == d, shift(right_piece(d), d), right)

    fwd_leaf, crit, other = leaf_update(x, own, received[1:], factor_blocks[5:17])
    crit = [crit[0]] + [shift(crit[d], d) for d in range(1, NX)]
    other = [other[0]] + [shift(other[d], d) for d in range(1, NX)]

    values = gather_columns(right[1:3] - reduce_columns(leaf_spread(table, crit)))
    fwd_middle, parts, acc_root = middle_forward(
        x, table, values, inverse_middle, factor_upper, other
    )
    values = gather_columns(right[0] - reduce_columns(parts))
    fwd_top, parts = top_forward(x, table, values, inverse_top, factor_upper, acc_root)
    total = reduce_columns(parts)
    total = total + lax.ppermute(total, "layer", [(0, 1), (1, 0)])
    values = gather_columns(right[3] - total)
    root = gather_columns(reduce_columns(root_solve(values, inverse_top)))
    parts = top_backward(x, table, root, fwd_top, inverse_top, factor_upper)
    top = gather_columns(reduce_columns(parts))
    parts = middle_backward(x, table, root, top, fwd_middle, inverse_middle, factor_upper)
    middle = gather_columns(reduce_columns(parts))

    early = jnp.concatenate([root[:, None], top[:, None], middle], 1)
    pieces = []
    for d in range(NX):
        piece = lax.dynamic_slice_in_dim(early, 8 * lax.rem(position + d, NX), 8, 0)
        pieces.append(shift(piece, d) if d else piece)

    parts = leaf_backward(x, table, root, top, middle, fwd_leaf, inverse_leaf, factor_leaf)
    parts = after(parts, *pieces)
    chunk = reduce_columns(parts).astype(BF)
    chunk = lax.all_to_all(chunk, "prow", 0, 0, tiled=True).reshape(4 * RX, 128)
    leaves = gather_columns(chunk)
    return tuple(finish(x, pieces, leaves))


def solution(mesh):
    in_specs = (
        P("layer", None, "prow"),
        P(None, "prow"),
        P("layer", "prow", "pcol"),
        P("prow", "pcol"),
        P("layer", "pcol", "prow"),
        P("layer", "prow"),
    )
    out_specs = (P("layer", None, "prow"), P(None, "prow"))
    return jax.shard_map(
        per_device, mesh=mesh, in_specs=in_specs, out_specs=out_specs, check_vma=False
    )
```

time: 412 us -> 336 us (0.82)
  waiting for transfers between devices: 151 us -> 51.7 us
  blocking collectives: 99.9 us -> 167 us
  starting transfers between devices: 102 us -> 49.9 us
  between operations: 1.24 us -> 14.2 us
    ppermute x33 -> x18, waiting for transfers between devices: 118 us -> 25.5 us  [shift(): lax.ppermute(value, 'prow', [(i, (i + distance) % NX) for i in range(NX)])]
    all_to_all x5 -> x10, blocking collectives: 89.7 us -> 159 us  [exchange(): return lax.all_to_all(value, 'pcol', 0, 0, tiled=True)]
    all_to_all x9 -> x4, starting transfers between devices: 59.2 us -> 26.1 us  [exchange(): return lax.all_to_all(value, 'pcol', 0, 0, tiled=True)]
    ppermute x33 -> x18, starting transfers between devices: 43 us -> 23.5 us  [shift(): lax.ppermute(value, 'prow', [(i, (i + distance) % NX) for i in range(NX)])]
    all_to_all x9 -> x4, waiting for transfers between devices: 32.3 us -> 17.7 us  [exchange(): return lax.all_to_all(value, 'pcol', 0, 0, tiled=True)]
    all_gather x0 -> x5, waiting for transfers between devices: none -> 7.36 us  [gather_rows(): return lax.all_gather(value, 'prow')]
    unnamed x89 -> x49, local copies, waits for them, and re-layouts: 6.84 us -> 2.07 us
  transfers between devices with their start and end apart: 43 -> 28, of which waited for: 20 -> 18; matrix products, arithmetic and copies ran while one was open for 3% -> 4% of each run, Pallas kernels for 3% -> 9%
where the time goes in v2:
time: 336 us; the launch traced here: 335 us
  blocking collectives  167 us (50%)
  waiting for transfers between devices  51.7 us (15%)
  starting transfers between devices  49.9 us (15%)
  Pallas kernels  33.6 us (10%)
  local copies, waits for them, and re-layouts  15.1 us (4%)
  between operations  14.2 us (4%)
    all_to_all x10, blocking collectives, exchange(): return lax.all_to_all(value, 'pcol', 0, 0, tiled=True)  159 us
    all_to_all x4, starting transfers between devices, exchange(): return lax.all_to_all(value, 'pcol', 0, 0, tiled=True)  26.1 us
    ppermute x18, waiting for transfers between devices, shift(): lax.ppermute(value, 'prow', [(i, (i + distance) % NX) for i in range(NX)])  25.5 us
    ppermute x18, starting transfers between devices, shift(): lax.ppermute(value, 'prow', [(i, (i + distance) % NX) for i in range(NX)])  23.5 us
    all_to_all x4, waiting for transfers between devices, exchange(): return lax.all_to_all(value, 'pcol', 0, 0, tiled=True)  17.7 us
    pallas_call x1, Pallas kernels, leaf_backward(): pl.pallas_call(leaf_backward_kernel, grid=(4,), out_shape=jax.ShapeDtypeS...  8.67 us
    all_to_all x1, blocking collectives, per_device(): chunk = lax.all_to_all(chunk, 'prow', 0, 0, tiled=True).reshape(4 * RX, 128)  8.31 us
    all_gather x5, waiting for transfers between devices, gather_rows(): return lax.all_gather(value, 'prow')  7.36 us
  transfers between devices with their start and end apart: 28, of which 18 were waited for; matrix products, arithmetic and copies ran while one was open for 4% of the time, Pallas kernels for 9%

profile of v2, /device:TPU:32, one launch (start us, length us, event | category | flops | bytes accessed | tf_op | source)
XLA Modules:
  0.0 335.0 jit_solution(12459481937229305741)
XLA Ops:
  13.5 2.7 slice.35.factor
  19.3 2.7 collective-permute-start.7
  32.7 2.8 leaf_update.1
  40.1 3.0 collective-permute-done.10.c2
  48.9 11.4 %all-to-all-start = ((bf16[32,2,16,128]{3,2,1,0:T(8,128)(2,1)}), bf16[32,2,16,128]{3,2,1,0:T(8,128)(2,1)S(1)}, u32[]{:S(2)}, u32[]{:S(2)}) async-start(bf16[32,2,16,128]{3,2,1,0:T(8,128)(2,1)} %leaf_spread.1), calls=%async_computation | async-start | bytes 524288 | tf_op jit(solution)/shard_map/all_to_all | solution.py:35
  68.1 3.2 all-to-all-done
  72.1 6.0 %all-to-all-start.1 = ((bf16[32,2,16,128]{3,2,1,0:T(8,128)(2,1)}), bf16[32,2,16,128]{3,2,1,0:T(8,128)(2,1)S(1)}, u32[]{:S(2)}, u32[]{:S(2)}) async-start(bf16[32,2,16,128]{3,2,1,0:T(8,128)(2,1)} %broadcast_in_dim.74), calls=%async_computation.1 | async-start | bytes 524288 | tf_op jit(solution)/shard_map/all_to_all | solution.py:35
  82.6 5.5 %collective-permute-done.12.o1 = bf16[8,16,512]{2,1,0:T(8,128)(2,1)S(1)} collective-permute-done((bf16[8,16,512]{2,1,0:T(8,128)(2,1)S(1)}, bf16[8,16,512]{2,1,0:T(8,128)(2,1)S(1)}, u32[]{:S(2)}, u32[]{:S(2)}) %collective-permute-start.12) | collective-permute-done | bytes 131104 | tf_op jit(solution)/shard_map/ppermute | solution.py:23
  88.1 4.5 %collective-permute-done.13.o2 = bf16[8,16,512]{2,1,0:T(8,128)(2,1)S(1)} collective-permute-done((bf16[8,16,512]{2,1,0:T(8,128)(2,1)S(1)}, bf16[8,16,512]{2,1,0:T(8,128)(2,1)S(1)}, u32[]{:S(2)}, u32[]{:S(2)}) %collective-permute-start.13) | collective-permute-done | bytes 131104 | tf_op jit(solution)/shard_map/ppermute | solution.py:23
  93.9 4.2 %middle_forward.1 = (f32[2,16,128]{2,1,0:T(8,128)}, bf16[32,16,128]{2,1,0:T(8,128)(2,1)}, f32[32,16,128]{2,1,0:T(8,128)}) custom-call(s32[1]{0:T(128)} %bitcast.x_ref, s32[136]{0:T(256)} %pad_add_fusion.lists.table, bf16[32,2,16,128]{3,2,1,0:T(8,128)(2,1)} %copy-done.4, bf16[4,2,1024,128]{3,2,1,0:T(8,128)(2,1)} %bitcast.37, ...), custom_call_target="tpu_custom_call" | custom-call | tf_op jit(solution)/shard_map/middle_forward/pallas_call | solution.py:195
  98.1 19.9 %all_to_all.75 = bf16[32,16,128]{2,1,0:T(8,128)(2,1)S(1)} all-to-all(bf16[32,16,128]{2,1,0:T(8,128)(2,1)} %get-tuple-element.25), channel_id=1, replica_groups=mesh['layer'=2,'prow'=4,'pcol'=32] {'pcol'}, dimensions={0} | all-to-all | bytes 262144 | tf_op jit(solution)/shard_map/all_to_all | solution.py:35
  118.7 4.3 %all-to-all-start.3 = ((bf16[32,16,128]{2,1,0:T(8,128)(2,1)}), bf16[32,16,128]{2,1,0:T(8,128)(2,1)S(1)}, u32[]{:S(2)}, u32[]{:S(2)}) async-start(bf16[32,16,128]{2,1,0:T(8,128)(2,1)} %broadcast_in_dim.76), calls=%async_computation.3 | async-start | bytes 262144 | tf_op jit(solution)/shard_map/all_to_all | solution.py:35
  123.0 6.3 %all-gather.15.cloned.1.call-done = bf16[8,1024,128]{2,1,0:T(8,128)(2,1)} async-done(((bf16[2,1024,128]{2,1,0:T(8,128)(2,1)}), bf16[8,1024,128]{2,1,0:T(8,128)(2,1)}) %all-gather.15.cloned.1.call-update) | async-done | bytes 2097168 | tf_op jit(solution)/shard_map/all_gather | solution.py:355
  129.3 3.5 %all-to-all-done.3.values = bf16[32,16,128]{2,1,0:T(8,128)(2,1)S(1)} async-done(((bf16[32,16,128]{2,1,0:T(8,128)(2,1)}), bf16[32,16,128]{2,1,0:T(8,128)(2,1)S(1)}, u32[]{:S(2)}, u32[]{:S(2)}) %all-to-all-start.3) | async-done | bytes 131104 | tf_op jit(solution)/shard_map/all_to_all | solution.py:35
  133.4 2.6 top_forward.1
  136.0 16.4 %all_to_all.76 = bf16[32,16,128]{2,1,0:T(8,128)(2,1)S(1)} all-to-all(bf16[32,16,128]{2,1,0:T(8,128)(2,1)} %get-tuple-element.27), channel_id=1, replica_groups=mesh['layer'=2,'prow'=4,'pcol'=32] {'pcol'}, dimensions={0} | all-to-all | bytes 262144 | tf_op jit(solution)/shard_map/all_to_all | solution.py:35
  153.8 14.5 %all_to_all.77.values = bf16[32,16,128]{2,1,0:T(8,128)(2,1)} all-to-all(bf16[32,16,128]{2,1,0:T(8,128)(2,1)S(1)} %broadcast_in_dim.78), channel_id=1, replica_groups=mesh['layer'=2,'prow'=4,'pcol'=32] {'pcol'}, dimensions={0} | all-to-all | bytes 262144 | tf_op jit(solution)/shard_map/all_to_all | solution.py:35
  168.2 2.6 root_solve.1
  170.8 14.2 %all_to_all.78 = bf16[32,16,128]{2,1,0:T(8,128)(2,1)S(1)} all-to-all(bf16[32,16,128]{2,1,0:T(8,128)(2,1)} %root_solve.1), channel_id=1, replica_groups=mesh['layer'=2,'prow'=4,'pcol'=32] {'pcol'}, dimensions={0} | all-to-all | bytes 262144 | tf_op jit(solution)/shard_map/all_to_all | solution.py:35
  185.1 14.0 %all_to_all.79.root = bf16[32,16,128]{2,1,0:T(8,128)(2,1)} all-to-all(bf16[32,16,128]{2,1,0:T(8,128)(2,1)S(1)} %broadcast_in_dim.79), channel_id=1, replica_groups=mesh['layer'=2,'prow'=4,'pcol'=32] {'pcol'}, dimensions={0} | all-to-all | bytes 262144 | tf_op jit(solution)/shard_map/all_to_all | solution.py:35
  199.0 3.2 top_backward.1
  202.2 14.2 %all_to_all.80 = bf16[32,16,128]{2,1,0:T(8,128)(2,1)S(1)} all-to-all(bf16[32,16,128]{2,1,0:T(8,128)(2,1)} %top_backward.1), channel_id=1, replica_groups=mesh['layer'=2,'prow'=4,'pcol'=32] {'pcol'}, dimensions={0} | all-to-all | bytes 262144 | tf_op jit(solution)/shard_map/all_to_all | solution.py:35
  216.5 14.0 %all_to_all.81.top = bf16[32,16,128]{2,1,0:T(8,128)(2,1)} all-to-all(bf16[32,16,128]{2,1,0:T(8,128)(2,1)S(1)} %broadcast_in_dim.81), channel_id=1, replica_groups=mesh['layer'=2,'prow'=4,'pcol'=32] {'pcol'}, dimensions={0} | all-to-all | bytes 262144 | tf_op jit(solution)/shard_map/all_to_all | solution.py:35
  230.5 5.1 %middle_backward.1 = bf16[32,2,16,128]{3,2,1,0:T(8,128)(2,1)} custom-call(s32[1]{0:T(128)} %bitcast.x_ref, s32[136]{0:T(256)} %pad_add_fusion.lists.table, bf16[32,16,128]{2,1,0:T(8,128)(2,1)} %all_to_all.79.root, bf16[32,16,128]{2,1,0:T(8,128)(2,1)} %all_to_all.81.top, f32[2,16,128]{2,1,0:T(8,128)} %get-tuple-element.29.fwd, ...), custom_call_target="tpu_custom_call" | custom-call | tf_op jit(solution)/shard_map/middle_backward/pallas_call | solution.py:288
  235.6 15.5 %all_to_all.82 = bf16[32,2,16,128]{3,2,1,0:T(8,128)(2,1)S(1)} all-to-all(bf16[32,2,16,128]{3,2,1,0:T(8,128)(2,1)} %middle_backward.1), channel_id=1, replica_groups=mesh['layer'=2,'prow'=4,'pcol'=32] {'pcol'}, dimensions={0} | all-to-all | bytes 524288 | tf_op jit(solution)/shard_map/all_to_all | solution.py:35
  251.9 4.5 %all-to-all-start.11 = ((bf16[32,2,16,128]{3,2,1,0:T(8,128)(2,1)}), bf16[32,2,16,128]{3,2,1,0:T(8,128)(2,1)S(1)}, u32[]{:S(2)}, u32[]{:S(2)}) async-start(bf16[32,2,16,128]{3,2,1,0:T(8,128)(2,1)} %broadcast_in_dim.83), calls=%async_computation.11 | async-start | bytes 524288 | tf_op jit(solution)/shard_map/all_to_all | solution.py:35
  256.4 10.9 %all-to-all-done.11.middle = bf16[32,2,16,128]{3,2,1,0:T(8,128)(2,1)S(1)} async-done(((bf16[32,2,16,128]{3,2,1,0:T(8,128)(2,1)}), bf16[32,2,16,128]{3,2,1,0:T(8,128)(2,1)S(1)}, u32[]{:S(2)}, u32[]{:S(2)}) %all-to-all-start.11) | async-done | bytes 262176 | tf_op jit(solution)/shard_map/all_to_all | solution.py:35
  272.4 8.7 %leaf_backward.1 = bf16[32,4,16,128]{3,2,1,0:T(8,128)(2,1)} custom-call(s32[1]{0:T(128)} %bitcast.x_ref, s32[136]{0:T(256)} %pad_add_fusion.lists.table, bf16[32,16,128]{2,1,0:T(8,128)(2,1)} %all_to_all.79.root, bf16[32,16,128]{2,1,0:T(8,128)(2,1)} %all_to_all.81.top, bf16[32,2,16,128]{3,2,1,0:T(8,128)(2,1)} %copy-done.2, ...), custom_call_target="tpu_custom_call" | custom-call | tf_op jit(solution)/shard_map/leaf_backward/pallas_call | solution.py:312
  281.1 17.9 %all_to_all.83 = bf16[32,4,16,128]{3,2,1,0:T(8,128)(2,1)S(1)} all-to-all(bf16[32,4,16,128]{3,2,1,0:T(8,128)(2,1)} %leaf_backward.1), channel_id=1, replica_groups=mesh['layer'=2,'prow'=4,'pcol'=32] {'pcol'}, dimensions={0} | all-to-all | bytes 1048576 | tf_op jit(solution)/shard_map/all_to_all | solution.py:35
  299.1 8.3 %all_to_all.84 = bf16[4,16,128]{2,1,0:T(8,128)(2,1)S(1)} all-to-all(bf16[4,16,128]{2,1,0:T(8,128)(2,1)S(1)} %reduce_sum.84), channel_id=1, replica_groups=mesh['layer'=2,'prow'=4,'pcol'=32] {'prow'}, dimensions={0} | all-to-all | bytes 32768 | tf_op jit(solution)/shard_map/all_to_all | solution.py:415
  307.6 18.2 %all_to_all.85.leaves = bf16[32,64,128]{2,1,0:T(8,128)(2,1)} all-to-all(bf16[32,64,128]{2,1,0:T(8,128)(2,1)S(1)} %broadcast_in_dim.85), channel_id=1, replica_groups=mesh['layer'=2,'prow'=4,'pcol'=32] {'pcol'}, dimensions={0} | all-to-all | bytes 1048576 | tf_op jit(solution)/shard_map/all_to_all | solution.py:35
  325.7 2.7 finish.1
  (139 shorter events, 53.5 us)
Async XLA Ops:
  7.2 85.7 %all-gather.11.cloned.1.call-start = ((), (), s32[]{:S(2)}) async-start(), calls=%async_computation.15 | async-start | bytes 2621440 | tf_op jit(solution)/shard_map/all_gather | solution.py:355
  9.2 84.7 %all-gather.13.cloned.1.call-start = ((), (), s32[]{:S(2)}) async-start(), calls=%async_computation.16 | async-start | bytes 3276800 | tf_op jit(solution)/shard_map/all_gather | solution.py:355
  11.4 117.9 %all-gather.15.cloned.1.call-start = ((), (), s32[]{:S(2)}) async-start(), calls=%async_computation.17 | async-start | bytes 2621440 | tf_op jit(solution)/shard_map/all_gather | solution.py:355
  12.3 260.1 %all-gather.17.cloned.1.call-start = ((), (), s32[]{:S(2)}) async-start(), calls=%async_computation.18 | async-start | bytes 5242880 | tf_op jit(solution)/shard_map/all_gather | solution.py:355
  13.5 259.0 %all-gather.19.cloned.1.call-start = ((), (), s32[]{:S(2)}) async-start(), calls=%async_computation.19 | async-start | bytes 7864320 | tf_op jit(solution)/shard_map/all_gather | solution.py:355
  17.8 14.3 %collective-permute-start.6 = (bf16[4,64,128]{2,1,0:T(8,128)(2,1)S(1)}, bf16[4,64,128]{2,1,0:T(8,128)(2,1)S(1)}, u32[]{:S(2)}, u32[]{:S(2)}) collective-permute-start(bf16[4,64,128]{2,1,0:T(8,128)(2,1)S(1)} %convolution_convert_fusion.own), channel_id=1, source_target_pairs={{0,32},{32,64},{64,96},{96,0},{1,33},{33,65},{65,97},{97,1},{2,34}... | collective-permute-start | bytes 196616 | tf_op jit(solution)/shard_map/ppermute | solution.py:23
  19.3 12.7 %collective-permute-start.7 = (bf16[4,64,128]{2,1,0:T(8,128)(2,1)S(1)}, bf16[4,64,128]{2,1,0:T(8,128)(2,1)S(1)}, u32[]{:S(2)}, u32[]{:S(2)}) collective-permute-start(bf16[4,64,128]{2,1,0:T(8,128)(2,1)S(1)} %convolution_convert_fusion.own), channel_id=1, source_target_pairs={{0,64},{32,96},{64,0},{96,32},{1,65},{33,97},{65,1},{97,33},{2,66}... | collective-permute-start | bytes 196616 | tf_op jit(solution)/shard_map/ppermute | solution.py:23
  22.1 10.0 %collective-permute-start.8 = (bf16[4,64,128]{2,1,0:T(8,128)(2,1)S(1)}, bf16[4,64,128]{2,1,0:T(8,128)(2,1)S(1)}, u32[]{:S(2)}, u32[]{:S(2)}) collective-permute-start(bf16[4,64,128]{2,1,0:T(8,128)(2,1)S(1)} %convolution_convert_fusion.own), channel_id=1, source_target_pairs={{0,96},{32,0},{64,32},{96,64},{1,97},{33,1},{65,33},{97,65},{2,98}... | collective-permute-start | bytes 196616 | tf_op jit(solution)/shard_map/ppermute | solution.py:23
  23.5 4.8 %collective-permute-start.3 = (s32[17,2]{0,1:T(2,128)S(1)}, s32[17,2]{0,1:T(2,128)S(1)}, u32[]{:S(2)}, u32[]{:S(2)}) collective-permute-start(s32[17,2]{0,1:T(2,128)S(1)} %copy-done.20), channel_id=1, source_target_pairs={{0,32},{32,64},{64,96},{96,0},{1,33},{33,65},{65,97},{97,1},{2,34}... | collective-permute-start | bytes 416 | tf_op jit(solution)/shard_map/ppermute | solution.py:23
  24.1 5.1 %collective-permute-start.4 = (s32[17,2]{0,1:T(2,128)S(1)}, s32[17,2]{0,1:T(2,128)S(1)}, u32[]{:S(2)}, u32[]{:S(2)}) collective-permute-start(s32[17,2]{0,1:T(2,128)S(1)} %copy-done.20), channel_id=1, source_target_pairs={{0,64},{32,96},{64,0},{96,32},{1,65},{33,97},{65,1},{97,33},{2,66}... | collective-permute-start | bytes 416 | tf_op jit(solution)/shard_map/ppermute | solution.py:23
  28.3 3.6 %collective-permute-start.5 = (s32[17,2]{0,1:T(2,128)S(1)}, s32[17,2]{0,1:T(2,128)S(1)}, u32[]{:S(2)}, u32[]{:S(2)}) collective-permute-start(s32[17,2]{0,1:T(2,128)S(1)} %copy-done.20), channel_id=1, source_target_pairs={{0,96},{32,0},{64,32},{96,64},{1,97},{33,1},{65,33},{97,65},{2,98}... | collective-permute-start | bytes 416 | tf_op jit(solution)/shard_map/ppermute | solution.py:23
  35.5 46.5 %copy-start.21 = (bf16[8,16,512]{2,1,0:T(8,128)(2,1)S(1)}, bf16[8,16,512]{2,1,0:T(8,128)(2,1)}, u32[]{:S(2)}) copy-start(bf16[8,16,512]{2,1,0:T(8,128)(2,1)} %get-tuple-element.24) | copy-start | bytes 393220
  35.5 7.6 %collective-permute-start.10 = (bf16[4,16,512]{2,1,0:T(8,128)(2,1)}, bf16[4,16,512]{2,1,0:T(8,128)(2,1)S(1)}, u32[]{:S(2)}, u32[]{:S(2)}) collective-permute-start(bf16[4,16,512]{2,1,0:T(8,128)(2,1)} %get-tuple-element.19), channel_id=1, source_target_pairs={{0,64},{32,96},{64,0},{96,32},{1,65},{33,97},{65,1},{97,33},{2,66}... | collective-permute-start | bytes 196616 | tf_op jit(solution)/shard_map/ppermute | solution.py:23
  36.9 7.5 %collective-permute-start.11 = (bf16[4,16,512]{2,1,0:T(8,128)(2,1)}, bf16[4,16,512]{2,1,0:T(8,128)(2,1)S(1)}, u32[]{:S(2)}, u32[]{:S(2)}) collective-permute-start(bf16[4,16,512]{2,1,0:T(8,128)(2,1)} %get-tuple-element.20), channel_id=1, source_target_pairs={{0,96},{32,0},{64,32},{96,64},{1,97},{33,1},{65,33},{97,65},{2,98}... | collective-permute-start | bytes 196616 | tf_op jit(solution)/shard_map/ppermute | solution.py:23
  39.5 7.1 %collective-permute-start.9 = (bf16[4,16,512]{2,1,0:T(8,128)(2,1)}, bf16[4,16,512]{2,1,0:T(8,128)(2,1)S(1)}, u32[]{:S(2)}, u32[]{:S(2)}) collective-permute-start(bf16[4,16,512]{2,1,0:T(8,128)(2,1)} %get-tuple-element.18), channel_id=1, source_target_pairs={{0,32},{32,64},{64,96},{96,0},{1,33},{33,65},{65,97},{97,1},{2,34}... | collective-permute-start | bytes 196616 | tf_op jit(solution)/shard_map/ppermute | solution.py:23
  48.9 22.4 %all-to-all-start = ((bf16[32,2,16,128]{3,2,1,0:T(8,128)(2,1)}), bf16[32,2,16,128]{3,2,1,0:T(8,128)(2,1)S(1)}, u32[]{:S(2)}, u32[]{:S(2)}) async-start(bf16[32,2,16,128]{3,2,1,0:T(8,128)(2,1)} %leaf_spread.1), calls=%async_computation | async-start | bytes 524288 | tf_op jit(solution)/shard_map/all_to_all | solution.py:35
  60.3 5.2 %collective-permute-start.2 = (f32[4,16,128]{2,1,0:T(8,128)S(1)}, f32[4,16,128]{2,1,0:T(8,128)S(1)}, u32[]{:S(2)}, u32[]{:S(2)}) collective-permute-start(f32[4,16,128]{2,1,0:T(8,128)S(1)} %pad_maximum_fusion.4), channel_id=1, source_target_pairs={{0,32},{32,64},{64,96},{96,0},{1,33},{33,65},{65,97},{97,1},{2,34}... | collective-permute-start | bytes 98312 | tf_op jit(solution)/shard_map/ppermute | solution.py:23
  60.4 5.5 %collective-permute-start.1 = (f32[4,16,128]{2,1,0:T(8,128)S(1)}, f32[4,16,128]{2,1,0:T(8,128)S(1)}, u32[]{:S(2)}, u32[]{:S(2)}) collective-permute-start(f32[4,16,128]{2,1,0:T(8,128)S(1)} %pad_maximum_fusion.3), channel_id=1, source_target_pairs={{0,64},{32,96},{64,0},{96,32},{1,65},{33,97},{65,1},{97,33},{2,66}... | collective-permute-start | bytes 98312 | tf_op jit(solution)/shard_map/ppermute | solution.py:23
  62.1 6.0 %collective-permute-start = (f32[4,16,128]{2,1,0:T(8,128)S(1)}, f32[4,16,128]{2,1,0:T(8,128)S(1)}, u32[]{:S(2)}, u32[]{:S(2)}) collective-permute-start(f32[4,16,128]{2,1,0:T(8,128)S(1)} %pad_maximum_fusion.2), channel_id=1, source_target_pairs={{0,96},{32,0},{64,32},{96,64},{1,97},{33,1},{65,33},{97,65},{2,98}... | collective-permute-start | bytes 98312 | tf_op jit(solution)/shard_map/ppermute | solution.py:23
  72.1 20.7 %all-to-all-start.1 = ((bf16[32,2,16,128]{3,2,1,0:T(8,128)(2,1)}), bf16[32,2,16,128]{3,2,1,0:T(8,128)(2,1)S(1)}, u32[]{:S(2)}, u32[]{:S(2)}) async-start(bf16[32,2,16,128]{3,2,1,0:T(8,128)(2,1)} %broadcast_in_dim.74), calls=%async_computation.1 | async-start | bytes 524288 | tf_op jit(solution)/shard_map/all_to_all | solution.py:35
  78.2 9.9 %collective-permute-start.12 = (bf16[8,16,512]{2,1,0:T(8,128)(2,1)S(1)}, bf16[8,16,512]{2,1,0:T(8,128)(2,1)S(1)}, u32[]{:S(2)}, u32[]{:S(2)}) collective-permute-start(bf16[8,16,512]{2,1,0:T(8,128)(2,1)S(1)} %copy-done.23), channel_id=1, source_target_pairs={{0,32},{32,64},{64,96},{96,0},{1,33},{33,65},{65,97},{97,1},{2,34}... | collective-permute-start | bytes 393224 | tf_op jit(solution)/shard_map/ppermute | solution.py:23
  79.8 12.8 %collective-permute-start.13 = (bf16[8,16,512]{2,1,0:T(8,128)(2,1)S(1)}, bf16[8,16,512]{2,1,0:T(8,128)(2,1)S(1)}, u32[]{:S(2)}, u32[]{:S(2)}) collective-permute-start(bf16[8,16,512]{2,1,0:T(8,128)(2,1)S(1)} %copy-done.22), channel_id=1, source_target_pairs={{0,64},{32,96},{64,0},{96,32},{1,65},{33,97},{65,1},{97,33},{2,66}... | collective-permute-start | bytes 393224 | tf_op jit(solution)/shard_map/ppermute | solution.py:23
  82.1 10.8 %collective-permute-start.14 = (bf16[8,16,512]{2,1,0:T(8,128)(2,1)S(1)}, bf16[8,16,512]{2,1,0:T(8,128)(2,1)S(1)}, u32[]{:S(2)}, u32[]{:S(2)}) collective-permute-start(bf16[8,16,512]{2,1,0:T(8,128)(2,1)S(1)} %copy-done.21), channel_id=1, source_target_pairs={{0,96},{32,0},{64,32},{96,64},{1,97},{33,1},{65,33},{97,65},{2,98}... | collective-permute-start | bytes 393224 | tf_op jit(solution)/shard_map/ppermute | solution.py:23
  118.7 14.0 %all-to-all-start.3 = ((bf16[32,16,128]{2,1,0:T(8,128)(2,1)}), bf16[32,16,128]{2,1,0:T(8,128)(2,1)S(1)}, u32[]{:S(2)}, u32[]{:S(2)}) async-start(bf16[32,16,128]{2,1,0:T(8,128)(2,1)} %broadcast_in_dim.76), calls=%async_computation.3 | async-start | bytes 262144 | tf_op jit(solution)/shard_map/all_to_all | solution.py:35
  152.5 1.3 collective-permute-start.15
  251.9 15.5 %all-to-all-start.11 = ((bf16[32,2,16,128]{3,2,1,0:T(8,128)(2,1)}), bf16[32,2,16,128]{3,2,1,0:T(8,128)(2,1)S(1)}, u32[]{:S(2)}, u32[]{:S(2)}) async-start(bf16[32,2,16,128]{3,2,1,0:T(8,128)(2,1)} %broadcast_in_dim.83), calls=%async_computation.11 | async-start | bytes 524288 | tf_op jit(solution)/shard_map/all_to_all | solution.py:35
  268.1 13.0 %collective-permute-start.16 = (bf16[8,4,16,128]{3,2,1,0:T(8,128)(2,1)S(1)}, bf16[8,4,16,128]{3,2,1,0:T(8,128)(2,1)S(1)}, u32[]{:S(2)}, u32[]{:S(2)}) collective-permute-start(bf16[8,4,16,128]{3,2,1,0:T(8,128)(2,1)S(1)} %get-tuple-element.38), channel_id=1, source_target_pairs={{0,32},{32,64},{64,96},{96,0},{1,33},{33,65},{65,97},{97,1},{2,34}... | collective-permute-start | bytes 393224 | tf_op jit(solution)/shard_map/ppermute | solution.py:23
  268.5 12.5 %collective-permute-start.17 = (bf16[8,4,16,128]{3,2,1,0:T(8,128)(2,1)S(1)}, bf16[8,4,16,128]{3,2,1,0:T(8,128)(2,1)S(1)}, u32[]{:S(2)}, u32[]{:S(2)}) collective-permute-start(bf16[8,4,16,128]{3,2,1,0:T(8,128)(2,1)S(1)} %get-tuple-element.37), channel_id=1, source_target_pairs={{0,64},{32,96},{64,0},{96,32},{1,65},{33,97},{65,1},{97,33},{2,66}... | collective-permute-start | bytes 393224 | tf_op jit(solution)/shard_map/ppermute | solution.py:23
  270.4 10.7 %collective-permute-start.18 = (bf16[8,4,16,128]{3,2,1,0:T(8,128)(2,1)S(1)}, bf16[8,4,16,128]{3,2,1,0:T(8,128)(2,1)S(1)}, u32[]{:S(2)}, u32[]{:S(2)}) collective-permute-start(bf16[8,4,16,128]{3,2,1,0:T(8,128)(2,1)S(1)} %get-tuple-element.36), channel_id=1, source_target_pairs={{0,96},{32,0},{64,32},{96,64},{1,97},{33,1},{65,33},{97,65},{2,98}... | collective-permute-start | bytes 393224 | tf_op jit(solution)/shard_map/ppermute | solution.py:23
  281.1 44.7 %copy-start.11 = (bf16[8,4,16,128]{3,2,1,0:T(8,128)(2,1)}, bf16[8,4,16,128]{3,2,1,0:T(8,128)(2,1)S(1)}, u32[]{:S(2)}) copy-start(bf16[8,4,16,128]{3,2,1,0:T(8,128)(2,1)S(1)} %collective-permute-done.16.e1) | copy-start | bytes 393220
  281.1 44.6 %copy-start.12 = (bf16[8,4,16,128]{3,2,1,0:T(8,128)(2,1)}, bf16[8,4,16,128]{3,2,1,0:T(8,128)(2,1)S(1)}, u32[]{:S(2)}) copy-start(bf16[8,4,16,128]{3,2,1,0:T(8,128)(2,1)S(1)} %collective-permute-done.17.e2) | copy-start | bytes 393220
  281.1 44.6 %copy-start.13 = (bf16[8,4,16,128]{3,2,1,0:T(8,128)(2,1)}, bf16[8,4,16,128]{3,2,1,0:T(8,128)(2,1)S(1)}, u32[]{:S(2)}) copy-start(bf16[8,4,16,128]{3,2,1,0:T(8,128)(2,1)S(1)} %collective-permute-done.18.e3) | copy-start | bytes 393220
  (21 other events, 217.2 us)
Sparse Core Ops, SparseCore 0:
  9.8 38.7 all-gather.10
  50.5 43.4 all-gather.12
  95.7 33.5 all-gather.14
  130.9 50.8 all-gather.16
  184.1 68.5 all-gather.18

commit v3 on v2

v3 whole, which is shorter than its diff:
```python
import jax
import jax.numpy as jnp
from jax import lax
from jax.experimental import pallas as pl
from jax.experimental.pallas import tpu as pltpu
from jax.sharding import PartitionSpec as P

NX = 4
NP = 32
RX = 16
BF = jnp.bfloat16
F32 = jnp.float32
LIMIT = 56 * 1024 * 1024

SMEM = pl.BlockSpec(memory_space=pltpu.SMEM)
VMEM = pl.BlockSpec(memory_space=pltpu.VMEM)


def whole(*shape):
    return pl.BlockSpec(shape, lambda n: (0,) * len(shape))


def params():
    return pltpu.CompilerParams(vmem_limit_bytes=LIMIT)


def shift(value, distance):
    return lax.ppermute(value, "prow", [(i, (i + distance) % NX) for i in range(NX)])


def around(value):
    return [value] + [shift(value, distance) for distance in range(1, NX)]


def after(value, *earlier):
    return lax.optimization_barrier((value, *earlier))[0]


def exchange(value):
    return lax.all_to_all(value, "pcol", 0, 0, tiled=True)


def reduce_columns(parts):
    return jnp.sum(exchange(parts).astype(F32), axis=0)


def gather_columns(chunk):
    chunk = chunk.astype(BF)
    return exchange(jnp.broadcast_to(chunk[None], (NP,) + chunk.shape))


def dot(left, right):
    return lax.dot_general(left, right, (((1,), (0,)), ((), ())), preferred_element_type=F32)


def dot_t(left, right):
    return lax.dot_general(left, right, (((1,), (1,)), ((), ())), preferred_element_type=F32)


def row_start(x, distance):
    return pl.multiple_of(lax.rem(x + distance, NX) * RX, RX)


def source(x, distance):
    return lax.rem(x + (NX - distance), NX)


def start_kernel(place, right_sub, right_root, inverse, inverse_root, factor, lists, own, *rest):
    pieces, (middle, top, leaf, rights, inverses, sems) = rest[0:4], rest[4:]
    row, column = place[0], place[1]

    def copy(source_ref, target_ref, index):
        pltpu.make_async_copy(source_ref, target_ref, sems.at[index]).start()

    copy(right_sub.at[3:7], rights, 0)
    copy(inverse.at[3:7], inverses, 1)

    def factor_copy(pair, target, first, index):
        for c in range(4):
            copy(factor.at[pair, :, 128 * c : 128 * (c + 1)], target.at[first + c], index)

    for m in range(2):
        copy(inverse.at[1 + m], middle.at[m, 0:8], 2)
        for i in range(2):
            factor_copy(1 + 2 * m + i, middle.at[m], 8 + 4 * i, 2)
    for d in range(NX):
        rows = pl.ds(row_start(row, d), RX)
        columns = pl.ds(pl.multiple_of(128 * column, 128), 128)
        copy(right_sub.at[0:3, rows, columns], pieces[d].at[0:3], 5 + d)
        copy(right_root.at[rows, columns], pieces[d].at[3], 5 + d)
        copy(lists, pieces[d].at[4], 5 + d)
    copy(inverse_root, top.at[0:8], 3)
    copy(inverse.at[0], top.at[8:16], 3)
    factor_copy(0, top, 16, 3)

    def leaf_copies(n, carry):
        copy(inverse.at[3 + n], leaf.at[n, 0:8], 4)
        for i in range(3):
            factor_copy(5 + 3 * n + i, leaf.at[n], (12, 16, 8)[i], 4)
        return carry

    lax.fori_loop(0, 4, leaf_copies, 0)
    pltpu.make_async_copy(rights, rights, sems.at[0]).wait()
    pltpu.make_async_copy(inverses, inverses, sems.at[1]).wait()
    for n in range(4):
        own[n] = dot(rights[n].astype(BF), inverses[n].reshape(1024, 128)).astype(BF)
    for target, index in ((middle, 2), (top, 3), (leaf, 4)):
        pltpu.make_async_copy(target, target, sems.at[index]).wait()
    for d in range(NX):
        pltpu.make_async_copy(pieces[d], pieces[d], sems.at[5 + d]).wait()


def start(place, right_sub, right_root, inverse, inverse_root, factor, lists):
    hbm = pl.BlockSpec(memory_space=pl.ANY)
    result = pl.pallas_call(
        start_kernel,
        out_shape=[jax.ShapeDtypeStruct((4, 64, 128), BF)]
        + [jax.ShapeDtypeStruct((5, RX, 128), F32)] * 4
        + [
            jax.ShapeDtypeStruct((2, 16, 128, 128), BF),
            jax.ShapeDtypeStruct((20, 128, 128), BF),
            jax.ShapeDtypeStruct((4, 20, 128, 128), BF),
        ],
        in_specs=[SMEM] + [hbm] * 6,
        out_specs=[VMEM] * 8,
        scratch_shapes=[
            pltpu.VMEM((4, 64, 1024), F32),
            pltpu.VMEM((4, 8, 128, 128), BF),
            pltpu.SemaphoreType.DMA((9,)),
        ],
        compiler_params=params(),
        name="start",
    )(
        place,
        right_sub,
        right_root,
        inverse.reshape(7, 8, 128, 128),
        inverse_root.reshape(8, 128, 128),
        factor,
        lists,
    )
    return result[0], result[1:5], result[5], result[6], result[7]


def leaf_update_kernel(x_ref, own, r1, r2, r3, f0, f1, f2, fwd, *rest):
    crit, other = rest[0:4], rest[4:8]
    x, n = x_ref[0], pl.program_id(0)

    def total(d):
        rows = pl.ds(row_start(x, d), RX)
        parts = [part[n, rows, :].astype(F32) for part in (own, r1, r2, r3)]
        return (parts[0] + parts[1]) + (parts[2] + parts[3])

    solved = [total(d) for d in range(NX)]
    fwd[n] = solved[0]
    left = jnp.concatenate(solved, axis=0).astype(BF)
    for i, factor in enumerate((f0, f1, f2)):
        update = dot(left, factor[0]).astype(BF)
        for d in range(NX):
            piece = update[RX * d : RX * (d + 1)]
            if i == 2:
                crit[d][n] = piece
            else:
                other[d][2 * n + i] = piece


def leaf_update(x, own, received, factor):
    part = whole(4, 64, 128)
    result = pl.pallas_call(
        leaf_update_kernel,
        grid=(4,),
        out_shape=[jax.ShapeDtypeStruct((4, RX, 128), F32)]
        + [jax.ShapeDtypeStruct((4, RX, 512), BF)] * 4
        + [jax.ShapeDtypeStruct((8, RX, 512), BF)] * 4,
        in_specs=[SMEM]
        + [part] * 4
        + [pl.BlockSpec((1, 128, 512), lambda n, i=i: (5 + 3 * n + i, 0, 0)) for i in range(3)],
        out_specs=[whole(4, RX, 128)] + [whole(4, RX, 512)] * 4 + [whole(8, RX, 512)] * 4,
        compiler_params=params(),
        name="leaf_update",
    )(x, own, *received, factor, factor, factor)
    return result[0], result[1:5], result[5:9]


def listed(table, distance, pair, j):
    return table[(distance * 17 + pair) * 2 + j]


def add_update(acc, table, distance, pair, update, *lead):
    for j in range(2):
        block = listed(table, distance, pair, j)
        for h in range(2):
            index = (2 * block + h, *lead)
            tile = update[:, 256 * j + 128 * h : 256 * j + 128 * (h + 1)]
            acc[index] = acc[index] + tile.astype(F32)


def leaf_spread_kernel(lists, c0, c1, c2, c3, out, acc):
    acc[...] = jnp.zeros(acc.shape, F32)
    for d, crit in enumerate((c0, c1, c2, c3)):
        for n in range(4):
            add_update(acc, lists, d, 5 + 3 * n + 2, crit[n], n // 2)
    out[...] = acc[...].astype(BF)


def leaf_spread(lists, crit):
    return pl.pallas_call(
        leaf_spread_kernel,
        out_shape=jax.ShapeDtypeStruct((NP, 2, RX, 128), BF),
        in_specs=[SMEM] + [pl.BlockSpec(memory_space=pltpu.VMEM)] * 4,
        scratch_shapes=[pltpu.VMEM((NP, 2, RX, 128), F32)],
        compiler_params=params(),
        name="leaf_spread",
    )(lists, *crit)


def inverse_share(tiles):
    return tiles.reshape(1024, 128)


def factor_share(tiles):
    return jnp.concatenate([tiles[c] for c in range(4)], axis=1)


def solve_columns(values, inverse, *lead):
    total = None
    for r in range(NX):
        left = jnp.concatenate([values[(8 * r + k, *lead)] for k in range(8)], axis=1)
        term = dot(left, inverse(r))
        total = term if total is None else total + term
    return total


def solve_rows(target, inverse, store):
    for r in range(NX):
        wide = dot_t(target, inverse(r)).astype(BF)
        for k in range(8):
            store(r, k, wide[:, 128 * k : 128 * (k + 1)])


def multiply_update(acc, x, table, pair, rounded, factor, *lead):
    for r in range(NX):
        update = dot(rounded, factor(r))
        add_update(acc, table, source(x, r), pair, update, *lead)


def pick_product(x, table, pair, values, factor, *lead):
    total = None
    for r in range(NX):
        tiles = []
        for j in range(2):
            block = listed(table, source(x, r), pair, j)
            tiles += [values[(2 * block, *lead)], values[(2 * block + 1, *lead)]]
        term = dot_t(jnp.concatenate(tiles, axis=1), factor(r))
        total = term if total is None else total + term
    return total


TILES = whole(NP, RX, 128)
TOP_INVERSE = pl.BlockSpec((NX, 8, 128, 128), lambda n: (0, 1, 0, 0))
TOP_FACTOR = pl.BlockSpec((NX, 4, 128, 128), lambda n: (0, 4, 0, 0))


def middle_inverse(weights, m):
    return lambda r: inverse_share(weights[r, m, 0:8])


def middle_factor(weights, m, i):
    return lambda r: factor_share(weights[r, m, 8 + 4 * i : 12 + 4 * i])


def middle_forward_kernel(x_ref, table, values, weights, o0, o1, o2, o3, fwd, out, acc_root, acc):
    x = x_ref[0]
    acc[...] = jnp.zeros(acc.shape, F32)
    acc_root[...] = jnp.zeros(acc_root.shape, F32)
    for d, other in enumerate((o0, o1, o2, o3)):
        for n in range(4):
            add_update(acc_root, table, d, 5 + 3 * n, other[2 * n])
            add_update(acc, table, d, 5 + 3 * n + 1, other[2 * n + 1])
    for m in range(2):
        solved = solve_columns(values, middle_inverse(weights, m), m)
        fwd[m] = solved
        rounded = solved.astype(BF)
        multiply_update(acc_root, x, table, 1 + 2 * m, rounded, middle_factor(weights, m, 0))
        multiply_update(acc, x, table, 2 + 2 * m, rounded, middle_factor(weights, m, 1))
    out[...] = acc[...].astype(BF)


def middle_forward(x, table, values, weights, other):
    return pl.pallas_call(
        middle_forward_kernel,
        out_shape=[
            jax.ShapeDtypeStruct((2, RX, 128), F32),
            jax.ShapeDtypeStruct((NP, RX, 128), BF),
            jax.ShapeDtypeStruct((NP, RX, 128), F32),
        ],
        in_specs=[SMEM] * 2 + [VMEM] * 6,
        scratch_shapes=[pltpu.VMEM((NP, RX, 128), F32)],
        compiler_params=params(),
        name="middle_forward",
    )(x, table, values, weights, *other)


def top_forward_kernel(x_ref, table, values, inverse, factor, acc_in, fwd, out, acc):
    acc[...] = acc_in[...]
    solved = solve_columns(values, lambda r: inverse_share(inverse[r]))
    fwd[...] = solved
    multiply_update(
        acc, x_ref[0], table, 0, solved.astype(BF), lambda r: factor_share(factor[r])
    )
    out[...] = acc[...].astype(BF)


def top_forward(x, table, values, weights, acc_root):
    return pl.pallas_call(
        top_forward_kernel,
        grid=(1,),
        out_shape=[
            jax.ShapeDtypeStruct((RX, 128), F32),
            jax.ShapeDtypeStruct((NP, RX, 128), BF),
        ],
        in_specs=[SMEM] * 2 + [TILES, TOP_INVERSE, TOP_FACTOR, TILES],
        out_specs=[whole(RX, 128), TILES],
        scratch_shapes=[pltpu.VMEM((NP, RX, 128), F32)],
        compiler_params=params(),
        name="top_forward",
    )(x, table, values, weights, weights, acc_root)


def root_kernel(values, weights, out):
    inverse = lambda r: inverse_share(weights[r])
    rounded = solve_columns(values, inverse).astype(BF)

    def store(r, k, tile):
        out[8 * r + k] = tile

    solve_rows(rounded, inverse, store)


def root_solve(values, weights):
    return pl.pallas_call(
        root_kernel,
        grid=(1,),
        out_shape=jax.ShapeDtypeStruct((NP, RX, 128), BF),
        in_specs=[TILES, whole(NX, 8, 128, 128)],
        out_specs=TILES,
        compiler_params=params(),
        name="root_solve",
    )(values, weights)


def top_backward_kernel(x_ref, table, root, fwd, inverse, factor, out):
    down = pick_product(x_ref[0], table, 0, root, lambda r: factor_share(factor[r]))

    def store(r, k, tile):
        out[8 * r + k] = tile

    solve_rows((fwd[...] - down).astype(BF), lambda r: inverse_share(inverse[r]), store)


def top_backward(x, table, root, fwd, weights):
    return pl.pallas_call(
        top_backward_kernel,
        grid=(1,),
        out_shape=jax.ShapeDtypeStruct((NP, RX, 128), BF),
        in_specs=[SMEM] * 2 + [TILES, whole(RX, 128), TOP_INVERSE, TOP_FACTOR],
        out_specs=TILES,
        compiler_params=params(),
        name="top_backward",
    )(x, table, root, fwd, weights, weights)


def middle_backward_kernel(x_ref, table, root, top, fwd, weights, out):
    x = x_ref[0]
    for m in range(2):
        down = pick_product(x, table, 1 + 2 * m, root, middle_factor(weights, m, 0))
        down = down + pick_product(x, table, 2 + 2 * m, top, middle_factor(weights, m, 1))

        def store(r, k, tile, m=m):
            out[8 * r + k, m] = tile

        solve_rows((fwd[m] - down).astype(BF), middle_inverse(weights, m), store)


def middle_backward(x, table, root, top, fwd, weights):
    return pl.pallas_call(
        middle_backward_kernel,
        out_shape=jax.ShapeDtypeStruct((NP, 2, RX, 128), BF),
        in_specs=[SMEM] * 2 + [VMEM] * 4,
        compiler_params=params(),
        name="middle_backward",
    )(x, table, root, top, fwd, weights)


def leaf_down_kernel(x_ref, table, root, top, fwd, to_root, to_top, out):
    x = x_ref[0]
    first = 5 + 3 * pl.program_id(0)
    down = pick_product(x, table, first, root, lambda r: factor_share(to_root[r, 0]))
    down = down + pick_product(x, table, first + 1, top, lambda r: factor_share(to_top[r, 0]))
    out[0] = fwd[0] - down


def leaf_down(x, table, root, top, fwd, weights):
    factor_at = lambda i: pl.BlockSpec((NX, 1, 4, 128, 128), lambda n: (0, n, i, 0, 0))
    return pl.pallas_call(
        leaf_down_kernel,
        grid=(4,),
        out_shape=jax.ShapeDtypeStruct((4, RX, 128), F32),
        in_specs=[SMEM] * 2
        + [TILES, TILES, pl.BlockSpec((1, RX, 128), lambda n: (n, 0, 0)), factor_at(3), factor_at(4)],
        out_specs=pl.BlockSpec((1, RX, 128), lambda n: (n, 0, 0)),
        compiler_params=params(),
        name="leaf_down",
    )(x, table, root, top, fwd, weights, weights)


def leaf_backward_kernel(x_ref, table, middle, fwd, weights, out):
    x, n = x_ref[0], pl.program_id(0)
    down = pick_product(
        x, table, 7 + 3 * n, middle, lambda r: factor_share(weights[r, 0, 8:12]), n // 2
    )

    def store(r, k, tile):
        out[k, lax.rem(r + NX - x, NX)] = tile

    inverse = lambda r: inverse_share(weights[r, 0, 0:8])
    solve_rows((fwd[0] - down).astype(BF), inverse, store)


def leaf_backward(x, table, middle, fwd, weights):
    return pl.pallas_call(
        leaf_backward_kernel,
        grid=(4,),
        out_shape=jax.ShapeDtypeStruct((NP, NX, RX, 128), BF),
        in_specs=[SMEM] * 2
        + [
            whole(NP, 2, RX, 128),
            pl.BlockSpec((1, RX, 128), lambda n: (n, 0, 0)),
            pl.BlockSpec((NX, 1, 12, 128, 128), lambda n: (0, n, 0, 0, 0)),
        ],
        out_specs=pl.BlockSpec((8, NX, RX, 128), lambda n: (n, 0, 0, 0)),
        compiler_params=params(),
        name="leaf_backward",
    )(x, table, middle, fwd, weights)


def finish_kernel(x_ref, e0, e1, e2, e3, leaves, out_sub, out_root):
    x = x_ref[0]
    for d, early in enumerate((e0, e1, e2, e3)):
        rows = pl.ds(pl.multiple_of(RX * source(x, d), RX), RX)
        for k in range(8):
            columns = slice(128 * k, 128 * (k + 1))
            out_root[rows, columns] = early[k, 0].astype(F32)
            for t in range(3):
                out_sub[t, rows, columns] = early[k, 1 + t].astype(F32)
            for t in range(4):
                out_sub[3 + t, rows, columns] = leaves[8 * t + k, d].astype(F32)


def finish(x, early, leaves):
    return pl.pallas_call(
        finish_kernel,
        out_shape=[
            jax.ShapeDtypeStruct((7, 64, 1024), F32),
            jax.ShapeDtypeStruct((64, 1024), F32),
        ],
        in_specs=[SMEM] + [pl.BlockSpec(memory_space=pltpu.VMEM)] * 5,
        compiler_params=params(),
        name="finish",
    )(x, *early, leaves)


def gather_rows(value):
    return lax.all_gather(value, "prow")


def per_device(right_sub, right_root, inverse_sub, inverse_root, factor_blocks, block_lists):
    position = lax.axis_index("prow").astype(jnp.int32)
    column = lax.axis_index("pcol").astype(jnp.int32)
    x = position[None]
    lists = jnp.pad(block_lists.astype(F32).reshape(1, 34), ((0, RX - 1), (0, 94)))
    own, pieces, middle_weights, top_weights, leaf_weights = start(
        jnp.stack([position, column % 8]),
        right_sub,
        right_root,
        inverse_sub,
        inverse_root,
        factor_blocks,
        lists,
    )
    middle_weights = gather_rows(middle_weights)
    top_weights = gather_rows(top_weights)
    leaf_weights = gather_rows(leaf_weights)

    received = around(own)
    pieces = [pieces[0]] + [shift(pieces[d], d) for d in range(1, NX)]
    table = jnp.concatenate([piece[4, 0, :34] for piece in pieces]).astype(jnp.int32)
    held = lax.rem(position + NX - column // 8, NX)
    right = pieces[0][:4]
    for d in range(1, NX):
        right = jnp.where(held == d, pieces[d][:4], right)

    fwd_leaf, crit, other = leaf_update(x, own, received[1:], factor_blocks)
    crit = [crit[0]] + [shift(crit[d], d) for d in range(1, NX)]
    other = [other[0]] + [shift(other[d], d) for d in range(1, NX)]
    crit[0], right = lax.optimization_barrier((crit[0], right))
    parts = leaf_spread(table, crit)

    values = gather_columns(right[1:3] - reduce_columns(parts))
    fwd_middle, parts, acc_root = middle_forward(x, table, values, middle_weights, other)
    values = gather_columns(right[0] - reduce_columns(parts))
    fwd_top, parts = top_forward(x, table, values, top_weights, acc_root)
    total = reduce_columns(parts)
    total = total + lax.ppermute(total, "layer", [(0, 1), (1, 0)])
    values = gather_columns(right[3] - total)
    root = gather_columns(reduce_columns(root_solve(values, top_weights)))
    parts = top_backward(x, table, root, fwd_top, top_weights)
    top = gather_columns(reduce_columns(parts))
    parts = middle_backward(x, table, root, top, fwd_middle, middle_weights)
    fwd_leaf = leaf_down(x, table, root, top, fwd_leaf, leaf_weights)
    middle = gather_columns(reduce_columns(parts))

    early = jnp.concatenate([root[:, None], top[:, None], middle], 1)
    pieces = []
    for d in range(NX):
        piece = lax.dynamic_slice_in_dim(early, 8 * lax.rem(position + d, NX), 8, 0)
        pieces.append(shift(piece, d) if d else piece)

    parts = leaf_backward(x, table, middle, fwd_leaf, leaf_weights)
    chunk = reduce_columns(parts).astype(BF)
    chunk = jnp.stack([chunk[0]] + [shift(chunk[d], d) for d in range(1, NX)])
    leaves = gather_columns(after(chunk, *pieces))
    return tuple(finish(x, pieces, leaves))


def solution(mesh):
    in_specs = (
        P("layer", None, "prow"),
        P(None, "prow"),
        P("layer", "prow", "pcol"),
        P("prow", "pcol"),
        P("layer", "pcol", "prow"),
        P("layer", "prow"),
    )
    out_specs = (P("layer", None, "prow"), P(None, "prow"))
    return jax.shard_map(
        per_device, mesh=mesh, in_specs=in_specs, out_specs=out_specs, check_vma=False
    )
```

time: 336 us -> 321 us (0.955)
  Pallas kernels: 33.6 us -> 42.4 us
  starting transfers between devices: 49.9 us -> 41.2 us
  blocking collectives: 167 us -> 159 us
  local copies, waits for them, and re-layouts: 15.1 us -> 7.74 us
    pallas_call x1 -> x3, Pallas kernels: 2.79 us -> 14 us  [the longest x1 5.68 us: start(): pl.pallas_call(start_kernel, out_shape=[jax.ShapeDtypeStruct((4, 64, 128)...]
    all_to_all x1 -> x0, blocking collectives: 8.31 us -> none  [per_device(): chunk = lax.all_to_all(chunk, 'prow', 0, 0, tiled=True).reshape(4 * RX, 128)]
    all_to_all x4, waiting for transfers between devices: 17.7 us -> 25.9 us  [exchange(): return lax.all_to_all(value, 'pcol', 0, 0, tiled=True)]
    all_to_all x4, starting transfers between devices: 26.1 us -> 18 us  [exchange(): return lax.all_to_all(value, 'pcol', 0, 0, tiled=True)]
    slice x6 -> x1, local copies, waits for them, and re-layouts: 7.75 us -> 0.01 us  [per_device(): chunk = jnp.stack([chunk[0]] + [shift(chunk[d], d) for d in range(1, NX)])]
    all_gather x5 -> x3, waiting for transfers between devices: 7.36 us -> 0.04 us  [gather_rows(): return lax.all_gather(value, 'prow')]
  transfers between devices with their start and end apart: 28 -> 26, of which waited for: 18 -> 16; matrix products, arithmetic and copies ran while one was open for 4% -> 2% of each run, Pallas kernels for 9% -> 9%
where the time goes in v3:
time: 321 us; the launch traced here: 319 us
  blocking collectives  159 us (50%)
  waiting for transfers between devices  51.9 us (16%)
  Pallas kernels  42.4 us (13%)
  starting transfers between devices  41.2 us (13%)
  between operations  14.1 us (4%)
  local copies, waits for them, and re-layouts  7.74 us (2%)
  other arithmetic  3.33 us (1%)
    all_to_all x10, blocking collectives, exchange(): return lax.all_to_all(value, 'pcol', 0, 0, tiled=True)  159 us
    all_to_all x4, waiting for transfers between devices, exchange(): return lax.all_to_all(value, 'pcol', 0, 0, tiled=True)  25.9 us
    ppermute x18, waiting for transfers between devices, shift(): lax.ppermute(value, 'prow', [(i, (i + distance) % NX) for i in range(NX)])  23.4 us
    ppermute x18, starting transfers between devices, shift(): lax.ppermute(value, 'prow', [(i, (i + distance) % NX) for i in range(NX)])  23 us
    all_to_all x4, starting transfers between devices, exchange(): return lax.all_to_all(value, 'pcol', 0, 0, tiled=True)  18 us
  transfers between devices with their start and end apart: 26, of which 16 were waited for; matrix products, arithmetic and copies ran while one was open for 2% of the time, Pallas kernels for 9%

profile of v3, /device:TPU:32, one launch (start us, length us, event | category | flops | bytes accessed | tf_op | source)
XLA Modules:
  0.0 319.3 jit_solution(10329588459627665471)
XLA Ops:
  9.4 5.7 %start.1 = (bf16[4,64,128]{2,1,0:T(8,128)(2,1)}, f32[5,16,128]{2,1,0:T(8,128)}, f32[5,16,128]{2,1,0:T(8,128)}, f32[5,16,128]{2,1,0:T(8,128)}, f32[5,16,128]{2,1,...) custom-call(s32[2]{0:T(128)} %pad_add_fusion.place, ...), custom_call_target="tpu_custom_call" | custom-call | tf_op jit(solution)/shard_map/start/pallas_call | solution.py:115
  18.2 2.7 collective-permute-start.1
  28.0 3.6 %collective-permute-done.5 = f32[5,16,128]{2,1,0:T(8,128)S(1)} collective-permute-done((f32[5,16,128]{2,1,0:T(8,128)S(1)}, f32[5,16,128]{2,1,0:T(8,128)S(1)}, u32[]{:S(2)}, u32[]{:S(2)}) %collective-permute-start.5) | collective-permute-done | bytes 40992 | tf_op jit(solution)/shard_map/ppermute | solution.py:28
  32.9 3.8 %leaf_update.1 = (f32[4,16,128]{2,1,0:T(8,128)}, bf16[4,16,512]{2,1,0:T(8,128)(2,1)}, bf16[4,16,512]{2,1,0:T(8,128)(2,1)}, bf16[4,16,512]{2,1,0:T(8,128)(2,1)}, ...) custom-call(s32[1]{0:T(128)} %bitcast.x_ref, ...), custom_call_target="tpu_custom_call" | custom-call | tf_op jit(solution)/shard_map/leaf_update/pallas_call | solution.py:169
  40.6 3.5 %collective-permute-done.6.c1 = bf16[4,16,512]{2,1,0:T(8,128)(2,1)S(1)} collective-permute-done((bf16[4,16,512]{2,1,0:T(8,128)(2,1)}, bf16[4,16,512]{2,1,0:T(8,128)(2,1)S(1)}, u32[]{:S(2)}, u32[]{:S(2)}) %collective-permute-start.6) | collective-permute-done | bytes 65568 | tf_op jit(solution)/shard_map/ppermute | solution.py:28
  49.2 22.4 %all_to_all.70 = bf16[32,2,16,128]{3,2,1,0:T(8,128)(2,1)S(1)} all-to-all(bf16[32,2,16,128]{3,2,1,0:T(8,128)(2,1)} %leaf_spread.1), channel_id=1, replica_groups=mesh['layer'=2,'prow'=4,'pcol'=32] {'pcol'}, dimensions={0} | all-to-all | bytes 524288 | tf_op jit(solution)/shard_map/all_to_all | solution.py:40
  72.4 4.4 %all-to-all-start.1 = ((bf16[32,2,16,128]{3,2,1,0:T(8,128)(2,1)}), bf16[32,2,16,128]{3,2,1,0:T(8,128)(2,1)S(1)}, u32[]{:S(2)}, u32[]{:S(2)}) async-start(bf16[32,2,16,128]{3,2,1,0:T(8,128)(2,1)} %broadcast_in_dim.23), calls=%async_computation.1 | async-start | bytes 524288 | tf_op jit(solution)/shard_map/all_to_all | solution.py:40
  80.4 4.3 %collective-permute-done.9.o1 = bf16[8,16,512]{2,1,0:T(8,128)(2,1)S(1)} collective-permute-done((bf16[8,16,512]{2,1,0:T(8,128)(2,1)}, bf16[8,16,512]{2,1,0:T(8,128)(2,1)S(1)}, u32[]{:S(2)}, u32[]{:S(2)}) %collective-permute-start.9) | collective-permute-done | bytes 131104 | tf_op jit(solution)/shard_map/ppermute | solution.py:28
  88.5 4.0 %middle_forward.1 = (f32[2,16,128]{2,1,0:T(8,128)}, bf16[32,16,128]{2,1,0:T(8,128)(2,1)}, f32[32,16,128]{2,1,0:T(8,128)}) custom-call(s32[1]{0:T(128)} %bitcast.x_ref, s32[136]{0:T(256)} %maximum_convert_fusion.lists.table, bf16[32,2,16,128]{3,2,1,0:T(8,128)(2,1)} %copy-done.3, bf16[4,2,16,128,128]{4,3,2,1,0:T(8,128)(2,1)} %bitcast.46, ...), custom_call_target="tpu_custom_call" | custom-call | tf_op jit(solution)/shard_map/middle_forward/pallas_call | solution.py:290
  92.5 17.5 %all_to_all.71 = bf16[32,16,128]{2,1,0:T(8,128)(2,1)S(1)} all-to-all(bf16[32,16,128]{2,1,0:T(8,128)(2,1)} %get-tuple-element.43), channel_id=1, replica_groups=mesh['layer'=2,'prow'=4,'pcol'=32] {'pcol'}, dimensions={0} | all-to-all | bytes 262144 | tf_op jit(solution)/shard_map/all_to_all | solution.py:40
  110.7 4.6 %all-to-all-start.3 = ((bf16[32,16,128]{2,1,0:T(8,128)(2,1)}), bf16[32,16,128]{2,1,0:T(8,128)(2,1)S(1)}, u32[]{:S(2)}, u32[]{:S(2)}) async-start(bf16[32,16,128]{2,1,0:T(8,128)(2,1)} %broadcast_in_dim.25), calls=%async_computation.3 | async-start | bytes 262144 | tf_op jit(solution)/shard_map/all_to_all | solution.py:40
  115.4 9.8 %all-to-all-done.3.values = bf16[32,16,128]{2,1,0:T(8,128)(2,1)S(1)} async-done(((bf16[32,16,128]{2,1,0:T(8,128)(2,1)}), bf16[32,16,128]{2,1,0:T(8,128)(2,1)S(1)}, u32[]{:S(2)}, u32[]{:S(2)}) %all-to-all-start.3) | async-done | bytes 131104 | tf_op jit(solution)/shard_map/all_to_all | solution.py:40
  125.8 2.9 top_forward.1
  128.7 14.1 %all_to_all.72 = bf16[32,16,128]{2,1,0:T(8,128)(2,1)S(1)} all-to-all(bf16[32,16,128]{2,1,0:T(8,128)(2,1)} %get-tuple-element.46), channel_id=1, replica_groups=mesh['layer'=2,'prow'=4,'pcol'=32] {'pcol'}, dimensions={0} | all-to-all | bytes 262144 | tf_op jit(solution)/shard_map/all_to_all | solution.py:40
  144.1 14.6 %all_to_all.73.values = bf16[32,16,128]{2,1,0:T(8,128)(2,1)} all-to-all(bf16[32,16,128]{2,1,0:T(8,128)(2,1)S(1)} %broadcast_in_dim.26), channel_id=1, replica_groups=mesh['layer'=2,'prow'=4,'pcol'=32] {'pcol'}, dimensions={0} | all-to-all | bytes 262144 | tf_op jit(solution)/shard_map/all_to_all | solution.py:40
  161.3 14.1 %all_to_all.74 = bf16[32,16,128]{2,1,0:T(8,128)(2,1)S(1)} all-to-all(bf16[32,16,128]{2,1,0:T(8,128)(2,1)} %root_solve.1), channel_id=1, replica_groups=mesh['layer'=2,'prow'=4,'pcol'=32] {'pcol'}, dimensions={0} | all-to-all | bytes 262144 | tf_op jit(solution)/shard_map/all_to_all | solution.py:40
  175.5 14.1 %all_to_all.75.root = bf16[32,16,128]{2,1,0:T(8,128)(2,1)} all-to-all(bf16[32,16,128]{2,1,0:T(8,128)(2,1)S(1)} %broadcast_in_dim.27), channel_id=1, replica_groups=mesh['layer'=2,'prow'=4,'pcol'=32] {'pcol'}, dimensions={0} | all-to-all | bytes 262144 | tf_op jit(solution)/shard_map/all_to_all | solution.py:40
  189.5 3.0 top_backward.1
  192.5 14.3 %all_to_all.76 = bf16[32,16,128]{2,1,0:T(8,128)(2,1)S(1)} all-to-all(bf16[32,16,128]{2,1,0:T(8,128)(2,1)} %top_backward.1), channel_id=1, replica_groups=mesh['layer'=2,'prow'=4,'pcol'=32] {'pcol'}, dimensions={0} | all-to-all | bytes 262144 | tf_op jit(solution)/shard_map/all_to_all | solution.py:40
  206.9 14.0 %all_to_all.77.top = bf16[32,16,128]{2,1,0:T(8,128)(2,1)} all-to-all(bf16[32,16,128]{2,1,0:T(8,128)(2,1)S(1)} %broadcast_in_dim.29), channel_id=1, replica_groups=mesh['layer'=2,'prow'=4,'pcol'=32] {'pcol'}, dimensions={0} | all-to-all | bytes 262144 | tf_op jit(solution)/shard_map/all_to_all | solution.py:40
  220.9 4.9 %middle_backward.1 = bf16[32,2,16,128]{3,2,1,0:T(8,128)(2,1)} custom-call(s32[1]{0:T(128)} %bitcast.x_ref, s32[136]{0:T(256)} %maximum_convert_fusion.lists.table, bf16[32,16,128]{2,1,0:T(8,128)(2,1)} %all_to_all.75.root, bf16[32,16,128]{2,1,0:T(8,128)(2,1)} %all_to_all.77.top, f32[2,16,128]{2,1,0:T(8,128)} %get-tuple-element.48.fwd, ...), custom_call_target="tpu_custom_call" | custom-call | tf_op jit(solution)/shard_map/middle_backward/pallas_call | solution.py:386
  225.7 15.5 %all_to_all.78 = bf16[32,2,16,128]{3,2,1,0:T(8,128)(2,1)S(1)} all-to-all(bf16[32,2,16,128]{3,2,1,0:T(8,128)(2,1)} %middle_backward.1), channel_id=1, replica_groups=mesh['layer'=2,'prow'=4,'pcol'=32] {'pcol'}, dimensions={0} | all-to-all | bytes 524288 | tf_op jit(solution)/shard_map/all_to_all | solution.py:40
  242.0 4.5 %all-to-all-start.11 = ((bf16[32,2,16,128]{3,2,1,0:T(8,128)(2,1)}), bf16[32,2,16,128]{3,2,1,0:T(8,128)(2,1)S(1)}, u32[]{:S(2)}, u32[]{:S(2)}) async-start(bf16[32,2,16,128]{3,2,1,0:T(8,128)(2,1)} %broadcast_in_dim.62), calls=%async_computation.11 | async-start | bytes 524288 | tf_op jit(solution)/shard_map/all_to_all | solution.py:40
  246.5 4.6 %leaf_down.1.fwd = f32[4,16,128]{2,1,0:T(8,128)} custom-call(s32[1]{0:T(128)} %bitcast.x_ref, s32[136]{0:T(256)} %maximum_convert_fusion.lists.table, bf16[32,16,128]{2,1,0:T(8,128)(2,1)} %all_to_all.75.root, bf16[32,16,128]{2,1,0:T(8,128)(2,1)} %all_to_all.77.top, f32[4,16,128]{2,1,0:T(8,128)} %get-tuple-element.49.fwd, ...), custom_call_target="tpu_custom_call" | custom-call | tf_op jit(solution)/shard_map/leaf_down/pallas_call | solution.py:405
  251.1 6.4 %all-to-all-done.11.middle = bf16[32,2,16,128]{3,2,1,0:T(8,128)(2,1)S(1)} async-done(((bf16[32,2,16,128]{3,2,1,0:T(8,128)(2,1)}), bf16[32,2,16,128]{3,2,1,0:T(8,128)(2,1)S(1)}, u32[]{:S(2)}, u32[]{:S(2)}) %all-to-all-start.11) | async-done | bytes 262176 | tf_op jit(solution)/shard_map/all_to_all | solution.py:40
  258.2 6.3 %leaf_backward.1 = bf16[32,4,16,128]{3,2,1,0:T(8,128)(2,1)} custom-call(s32[1]{0:T(128)} %bitcast.x_ref, s32[136]{0:T(256)} %maximum_convert_fusion.lists.table, bf16[32,2,16,128]{3,2,1,0:T(8,128)(2,1)} %copy-done.1, f32[4,16,128]{2,1,0:T(8,128)} %leaf_down.1.fwd, bf16[4,4,20,128,128]{4,3,2,1,0:T(8,128)(2,1)} %bitcast.40), custom_call_target="tpu_custom_call" | custom-call | tf_op jit(solution)/shard_map/leaf_backward/pallas_call | solution.py:431
  264.5 4.5 %all-to-all-start.12 = ((bf16[32,4,16,128]{3,2,1,0:T(8,128)(2,1)}), bf16[32,4,16,128]{3,2,1,0:T(8,128)(2,1)S(1)}, u32[]{:S(2)}, u32[]{:S(2)}) async-start(bf16[32,4,16,128]{3,2,1,0:T(8,128)(2,1)} %leaf_backward.1), calls=%async_computation.12 | async-start | bytes 1048576 | tf_op jit(solution)/shard_map/all_to_all | solution.py:40
  271.4 3.5 %collective-permute-start.14 = (bf16[8,4,16,128]{3,2,1,0:T(8,128)(2,1)S(1)}, bf16[8,4,16,128]{3,2,1,0:T(8,128)(2,1)S(1)}, u32[]{:S(2)}, u32[]{:S(2)}) collective-permute-start(bf16[8,4,16,128]{3,2,1,0:T(8,128)(2,1)S(1)} %get-tuple-element.53), channel_id=1, source_target_pairs={{0,64},{32,96},{64,0},{96,32},{1,65},{33,97},{65,1},{97,33},{2,66}... | collective-permute-start | bytes 393224 | tf_op jit(solution)/shard_map/ppermute | solution.py:28
  274.9 7.6 %all-to-all-done.12 = bf16[32,4,16,128]{3,2,1,0:T(8,128)(2,1)S(1)} async-done(((bf16[32,4,16,128]{3,2,1,0:T(8,128)(2,1)}), bf16[32,4,16,128]{3,2,1,0:T(8,128)(2,1)S(1)}, u32[]{:S(2)}, u32[]{:S(2)}) %all-to-all-start.12) | async-done | bytes 524320 | tf_op jit(solution)/shard_map/all_to_all | solution.py:40
  286.8 3.5 %collective-permute-done.17 = bf16[16,128]{1,0:T(8,128)(2,1)S(1)} collective-permute-done((bf16[16,128]{1,0:T(8,128)(2,1)S(1)}, bf16[16,128]{1,0:T(8,128)(2,1)S(1)}, u32[]{:S(2)}, u32[]{:S(2)}) %collective-permute-start.17) | collective-permute-done | bytes 4128 | tf_op jit(solution)/shard_map/ppermute | solution.py:28
  291.9 18.2 %all_to_all.79.leaves = bf16[32,4,16,128]{3,2,1,0:T(8,128)(2,1)} all-to-all(bf16[32,4,16,128]{3,2,1,0:T(8,128)(2,1)S(1)} %broadcast_in_dim.63), channel_id=1, replica_groups=mesh['layer'=2,'prow'=4,'pcol'=32] {'pcol'}, dimensions={0} | all-to-all | bytes 1048576 | tf_op jit(solution)/shard_map/all_to_all | solution.py:40
  310.1 2.8 finish.1
  (120 shorter events, 45.8 us)
Async XLA Ops:
  7.2 80.6 %all-gather.7.cloned.1.call-start = ((), (), s32[]{:S(2)}) async-start(), calls=%async_computation.14 | async-start | bytes 5242880 | tf_op jit(solution)/shard_map/all_gather | solution.py:474
  15.1 11.3 %copy-start.19 = (f32[5,16,128]{2,1,0:T(8,128)S(1)}, f32[5,16,128]{2,1,0:T(8,128)}, u32[]{:S(2)}) copy-start(f32[5,16,128]{2,1,0:T(8,128)} %get-tuple-element.31) | copy-start | bytes 122884
  15.1 100.2 %all-gather.9.cloned.1.call-start = ((), (), s32[]{:S(2)}) async-start(), calls=%async_computation.15 | async-start | bytes 3276800 | tf_op jit(solution)/shard_map/all_gather | solution.py:474
  15.9 230.7 %all-gather.11.cloned.1.call-start = ((), (), s32[]{:S(2)}) async-start(), calls=%async_computation.16 | async-start | bytes 13107200 | tf_op jit(solution)/shard_map/all_gather | solution.py:474
  16.6 15.0 %collective-permute-start = (bf16[4,64,128]{2,1,0:T(8,128)(2,1)S(1)}, bf16[4,64,128]{2,1,0:T(8,128)(2,1)S(1)}, u32[]{:S(2)}, u32[]{:S(2)}) collective-permute-start(bf16[4,64,128]{2,1,0:T(8,128)(2,1)S(1)} %copy-done.11), channel_id=1, source_target_pairs={{0,32},{32,64},{64,96},{96,0},{1,33},{33,65},{65,97},{97,1},{2,34}... | collective-permute-start | bytes 196616 | tf_op jit(solution)/shard_map/ppermute | solution.py:28
  18.2 13.4 %collective-permute-start.1 = (bf16[4,64,128]{2,1,0:T(8,128)(2,1)S(1)}, bf16[4,64,128]{2,1,0:T(8,128)(2,1)S(1)}, u32[]{:S(2)}, u32[]{:S(2)}) collective-permute-start(bf16[4,64,128]{2,1,0:T(8,128)(2,1)S(1)} %copy-done.11), channel_id=1, source_target_pairs={{0,64},{32,96},{64,0},{96,32},{1,65},{33,97},{65,1},{97,33},{2,66}... | collective-permute-start | bytes 196616 | tf_op jit(solution)/shard_map/ppermute | solution.py:28
  20.9 10.7 %collective-permute-start.2 = (bf16[4,64,128]{2,1,0:T(8,128)(2,1)S(1)}, bf16[4,64,128]{2,1,0:T(8,128)(2,1)S(1)}, u32[]{:S(2)}, u32[]{:S(2)}) collective-permute-start(bf16[4,64,128]{2,1,0:T(8,128)(2,1)S(1)} %copy-done.11), channel_id=1, source_target_pairs={{0,96},{32,0},{64,32},{96,64},{1,97},{33,1},{65,33},{97,65},{2,98}... | collective-permute-start | bytes 196616 | tf_op jit(solution)/shard_map/ppermute | solution.py:28
  22.3 4.0 %collective-permute-start.3 = (f32[5,16,128]{2,1,0:T(8,128)S(1)}, f32[5,16,128]{2,1,0:T(8,128)S(1)}, u32[]{:S(2)}, u32[]{:S(2)}) collective-permute-start(f32[5,16,128]{2,1,0:T(8,128)S(1)} %copy-done.21), channel_id=1, source_target_pairs={{0,96},{32,0},{64,32},{96,64},{1,97},{33,1},{65,33},{97,65},{2,98}... | collective-permute-start | bytes 122888 | tf_op jit(solution)/shard_map/ppermute | solution.py:28
  22.4 5.6 %collective-permute-start.4 = (f32[5,16,128]{2,1,0:T(8,128)S(1)}, f32[5,16,128]{2,1,0:T(8,128)S(1)}, u32[]{:S(2)}, u32[]{:S(2)}) collective-permute-start(f32[5,16,128]{2,1,0:T(8,128)S(1)} %copy-done.20), channel_id=1, source_target_pairs={{0,64},{32,96},{64,0},{96,32},{1,65},{33,97},{65,1},{97,33},{2,66}... | collective-permute-start | bytes 122888 | tf_op jit(solution)/shard_map/ppermute | solution.py:28
  26.4 5.2 %collective-permute-start.5 = (f32[5,16,128]{2,1,0:T(8,128)S(1)}, f32[5,16,128]{2,1,0:T(8,128)S(1)}, u32[]{:S(2)}, u32[]{:S(2)}) collective-permute-start(f32[5,16,128]{2,1,0:T(8,128)S(1)} %copy-done.19), channel_id=1, source_target_pairs={{0,32},{32,64},{64,96},{96,0},{1,33},{33,65},{65,97},{97,1},{2,34}... | collective-permute-start | bytes 122888 | tf_op jit(solution)/shard_map/ppermute | solution.py:28
  36.6 7.4 %collective-permute-start.6 = (bf16[4,16,512]{2,1,0:T(8,128)(2,1)}, bf16[4,16,512]{2,1,0:T(8,128)(2,1)S(1)}, u32[]{:S(2)}, u32[]{:S(2)}) collective-permute-start(bf16[4,16,512]{2,1,0:T(8,128)(2,1)} %get-tuple-element.35), channel_id=1, source_target_pairs={{0,32},{32,64},{64,96},{96,0},{1,33},{33,65},{65,97},{97,1},{2,34}... | collective-permute-start | bytes 196616 | tf_op jit(solution)/shard_map/ppermute | solution.py:28
  36.7 8.6 %collective-permute-start.7 = (bf16[4,16,512]{2,1,0:T(8,128)(2,1)}, bf16[4,16,512]{2,1,0:T(8,128)(2,1)S(1)}, u32[]{:S(2)}, u32[]{:S(2)}) collective-permute-start(bf16[4,16,512]{2,1,0:T(8,128)(2,1)} %get-tuple-element.36), channel_id=1, source_target_pairs={{0,64},{32,96},{64,0},{96,32},{1,65},{33,97},{65,1},{97,33},{2,66}... | collective-permute-start | bytes 196616 | tf_op jit(solution)/shard_map/ppermute | solution.py:28
  39.3 7.4 %collective-permute-start.8 = (bf16[4,16,512]{2,1,0:T(8,128)(2,1)}, bf16[4,16,512]{2,1,0:T(8,128)(2,1)S(1)}, u32[]{:S(2)}, u32[]{:S(2)}) collective-permute-start(bf16[4,16,512]{2,1,0:T(8,128)(2,1)} %get-tuple-element.37), channel_id=1, source_target_pairs={{0,96},{32,0},{64,32},{96,64},{1,97},{33,1},{65,33},{97,65},{2,98}... | collective-permute-start | bytes 196616 | tf_op jit(solution)/shard_map/ppermute | solution.py:28
  72.4 15.4 %all-to-all-start.1 = ((bf16[32,2,16,128]{3,2,1,0:T(8,128)(2,1)}), bf16[32,2,16,128]{3,2,1,0:T(8,128)(2,1)S(1)}, u32[]{:S(2)}, u32[]{:S(2)}) async-start(bf16[32,2,16,128]{3,2,1,0:T(8,128)(2,1)} %broadcast_in_dim.23), calls=%async_computation.1 | async-start | bytes 524288 | tf_op jit(solution)/shard_map/all_to_all | solution.py:40
  76.8 7.9 %collective-permute-start.9 = (bf16[8,16,512]{2,1,0:T(8,128)(2,1)}, bf16[8,16,512]{2,1,0:T(8,128)(2,1)S(1)}, u32[]{:S(2)}, u32[]{:S(2)}) collective-permute-start(bf16[8,16,512]{2,1,0:T(8,128)(2,1)} %get-tuple-element.40), channel_id=1, source_target_pairs={{0,32},{32,64},{64,96},{96,0},{1,33},{33,65},{65,97},{97,1},{2,34}... | collective-permute-start | bytes 393224 | tf_op jit(solution)/shard_map/ppermute | solution.py:28
  76.9 7.8 %collective-permute-start.10 = (bf16[8,16,512]{2,1,0:T(8,128)(2,1)}, bf16[8,16,512]{2,1,0:T(8,128)(2,1)S(1)}, u32[]{:S(2)}, u32[]{:S(2)}) collective-permute-start(bf16[8,16,512]{2,1,0:T(8,128)(2,1)} %get-tuple-element.41), channel_id=1, source_target_pairs={{0,64},{32,96},{64,0},{96,32},{1,65},{33,97},{65,1},{97,33},{2,66}... | collective-permute-start | bytes 393224 | tf_op jit(solution)/shard_map/ppermute | solution.py:28
  79.5 6.0 %collective-permute-start.11 = (bf16[8,16,512]{2,1,0:T(8,128)(2,1)}, bf16[8,16,512]{2,1,0:T(8,128)(2,1)S(1)}, u32[]{:S(2)}, u32[]{:S(2)}) collective-permute-start(bf16[8,16,512]{2,1,0:T(8,128)(2,1)} %get-tuple-element.42), channel_id=1, source_target_pairs={{0,96},{32,0},{64,32},{96,64},{1,97},{33,1},{65,33},{97,65},{2,98}... | collective-permute-start | bytes 393224 | tf_op jit(solution)/shard_map/ppermute | solution.py:28
  110.7 14.4 %all-to-all-start.3 = ((bf16[32,16,128]{2,1,0:T(8,128)(2,1)}), bf16[32,16,128]{2,1,0:T(8,128)(2,1)S(1)}, u32[]{:S(2)}, u32[]{:S(2)}) async-start(bf16[32,16,128]{2,1,0:T(8,128)(2,1)} %broadcast_in_dim.25), calls=%async_computation.3 | async-start | bytes 262144 | tf_op jit(solution)/shard_map/all_to_all | solution.py:40
  142.8 1.3 collective-permute-start.12
  242.0 15.5 %all-to-all-start.11 = ((bf16[32,2,16,128]{3,2,1,0:T(8,128)(2,1)}), bf16[32,2,16,128]{3,2,1,0:T(8,128)(2,1)S(1)}, u32[]{:S(2)}, u32[]{:S(2)}) async-start(bf16[32,2,16,128]{3,2,1,0:T(8,128)(2,1)} %broadcast_in_dim.62), calls=%async_computation.11 | async-start | bytes 524288 | tf_op jit(solution)/shard_map/all_to_all | solution.py:40
  251.1 17.9 %copy-start = (bf16[32,16,128]{2,1,0:T(8,128)(2,1)S(1)}, bf16[32,16,128]{2,1,0:T(8,128)(2,1)}, u32[]{:S(2)}) copy-start(bf16[32,16,128]{2,1,0:T(8,128)(2,1)} %all_to_all.75.root) | copy-start | bytes 393220
  251.1 17.9 %copy-start.2 = (bf16[32,16,128]{2,1,0:T(8,128)(2,1)S(1)}, bf16[32,16,128]{2,1,0:T(8,128)(2,1)}, u32[]{:S(2)}) copy-start(bf16[32,16,128]{2,1,0:T(8,128)(2,1)} %all_to_all.77.top) | copy-start | bytes 393220
  264.5 17.9 %all-to-all-start.12 = ((bf16[32,4,16,128]{3,2,1,0:T(8,128)(2,1)}), bf16[32,4,16,128]{3,2,1,0:T(8,128)(2,1)S(1)}, u32[]{:S(2)}, u32[]{:S(2)}) async-start(bf16[32,4,16,128]{3,2,1,0:T(8,128)(2,1)} %leaf_backward.1), calls=%async_computation.12 | async-start | bytes 1048576 | tf_op jit(solution)/shard_map/all_to_all | solution.py:40
  270.8 20.9 %collective-permute-start.13 = (bf16[8,4,16,128]{3,2,1,0:T(8,128)(2,1)S(1)}, bf16[8,4,16,128]{3,2,1,0:T(8,128)(2,1)S(1)}, u32[]{:S(2)}, u32[]{:S(2)}) collective-permute-start(bf16[8,4,16,128]{3,2,1,0:T(8,128)(2,1)S(1)} %get-tuple-element.54), channel_id=1, source_target_pairs={{0,32},{32,64},{64,96},{96,0},{1,33},{33,65},{65,97},{97,1},{2,34}... | collective-permute-start | bytes 393224 | tf_op jit(solution)/shard_map/ppermute | solution.py:28
  271.4 20.3 %collective-permute-start.14 = (bf16[8,4,16,128]{3,2,1,0:T(8,128)(2,1)S(1)}, bf16[8,4,16,128]{3,2,1,0:T(8,128)(2,1)S(1)}, u32[]{:S(2)}, u32[]{:S(2)}) collective-permute-start(bf16[8,4,16,128]{3,2,1,0:T(8,128)(2,1)S(1)} %get-tuple-element.53), channel_id=1, source_target_pairs={{0,64},{32,96},{64,0},{96,32},{1,65},{33,97},{65,1},{97,33},{2,66}... | collective-permute-start | bytes 393224 | tf_op jit(solution)/shard_map/ppermute | solution.py:28
  274.9 16.9 %collective-permute-start.15 = (bf16[8,4,16,128]{3,2,1,0:T(8,128)(2,1)S(1)}, bf16[8,4,16,128]{3,2,1,0:T(8,128)(2,1)S(1)}, u32[]{:S(2)}, u32[]{:S(2)}) collective-permute-start(bf16[8,4,16,128]{3,2,1,0:T(8,128)(2,1)S(1)} %get-tuple-element.52), channel_id=1, source_target_pairs={{0,96},{32,0},{64,32},{96,64},{1,97},{33,1},{65,33},{97,65},{2,98}... | collective-permute-start | bytes 393224 | tf_op jit(solution)/shard_map/ppermute | solution.py:28
  282.5 4.1 %collective-permute-start.18 = (bf16[16,128]{1,0:T(8,128)(2,1)S(1)}, bf16[16,128]{1,0:T(8,128)(2,1)S(1)}, u32[]{:S(2)}, u32[]{:S(2)}) collective-permute-start(bf16[16,128]{1,0:T(8,128)(2,1)S(1)} %get-tuple-element.57), channel_id=1, source_target_pairs={{0,96},{32,0},{64,32},{96,64},{1,97},{33,1},{65,33},{97,65},{2,98}... | collective-permute-start | bytes 12296 | tf_op jit(solution)/shard_map/ppermute | solution.py:28
  285.3 5.1 %collective-permute-start.17 = (bf16[16,128]{1,0:T(8,128)(2,1)S(1)}, bf16[16,128]{1,0:T(8,128)(2,1)S(1)}, u32[]{:S(2)}, u32[]{:S(2)}) collective-permute-start(bf16[16,128]{1,0:T(8,128)(2,1)S(1)} %get-tuple-element.58), channel_id=1, source_target_pairs={{0,64},{32,96},{64,0},{96,32},{1,65},{33,97},{65,1},{97,33},{2,66}... | collective-permute-start | bytes 12296 | tf_op jit(solution)/shard_map/ppermute | solution.py:28
  286.6 5.1 %collective-permute-start.16 = (bf16[16,128]{1,0:T(8,128)(2,1)S(1)}, bf16[16,128]{1,0:T(8,128)(2,1)S(1)}, u32[]{:S(2)}, u32[]{:S(2)}) collective-permute-start(bf16[16,128]{1,0:T(8,128)(2,1)S(1)} %get-tuple-element.59), channel_id=1, source_target_pairs={{0,32},{32,64},{64,96},{96,0},{1,33},{33,65},{65,97},{97,1},{2,34}... | collective-permute-start | bytes 12296 | tf_op jit(solution)/shard_map/ppermute | solution.py:28
  291.7 18.4 %copy-start.8 = (bf16[8,4,16,128]{3,2,1,0:T(8,128)(2,1)}, bf16[8,4,16,128]{3,2,1,0:T(8,128)(2,1)S(1)}, u32[]{:S(2)}) copy-start(bf16[8,4,16,128]{3,2,1,0:T(8,128)(2,1)S(1)} %collective-permute-done.13.e1) | copy-start | bytes 393220
  291.7 18.3 %copy-start.9 = (bf16[8,4,16,128]{3,2,1,0:T(8,128)(2,1)}, bf16[8,4,16,128]{3,2,1,0:T(8,128)(2,1)S(1)}, u32[]{:S(2)}) copy-start(bf16[8,4,16,128]{3,2,1,0:T(8,128)(2,1)S(1)} %collective-permute-done.14.e2) | copy-start | bytes 393220
  291.7 18.3 %copy-start.10 = (bf16[8,4,16,128]{3,2,1,0:T(8,128)(2,1)}, bf16[8,4,16,128]{3,2,1,0:T(8,128)(2,1)S(1)}, u32[]{:S(2)}) copy-start(bf16[8,4,16,128]{3,2,1,0:T(8,128)(2,1)S(1)} %collective-permute-done.15.e3) | copy-start | bytes 393220
  (16 other events, 43.3 us)
Sparse Core Ops, SparseCore 0:
  15.2 56.2 all-gather.6
  73.3 38.0 all-gather.8
  113.2 103.5 all-gather.10

commit v4 on v3

--- a/solution.py
+++ b/solution.py
@@ -10,7 +10,8 @@
 RX = 16
 BF = jnp.bfloat16
 F32 = jnp.float32
-LIMIT = 56 * 1024 * 1024
+LIMIT = 14 * 1024 * 1024
+LARGE = 56 * 1024 * 1024
 
 SMEM = pl.BlockSpec(memory_space=pltpu.SMEM)
 VMEM = pl.BlockSpec(memory_space=pltpu.VMEM)
@@ -20,8 +21,8 @@
     return pl.BlockSpec(shape, lambda n: (0,) * len(shape))
 
 
-def params():
-    return pltpu.CompilerParams(vmem_limit_bytes=LIMIT)
+def params(limit=LIMIT):
+    return pltpu.CompilerParams(vmem_limit_bytes=limit)
 
 
 def shift(value, distance):
@@ -65,15 +66,20 @@
     return lax.rem(x + (NX - distance), NX)
 
 
-def start_kernel(place, right_sub, right_root, inverse, inverse_root, factor, lists, own, *rest):
-    pieces, (middle, top, leaf, rights, inverses, sems) = rest[0:4], rest[4:]
-    row, column = place[0], place[1]
+SENT = 25
+
+
+def start_kernel(place, right_sub, right_root, inverse, inverse_root, factor, lists, sent, middle, top, rights, inverses, pieces, sems):
+    column = place[0]
 
     def copy(source_ref, target_ref, index):
         pltpu.make_async_copy(source_ref, target_ref, sems.at[index]).start()
 
     copy(right_sub.at[3:7], rights, 0)
     copy(inverse.at[3:7], inverses, 1)
+    columns = pl.ds(pl.multiple_of(128 * column, 128), 128)
+    copy(right_sub.at[0:3, :, columns], pieces.at[0:3], 4)
+    copy(right_root.at[:, columns], pieces.at[3], 4)
 
     def factor_copy(pair, target, first, index):
         for c in range(4):
@@ -83,78 +89,70 @@
         copy(inverse.at[1 + m], middle.at[m, 0:8], 2)
         for i in range(2):
             factor_copy(1 + 2 * m + i, middle.at[m], 8 + 4 * i, 2)
-    for d in range(NX):
-        rows = pl.ds(row_start(row, d), RX)
-        columns = pl.ds(pl.multiple_of(128 * column, 128), 128)
-        copy(right_sub.at[0:3, rows, columns], pieces[d].at[0:3], 5 + d)
-        copy(right_root.at[rows, columns], pieces[d].at[3], 5 + d)
-        copy(lists, pieces[d].at[4], 5 + d)
     copy(inverse_root, top.at[0:8], 3)
     copy(inverse.at[0], top.at[8:16], 3)
     factor_copy(0, top, 16, 3)
 
-    def leaf_copies(n, carry):
-        copy(inverse.at[3 + n], leaf.at[n, 0:8], 4)
-        for i in range(3):
-            factor_copy(5 + 3 * n + i, leaf.at[n], (12, 16, 8)[i], 4)
-        return carry
-
-    lax.fori_loop(0, 4, leaf_copies, 0)
+    names = lists[...].astype(F32).astype(BF)
+    pltpu.make_async_copy(pieces, pieces, sems.at[4]).wait()
+    for r in range(NX):
+        sent[r, 24] = jnp.zeros((RX, 128), BF)
+        sent[r, 24, 0:2, 0:17] = names
+        for t in range(4):
+            piece = pieces[t, RX * r : RX * (r + 1), :]
+            high = piece.astype(BF)
+            sent[r, 16 + t] = high
+            sent[r, 20 + t] = (piece - high.astype(F32)).astype(BF)
     pltpu.make_async_copy(rights, rights, sems.at[0]).wait()
     pltpu.make_async_copy(inverses, inverses, sems.at[1]).wait()
     for n in range(4):
-        own[n] = dot(rights[n].astype(BF), inverses[n].reshape(1024, 128)).astype(BF)
-    for target, index in ((middle, 2), (top, 3), (leaf, 4)):
-        pltpu.make_async_copy(target, target, sems.at[index]).wait()
-    for d in range(NX):
-        pltpu.make_async_copy(pieces[d], pieces[d], sems.at[5 + d]).wait()
+        own = dot(rights[n].astype(BF), inverses[n].reshape(1024, 128)).astype(BF)
+        for r in range(NX):
+            for g in range(NX):
+                sent[r, 4 * n + g] = own[RX * g : RX * (g + 1)]
+    pltpu.make_async_copy(middle, middle, sems.at[2]).wait()
+    pltpu.make_async_copy(top, top, sems.at[3]).wait()
 
 
 def start(place, right_sub, right_root, inverse, inverse_root, factor, lists):
     hbm = pl.BlockSpec(memory_space=pl.ANY)
-    result = pl.pallas_call(
+    return pl.pallas_call(
         start_kernel,
-        out_shape=[jax.ShapeDtypeStruct((4, 64, 128), BF)]
-        + [jax.ShapeDtypeStruct((5, RX, 128), F32)] * 4
-        + [
+        out_shape=[
+            jax.ShapeDtypeStruct((NX, SENT, RX, 128), BF),
             jax.ShapeDtypeStruct((2, 16, 128, 128), BF),
             jax.ShapeDtypeStruct((20, 128, 128), BF),
-            jax.ShapeDtypeStruct((4, 20, 128, 128), BF),
         ],
-        in_specs=[SMEM] + [hbm] * 6,
-        out_specs=[VMEM] * 8,
+        in_specs=[SMEM] + [hbm] * 5 + [VMEM],
+        out_specs=[VMEM] * 3,
         scratch_shapes=[
             pltpu.VMEM((4, 64, 1024), F32),
             pltpu.VMEM((4, 8, 128, 128), BF),
-            pltpu.SemaphoreType.DMA((9,)),
+            pltpu.VMEM((4, 64, 128), F32),
+            pltpu.SemaphoreType.DMA((5,)),
         ],
-        compiler_params=params(),
+        compiler_params=params(LARGE),
         name="start",
-    )(
-        place,
-        right_sub,
-        right_root,
-        inverse.reshape(7, 8, 128, 128),
-        inverse_root.reshape(8, 128, 128),
-        factor,
-        lists,
-    )
-    return result[0], result[1:5], result[5], result[6], result[7]
-
-
-def leaf_update_kernel(x_ref, own, r1, r2, r3, f0, f1, f2, fwd, *rest):
-    crit, other = rest[0:4], rest[4:8]
+    )(place, right_sub, right_root, inverse, inverse_root, factor, lists)
+
+
+def leaf_update_kernel(x_ref, got, inverse, f0, f1, f2, fwd, *rest):
+    crit, other, packed = rest[0:4], rest[4:8], rest[8]
     x, n = x_ref[0], pl.program_id(0)
 
     def total(d):
-        rows = pl.ds(row_start(x, d), RX)
-        parts = [part[n, rows, :].astype(F32) for part in (own, r1, r2, r3)]
+        tile = 4 * n + lax.rem(x + d, NX)
+        parts = [got[r, tile].astype(F32) for r in range(NX)]
         return (parts[0] + parts[1]) + (parts[2] + parts[3])
 
     solved = [total(d) for d in range(NX)]
     fwd[n] = solved[0]
     left = jnp.concatenate(solved, axis=0).astype(BF)
+    packed[0, 0:8] = inverse[0]
     for i, factor in enumerate((f0, f1, f2)):
+        first = (12, 16, 8)[i]
+        for c in range(4):
+            packed[0, first + c] = factor[0, :, 128 * c : 128 * (c + 1)]
         update = dot(left, factor[0]).astype(BF)
         for d in range(NX):
             piece = update[RX * d : RX * (d + 1)]
@@ -164,54 +162,61 @@
                 other[d][2 * n + i] = piece
 
 
-def leaf_update(x, own, received, factor):
-    part = whole(4, 64, 128)
+def leaf_update(x, got, inverse, factor):
     result = pl.pallas_call(
         leaf_update_kernel,
         grid=(4,),
         out_shape=[jax.ShapeDtypeStruct((4, RX, 128), F32)]
         + [jax.ShapeDtypeStruct((4, RX, 512), BF)] * 4
-        + [jax.ShapeDtypeStruct((8, RX, 512), BF)] * 4,
-        in_specs=[SMEM]
-        + [part] * 4
+        + [jax.ShapeDtypeStruct((8, RX, 512), BF)] * 4
+        + [jax.ShapeDtypeStruct((4, 20, 128, 128), BF)],
+        in_specs=[
+            SMEM,
+            whole(NX, SENT, RX, 128),
+            pl.BlockSpec((1, 8, 128, 128), lambda n: (3 + n, 0, 0, 0)),
+        ]
         + [pl.BlockSpec((1, 128, 512), lambda n, i=i: (5 + 3 * n + i, 0, 0)) for i in range(3)],
-        out_specs=[whole(4, RX, 128)] + [whole(4, RX, 512)] * 4 + [whole(8, RX, 512)] * 4,
-        compiler_params=params(),
+        out_specs=[whole(4, RX, 128)]
+        + [whole(4, RX, 512)] * 4
+        + [whole(8, RX, 512)] * 4
+        + [pl.BlockSpec((1, 20, 128, 128), lambda n: (n, 0, 0, 0))],
+        compiler_params=params(LARGE),
         name="leaf_update",
-    )(x, own, *received, factor, factor, factor)
-    return result[0], result[1:5], result[5:9]
-
-
-def listed(table, distance, pair, j):
-    return table[(distance * 17 + pair) * 2 + j]
-
-
-def add_update(acc, table, distance, pair, update, *lead):
+    )(x, got, inverse, factor, factor, factor)
+    return result[0], result[1:5], result[5:9], result[9]
+
+
+def listed(table, r, pair, j):
+    return table[r, j, pair]
+
+
+def add_update(acc, table, r, pair, update, *lead):
     for j in range(2):
-        block = listed(table, distance, pair, j)
+        block = listed(table, r, pair, j)
         for h in range(2):
             index = (2 * block + h, *lead)
             tile = update[:, 256 * j + 128 * h : 256 * j + 128 * (h + 1)]
             acc[index] = acc[index] + tile.astype(F32)
 
 
-def leaf_spread_kernel(lists, c0, c1, c2, c3, out, acc):
+def leaf_spread_kernel(x_ref, table, c0, c1, c2, c3, out, acc):
+    x = x_ref[0]
     acc[...] = jnp.zeros(acc.shape, F32)
     for d, crit in enumerate((c0, c1, c2, c3)):
         for n in range(4):
-            add_update(acc, lists, d, 5 + 3 * n + 2, crit[n], n // 2)
+            add_update(acc, table, source(x, d), 5 + 3 * n + 2, crit[n], n // 2)
     out[...] = acc[...].astype(BF)
 
 
-def leaf_spread(lists, crit):
+def leaf_spread(x, table, crit):
     return pl.pallas_call(
         leaf_spread_kernel,
         out_shape=jax.ShapeDtypeStruct((NP, 2, RX, 128), BF),
-        in_specs=[SMEM] + [pl.BlockSpec(memory_space=pltpu.VMEM)] * 4,
+        in_specs=[SMEM] * 2 + [VMEM] * 4,
         scratch_shapes=[pltpu.VMEM((NP, 2, RX, 128), F32)],
         compiler_params=params(),
         name="leaf_spread",
-    )(lists, *crit)
+    )(x, table, *crit)
 
 
 def inverse_share(tiles):
@@ -241,7 +246,7 @@
 def multiply_update(acc, x, table, pair, rounded, factor, *lead):
     for r in range(NX):
         update = dot(rounded, factor(r))
-        add_update(acc, table, source(x, r), pair, update, *lead)
+        add_update(acc, table, r, pair, update, *lead)
 
 
 def pick_product(x, table, pair, values, factor, *lead):
@@ -249,7 +254,7 @@
     for r in range(NX):
         tiles = []
         for j in range(2):
-            block = listed(table, source(x, r), pair, j)
+            block = listed(table, r, pair, j)
             tiles += [values[(2 * block, *lead)], values[(2 * block + 1, *lead)]]
         term = dot_t(jnp.concatenate(tiles, axis=1), factor(r))
         total = term if total is None else total + term
@@ -275,8 +280,9 @@
     acc_root[...] = jnp.zeros(acc_root.shape, F32)
     for d, other in enumerate((o0, o1, o2, o3)):
         for n in range(4):
-            add_update(acc_root, table, d, 5 + 3 * n, other[2 * n])
-            add_update(acc, table, d, 5 + 3 * n + 1, other[2 * n + 1])
+            r = source(x, d)
+            add_update(acc_root, table, r, 5 + 3 * n, other[2 * n])
+            add_update(acc, table, r, 5 + 3 * n + 1, other[2 * n + 1])
     for m in range(2):
         solved = solve_columns(values, middle_inverse(weights, m), m)
         fwd[m] = solved
@@ -387,7 +393,7 @@
         middle_backward_kernel,
         out_shape=jax.ShapeDtypeStruct((NP, 2, RX, 128), BF),
         in_specs=[SMEM] * 2 + [VMEM] * 4,
-        compiler_params=params(),
+        compiler_params=params(LARGE),
         name="middle_backward",
     )(x, table, root, top, fwd, weights)
 
@@ -409,7 +415,7 @@
         in_specs=[SMEM] * 2
         + [TILES, TILES, pl.BlockSpec((1, RX, 128), lambda n: (n, 0, 0)), factor_at(3), factor_at(4)],
         out_specs=pl.BlockSpec((1, RX, 128), lambda n: (n, 0, 0)),
-        compiler_params=params(),
+        compiler_params=params(LARGE),
         name="leaf_down",
     )(x, table, root, top, fwd, weights, weights)
 
@@ -439,7 +445,7 @@
             pl.BlockSpec((NX, 1, 12, 128, 128), lambda n: (0, n, 0, 0, 0)),
         ],
         out_specs=pl.BlockSpec((8, NX, RX, 128), lambda n: (n, 0, 0, 0)),
-        compiler_params=params(),
+        compiler_params=params(LARGE),
         name="leaf_backward",
     )(x, table, middle, fwd, weights)
 
@@ -478,33 +484,28 @@
     position = lax.axis_index("prow").astype(jnp.int32)
     column = lax.axis_index("pcol").astype(jnp.int32)
     x = position[None]
-    lists = jnp.pad(block_lists.astype(F32).reshape(1, 34), ((0, RX - 1), (0, 94)))
-    own, pieces, middle_weights, top_weights, leaf_weights = start(
-        jnp.stack([position, column % 8]),
+    inverse_sub = inverse_sub.reshape(7, 8, 128, 128)
+    sent, middle_weights, top_weights = start(
+        (column % 8)[None],
         right_sub,
         right_root,
         inverse_sub,
-        inverse_root,
+        inverse_root.reshape(8, 128, 128),
         factor_blocks,
-        lists,
+        block_lists.T,
     )
     middle_weights = gather_rows(middle_weights)
     top_weights = gather_rows(top_weights)
+
+    got = lax.all_to_all(sent, "prow", 0, 0, tiled=True)
+    fwd_leaf, crit, other, leaf_weights = leaf_update(x, got, inverse_sub, factor_blocks)
     leaf_weights = gather_rows(leaf_weights)
-
-    received = around(own)
-    pieces = [pieces[0]] + [shift(pieces[d], d) for d in range(1, NX)]
-    table = jnp.concatenate([piece[4, 0, :34] for piece in pieces]).astype(jnp.int32)
-    held = lax.rem(position + NX - column // 8, NX)
-    right = pieces[0][:4]
-    for d in range(1, NX):
-        right = jnp.where(held == d, pieces[d][:4], right)
-
-    fwd_leaf, crit, other = leaf_update(x, own, received[1:], factor_blocks)
     crit = [crit[0]] + [shift(crit[d], d) for d in range(1, NX)]
     other = [other[0]] + [shift(other[d], d) for d in range(1, NX)]
-    crit[0], right = lax.optimization_barrier((crit[0], right))
-    parts = leaf_spread(table, crit)
+    table = got[:, 24, 0:2, 0:17].astype(jnp.int32)
+    right = lax.dynamic_index_in_dim(got, column // 8, 0, keepdims=False)
+    right = right[16:20].astype(F32) + right[20:24].astype(F32)
+    parts = leaf_spread(x, table, crit)
 
     values = gather_columns(right[1:3] - reduce_columns(parts))
     fwd_middle, parts, acc_root = middle_forward(x, table, values, middle_weights, other)

time: 321 us -> 305 us (0.950)
  blocking collectives: 159 us -> 134 us
  waiting for transfers between devices: 51.9 us -> 64.4 us
  Pallas kernels: 42.4 us -> 32.5 us
  starting transfers between devices: 41.2 us -> 47.5 us
    all_to_all x10 -> x9, blocking collectives: 159 us -> 134 us  [exchange(): return lax.all_to_all(value, 'pcol', 0, 0, tiled=True)]
    all_to_all x4 -> x5, starting transfers between devices: 18 us -> 29.2 us  [exchange(): return lax.all_to_all(value, 'pcol', 0, 0, tiled=True)]
    all_to_all x4 -> x5, waiting for transfers between devices: 25.9 us -> 36.6 us  [exchange(): return lax.all_to_all(value, 'pcol', 0, 0, tiled=True)]
    ppermute x18 -> x12, starting transfers between devices: 23 us -> 13.9 us  [shift(): lax.ppermute(value, 'prow', [(i, (i + distance) % NX) for i in range(NX)])]
    all_to_all x0 -> x1, waiting for transfers between devices: none -> 8.25 us  [per_device(): got = lax.all_to_all(sent, 'prow', 0, 0, tiled=True)]
    ppermute x18 -> x12, waiting for transfers between devices: 23.4 us -> 17.2 us  [shift(): lax.ppermute(value, 'prow', [(i, (i + distance) % NX) for i in range(NX)])]
    all_to_all x0 -> x1, starting transfers between devices: none -> 4.3 us  [per_device(): got = lax.all_to_all(sent, 'prow', 0, 0, tiled=True)]
    unnamed x44 -> x36, local copies, waits for them, and re-layouts: 3.94 us -> 6.43 us
  transfers between devices with their start and end apart: 26 -> 22, of which waited for: 16 -> 16; matrix products, arithmetic and copies ran while one was open for 2% -> 2% of each run, Pallas kernels for 9% -> 7%
where the time goes in v4:
time: 305 us; the launch traced here: 304 us
  blocking collectives  134 us (44%)
  waiting for transfers between devices  64.4 us (21%)
  starting transfers between devices  47.5 us (16%)
  Pallas kernels  32.5 us (11%)
  between operations  14.1 us (5%)
  local copies, waits for them, and re-layouts  8.8 us (3%)
    all_to_all x9, blocking collectives, exchange(): return lax.all_to_all(value, 'pcol', 0, 0, tiled=True)  134 us
    all_to_all x5, waiting for transfers between devices, exchange(): return lax.all_to_all(value, 'pcol', 0, 0, tiled=True)  36.6 us
    all_to_all x5, starting transfers between devices, exchange(): return lax.all_to_all(value, 'pcol', 0, 0, tiled=True)  29.2 us
    ppermute x12, waiting for transfers between devices, shift(): lax.ppermute(value, 'prow', [(i, (i + distance) % NX) for i in range(NX)])  17.2 us
    ppermute x12, starting transfers between devices, shift(): lax.ppermute(value, 'prow', [(i, (i + distance) % NX) for i in range(NX)])  13.9 us
    all_to_all x1, waiting for transfers between devices, per_device(): got = lax.all_to_all(sent, 'prow', 0, 0, tiled=True)  8.25 us
    unnamed x36, local copies, waits for them, and re-layouts  6.43 us
    pallas_call x1, Pallas kernels, leaf_backward(): pl.pallas_call(leaf_backward_kernel, grid=(4,), out_shape=jax.ShapeDtypeS...  6.35 us
  transfers between devices with their start and end apart: 22, of which 16 were waited for; matrix products, arithmetic and copies ran while one was open for 2% of the time, Pallas kernels for 7%

profile of v4, /device:TPU:32, one launch (start us, length us, event | category | flops | bytes accessed | tf_op | source)
XLA Modules:
  0.0 304.0 jit_solution(7438563004428174587)
XLA Ops:
  7.2 4.1 %start.1 = (bf16[4,25,16,128]{3,2,1,0:T(8,128)(2,1)}, bf16[2,16,128,128]{3,2,1,0:T(8,128)(2,1)}, bf16[20,128,128]{2,1,0:T(8,128)(2,1)}) custom-call(s32[1]{0:T(128)} %bitcast.1.place, f32[7,64,1024]{2,1,0:T(8,128)} %right_sub.1, f32[64,1024]{1,0:T(8,128)} %right_root.1, bf16[7,8,128,128]{3,2,1,0:T(8,128)(2,1)} %bitcast.63, bf16[8,128,128]{2,1,0:T(8,128)(2,1)} %bitcast.66, ...), custom_call_target="tpu_custom_call" | custom-call | tf_op jit(solution)/shard_map/start/pallas_call | solution.py:119
  12.1 4.3 %all-to-all-start = ((bf16[4,25,16,128]{3,2,1,0:T(8,128)(2,1)}), bf16[4,25,16,128]{3,2,1,0:T(8,128)(2,1)S(1)}, u32[]{:S(2)}, u32[]{:S(2)}) async-start(bf16[4,25,16,128]{3,2,1,0:T(8,128)(2,1)} %get-tuple-element.21), calls=%async_computation | async-start | bytes 819200 | tf_op jit(solution)/shard_map/all_to_all | solution.py:500
  16.4 8.2 %all-to-all-done.got = bf16[4,25,16,128]{3,2,1,0:T(8,128)(2,1)S(1)} async-done(((bf16[4,25,16,128]{3,2,1,0:T(8,128)(2,1)}), bf16[4,25,16,128]{3,2,1,0:T(8,128)(2,1)S(1)}, u32[]{:S(2)}, u32[]{:S(2)}) %all-to-all-start) | async-done | bytes 409632 | tf_op jit(solution)/shard_map/all_to_all | solution.py:500
  25.4 4.9 %leaf_update.1 = (f32[4,16,128]{2,1,0:T(8,128)}, bf16[4,16,512]{2,1,0:T(8,128)(2,1)}, bf16[4,16,512]{2,1,0:T(8,128)(2,1)}, bf16[4,16,512]{2,1,0:T(8,128)(2,1)}, ...) custom-call(s32[1]{0:T(128)} %bitcast.x_ref, ...), custom_call_target="tpu_custom_call" | custom-call | tf_op jit(solution)/shard_map/leaf_update/pallas_call | solution.py:166
  35.2 3.4 %collective-permute-done.c1 = bf16[4,16,512]{2,1,0:T(8,128)(2,1)S(1)} collective-permute-done((bf16[4,16,512]{2,1,0:T(8,128)(2,1)S(1)}, bf16[4,16,512]{2,1,0:T(8,128)(2,1)S(1)}, u32[]{:S(2)}, u32[]{:S(2)}) %collective-permute-start) | collective-permute-done | bytes 65568 | tf_op jit(solution)/shard_map/ppermute | solution.py:29
  42.9 11.3 %all-to-all-start.1 = ((bf16[32,2,16,128]{3,2,1,0:T(8,128)(2,1)}), bf16[32,2,16,128]{3,2,1,0:T(8,128)(2,1)S(1)}, u32[]{:S(2)}, u32[]{:S(2)}) async-start(bf16[32,2,16,128]{3,2,1,0:T(8,128)(2,1)} %leaf_spread.1), calls=%async_computation.1 | async-start | bytes 524288 | tf_op jit(solution)/shard_map/all_to_all | solution.py:41
  55.0 10.2 %all-to-all-done.1 = bf16[32,2,16,128]{3,2,1,0:T(8,128)(2,1)S(1)} async-done(((bf16[32,2,16,128]{3,2,1,0:T(8,128)(2,1)}), bf16[32,2,16,128]{3,2,1,0:T(8,128)(2,1)S(1)}, u32[]{:S(2)}, u32[]{:S(2)}) %all-to-all-start.1) | async-done | bytes 262176 | tf_op jit(solution)/shard_map/all_to_all | solution.py:41
  66.0 4.5 %all-to-all-start.2 = ((bf16[32,2,16,128]{3,2,1,0:T(8,128)(2,1)}), bf16[32,2,16,128]{3,2,1,0:T(8,128)(2,1)S(1)}, u32[]{:S(2)}, u32[]{:S(2)}) async-start(bf16[32,2,16,128]{3,2,1,0:T(8,128)(2,1)} %broadcast_in_dim.26), calls=%async_computation.2 | async-start | bytes 524288 | tf_op jit(solution)/shard_map/all_to_all | solution.py:41
  74.0 4.2 %collective-permute-done.3.o1 = bf16[8,16,512]{2,1,0:T(8,128)(2,1)S(1)} collective-permute-done((bf16[8,16,512]{2,1,0:T(8,128)(2,1)S(1)}, bf16[8,16,512]{2,1,0:T(8,128)(2,1)S(1)}, u32[]{:S(2)}, u32[]{:S(2)}) %collective-permute-start.3) | collective-permute-done | bytes 131104 | tf_op jit(solution)/shard_map/ppermute | solution.py:29
  79.0 2.5 all-to-all-done.2.values
  81.5 2.4 copy-done.2
  85.5 16.5 %all_to_all.75 = bf16[32,16,128]{2,1,0:T(8,128)(2,1)S(1)} all-to-all(bf16[32,16,128]{2,1,0:T(8,128)(2,1)S(1)} %get-tuple-element.31), channel_id=1, replica_groups=mesh['layer'=2,'prow'=4,'pcol'=32] {'pcol'}, dimensions={0} | all-to-all | bytes 262144 | tf_op jit(solution)/shard_map/all_to_all | solution.py:41
  102.8 4.4 %all-to-all-start.4 = ((bf16[32,16,128]{2,1,0:T(8,128)(2,1)}), bf16[32,16,128]{2,1,0:T(8,128)(2,1)S(1)}, u32[]{:S(2)}, u32[]{:S(2)}) async-start(bf16[32,16,128]{2,1,0:T(8,128)(2,1)} %broadcast_in_dim.28), calls=%async_computation.4 | async-start | bytes 262144 | tf_op jit(solution)/shard_map/all_to_all | solution.py:41
  107.6 9.3 %all-to-all-done.4.values = bf16[32,16,128]{2,1,0:T(8,128)(2,1)S(1)} async-done(((bf16[32,16,128]{2,1,0:T(8,128)(2,1)}), bf16[32,16,128]{2,1,0:T(8,128)(2,1)S(1)}, u32[]{:S(2)}, u32[]{:S(2)}) %all-to-all-start.4) | async-done | bytes 131104 | tf_op jit(solution)/shard_map/all_to_all | solution.py:41
  119.7 13.9 %all_to_all.76 = bf16[32,16,128]{2,1,0:T(8,128)(2,1)S(1)} all-to-all(bf16[32,16,128]{2,1,0:T(8,128)(2,1)S(1)} %get-tuple-element.34), channel_id=1, replica_groups=mesh['layer'=2,'prow'=4,'pcol'=32] {'pcol'}, dimensions={0} | all-to-all | bytes 262144 | tf_op jit(solution)/shard_map/all_to_all | solution.py:41
  134.9 14.2 %all_to_all.77.values = bf16[32,16,128]{2,1,0:T(8,128)(2,1)S(1)} all-to-all(bf16[32,16,128]{2,1,0:T(8,128)(2,1)S(1)} %broadcast_in_dim.29), channel_id=1, replica_groups=mesh['layer'=2,'prow'=4,'pcol'=32] {'pcol'}, dimensions={0} | all-to-all | bytes 262144 | tf_op jit(solution)/shard_map/all_to_all | solution.py:41
  149.8 13.9 %all_to_all.78 = bf16[32,16,128]{2,1,0:T(8,128)(2,1)S(1)} all-to-all(bf16[32,16,128]{2,1,0:T(8,128)(2,1)S(1)} %root_solve.1), channel_id=1, replica_groups=mesh['layer'=2,'prow'=4,'pcol'=32] {'pcol'}, dimensions={0} | all-to-all | bytes 262144 | tf_op jit(solution)/shard_map/all_to_all | solution.py:41
  163.8 13.8 %all_to_all.79.root = bf16[32,16,128]{2,1,0:T(8,128)(2,1)S(1)} all-to-all(bf16[32,16,128]{2,1,0:T(8,128)(2,1)S(1)} %broadcast_in_dim.30), channel_id=1, replica_groups=mesh['layer'=2,'prow'=4,'pcol'=32] {'pcol'}, dimensions={0} | all-to-all | bytes 262144 | tf_op jit(solution)/shard_map/all_to_all | solution.py:41
  179.1 14.0 %all_to_all.80 = bf16[32,16,128]{2,1,0:T(8,128)(2,1)S(1)} all-to-all(bf16[32,16,128]{2,1,0:T(8,128)(2,1)S(1)} %top_backward.1), channel_id=1, replica_groups=mesh['layer'=2,'prow'=4,'pcol'=32] {'pcol'}, dimensions={0} | all-to-all | bytes 262144 | tf_op jit(solution)/shard_map/all_to_all | solution.py:41
  193.1 14.0 %all_to_all.81.top = bf16[32,16,128]{2,1,0:T(8,128)(2,1)} all-to-all(bf16[32,16,128]{2,1,0:T(8,128)(2,1)S(1)} %broadcast_in_dim.64), channel_id=1, replica_groups=mesh['layer'=2,'prow'=4,'pcol'=32] {'pcol'}, dimensions={0} | all-to-all | bytes 262144 | tf_op jit(solution)/shard_map/all_to_all | solution.py:41
  207.1 4.9 %middle_backward.1 = bf16[32,2,16,128]{3,2,1,0:T(8,128)(2,1)} custom-call(s32[1]{0:T(128)} %bitcast.x_ref, s32[4,2,17]{2,1,0:T(2,128)} %copy-done.5, bf16[32,16,128]{2,1,0:T(8,128)(2,1)} %copy-done.3, bf16[32,16,128]{2,1,0:T(8,128)(2,1)} %all_to_all.81.top, f32[2,16,128]{2,1,0:T(8,128)} %copy-done.8, bf16[4,2,16,128,128]{4,3,2,1,0:T(8,128)(2,1)} %bitcast.57), custom_call_target="tpu_custom_call" | custom-call | tf_op jit(solution)/shard_map/middle_backward/pallas_call | solution.py:392
  212.0 15.4 %all_to_all.82 = bf16[32,2,16,128]{3,2,1,0:T(8,128)(2,1)S(1)} all-to-all(bf16[32,2,16,128]{3,2,1,0:T(8,128)(2,1)} %middle_backward.1), channel_id=1, replica_groups=mesh['layer'=2,'prow'=4,'pcol'=32] {'pcol'}, dimensions={0} | all-to-all | bytes 524288 | tf_op jit(solution)/shard_map/all_to_all | solution.py:41
  228.2 4.5 %all-to-all-start.12 = ((bf16[32,2,16,128]{3,2,1,0:T(8,128)(2,1)}), bf16[32,2,16,128]{3,2,1,0:T(8,128)(2,1)S(1)}, u32[]{:S(2)}, u32[]{:S(2)}) async-start(bf16[32,2,16,128]{3,2,1,0:T(8,128)(2,1)} %broadcast_in_dim.66), calls=%async_computation.12 | async-start | bytes 524288 | tf_op jit(solution)/shard_map/all_to_all | solution.py:41
  232.8 4.6 %leaf_down.1.fwd = f32[4,16,128]{2,1,0:T(8,128)} custom-call(s32[1]{0:T(128)} %bitcast.x_ref, s32[4,2,17]{2,1,0:T(2,128)} %copy-done.5, bf16[32,16,128]{2,1,0:T(8,128)(2,1)} %copy-done.3, bf16[32,16,128]{2,1,0:T(8,128)(2,1)} %all_to_all.81.top, f32[4,16,128]{2,1,0:T(8,128)} %get-tuple-element.37.fwd, bf16[4,4,20,128,128]{4,3,2,1,0:T(8,128)(2,1)} %bitcast.60, ...), custom_call_target="tpu_custom_call" | custom-call | tf_op jit(solution)/shard_map/leaf_down/pallas_call | solution.py:411
  237.4 6.4 %all-to-all-done.12.middle = bf16[32,2,16,128]{3,2,1,0:T(8,128)(2,1)S(1)} async-done(((bf16[32,2,16,128]{3,2,1,0:T(8,128)(2,1)}), bf16[32,2,16,128]{3,2,1,0:T(8,128)(2,1)S(1)}, u32[]{:S(2)}, u32[]{:S(2)}) %all-to-all-start.12) | async-done | bytes 262176 | tf_op jit(solution)/shard_map/all_to_all | solution.py:41
  244.4 6.3 %leaf_backward.1 = bf16[32,4,16,128]{3,2,1,0:T(8,128)(2,1)} custom-call(s32[1]{0:T(128)} %bitcast.x_ref, s32[4,2,17]{2,1,0:T(2,128)} %copy-done.5, bf16[32,2,16,128]{3,2,1,0:T(8,128)(2,1)} %copy-done.9, f32[4,16,128]{2,1,0:T(8,128)} %leaf_down.1.fwd, bf16[4,4,20,128,128]{4,3,2,1,0:T(8,128)(2,1)} %bitcast.62), custom_call_target="tpu_custom_call" | custom-call | tf_op jit(solution)/shard_map/leaf_backward/pallas_call | solution.py:437
  250.8 4.5 %all-to-all-start.13 = ((bf16[32,4,16,128]{3,2,1,0:T(8,128)(2,1)}), bf16[32,4,16,128]{3,2,1,0:T(8,128)(2,1)S(1)}, u32[]{:S(2)}, u32[]{:S(2)}) async-start(bf16[32,4,16,128]{3,2,1,0:T(8,128)(2,1)} %leaf_backward.1), calls=%async_computation.13 | async-start | bytes 1048576 | tf_op jit(solution)/shard_map/all_to_all | solution.py:41
  257.0 3.4 %collective-permute-start.8 = (bf16[8,4,16,128]{3,2,1,0:T(8,128)(2,1)S(1)}, bf16[8,4,16,128]{3,2,1,0:T(8,128)(2,1)S(1)}, u32[]{:S(2)}, u32[]{:S(2)}) collective-permute-start(bf16[8,4,16,128]{3,2,1,0:T(8,128)(2,1)S(1)} %get-tuple-element.41), channel_id=1, source_target_pairs={{0,64},{32,96},{64,0},{96,32},{1,65},{33,97},{65,1},{97,33},{2,66}... | collective-permute-start | bytes 393224 | tf_op jit(solution)/shard_map/ppermute | solution.py:29
  260.4 8.3 %all-to-all-done.13 = bf16[32,4,16,128]{3,2,1,0:T(8,128)(2,1)S(1)} async-done(((bf16[32,4,16,128]{3,2,1,0:T(8,128)(2,1)}), bf16[32,4,16,128]{3,2,1,0:T(8,128)(2,1)S(1)}, u32[]{:S(2)}, u32[]{:S(2)}) %all-to-all-start.13) | async-done | bytes 524320 | tf_op jit(solution)/shard_map/all_to_all | solution.py:41
  268.8 2.6 collective-permute-start.12
  273.0 3.4 %collective-permute-done.11 = bf16[16,128]{1,0:T(8,128)(2,1)S(1)} collective-permute-done((bf16[16,128]{1,0:T(8,128)(2,1)S(1)}, bf16[16,128]{1,0:T(8,128)(2,1)S(1)}, u32[]{:S(2)}, u32[]{:S(2)}) %collective-permute-start.11) | collective-permute-done | bytes 4128 | tf_op jit(solution)/shard_map/ppermute | solution.py:29
  277.9 18.1 %all_to_all.83.leaves = bf16[32,4,16,128]{3,2,1,0:T(8,128)(2,1)S(1)} all-to-all(bf16[32,4,16,128]{3,2,1,0:T(8,128)(2,1)S(1)} %broadcast_in_dim.67), channel_id=1, replica_groups=mesh['layer'=2,'prow'=4,'pcol'=32] {'pcol'}, dimensions={0} | all-to-all | bytes 1048576 | tf_op jit(solution)/shard_map/all_to_all | solution.py:41
  (94 shorter events, 33.5 us)
Async XLA Ops:
  7.2 74.4 %all-gather.7.cloned.1.call-start = ((), (), s32[]{:S(2)}) async-start(), calls=%async_computation.15 | async-start | bytes 5242880 | tf_op jit(solution)/shard_map/all_gather | solution.py:480
  11.3 96.3 %all-gather.9.cloned.1.call-start = ((), (), s32[]{:S(2)}) async-start(), calls=%async_computation.16 | async-start | bytes 3276800 | tf_op jit(solution)/shard_map/all_gather | solution.py:480
  12.1 12.6 %all-to-all-start = ((bf16[4,25,16,128]{3,2,1,0:T(8,128)(2,1)}), bf16[4,25,16,128]{3,2,1,0:T(8,128)(2,1)S(1)}, u32[]{:S(2)}, u32[]{:S(2)}) async-start(bf16[4,25,16,128]{3,2,1,0:T(8,128)(2,1)} %get-tuple-element.21), calls=%async_computation | async-start | bytes 819200 | tf_op jit(solution)/shard_map/all_to_all | solution.py:500
  16.4 216.4 %all-gather.11.cloned.1.call-start = ((), (), s32[]{:S(2)}) async-start(), calls=%async_computation.17 | async-start | bytes 13107200 | tf_op jit(solution)/shard_map/all_gather | solution.py:480
  30.3 11.0 %copy-start.7 = (bf16[4,16,512]{2,1,0:T(8,128)(2,1)S(1)}, bf16[4,16,512]{2,1,0:T(8,128)(2,1)}, u32[]{:S(2)}) copy-start(bf16[4,16,512]{2,1,0:T(8,128)(2,1)} %get-tuple-element.22.c0) | copy-start | bytes 196612
  30.4 40.1 %copy-start.14 = (bf16[8,16,512]{2,1,0:T(8,128)(2,1)S(1)}, bf16[8,16,512]{2,1,0:T(8,128)(2,1)}, u32[]{:S(2)}) copy-start(bf16[8,16,512]{2,1,0:T(8,128)(2,1)} %get-tuple-element.28) | copy-start | bytes 393220
  30.4 40.2 %copy-start.13 = (bf16[8,16,512]{2,1,0:T(8,128)(2,1)S(1)}, bf16[8,16,512]{2,1,0:T(8,128)(2,1)}, u32[]{:S(2)}) copy-start(bf16[8,16,512]{2,1,0:T(8,128)(2,1)} %get-tuple-element.29) | copy-start | bytes 393220
  30.4 42.3 %copy-start.12 = (bf16[8,16,512]{2,1,0:T(8,128)(2,1)S(1)}, bf16[8,16,512]{2,1,0:T(8,128)(2,1)}, u32[]{:S(2)}) copy-start(bf16[8,16,512]{2,1,0:T(8,128)(2,1)} %get-tuple-element.30) | copy-start | bytes 393220
  30.4 51.1 %copy-start.6 = (bf16[8,16,512]{2,1,0:T(8,128)(2,1)S(1)}, bf16[8,16,512]{2,1,0:T(8,128)(2,1)}, u32[]{:S(2)}) copy-start(bf16[8,16,512]{2,1,0:T(8,128)(2,1)} %get-tuple-element.27.o0) | copy-start | bytes 393220
  31.2 7.4 %collective-permute-start = (bf16[4,16,512]{2,1,0:T(8,128)(2,1)S(1)}, bf16[4,16,512]{2,1,0:T(8,128)(2,1)S(1)}, u32[]{:S(2)}, u32[]{:S(2)}) collective-permute-start(bf16[4,16,512]{2,1,0:T(8,128)(2,1)S(1)} %copy-done.17), channel_id=1, source_target_pairs={{0,32},{32,64},{64,96},{96,0},{1,33},{33,65},{65,97},{97,1},{2,34}... | collective-permute-start | bytes 196616 | tf_op jit(solution)/shard_map/ppermute | solution.py:29
  31.7 8.2 %collective-permute-start.1 = (bf16[4,16,512]{2,1,0:T(8,128)(2,1)S(1)}, bf16[4,16,512]{2,1,0:T(8,128)(2,1)S(1)}, u32[]{:S(2)}, u32[]{:S(2)}) collective-permute-start(bf16[4,16,512]{2,1,0:T(8,128)(2,1)S(1)} %copy-done.16), channel_id=1, source_target_pairs={{0,64},{32,96},{64,0},{96,32},{1,65},{33,97},{65,1},{97,33},{2,66}... | collective-permute-start | bytes 196616 | tf_op jit(solution)/shard_map/ppermute | solution.py:29
  33.7 7.7 %collective-permute-start.2 = (bf16[4,16,512]{2,1,0:T(8,128)(2,1)S(1)}, bf16[4,16,512]{2,1,0:T(8,128)(2,1)S(1)}, u32[]{:S(2)}, u32[]{:S(2)}) collective-permute-start(bf16[4,16,512]{2,1,0:T(8,128)(2,1)S(1)} %copy-done.15), channel_id=1, source_target_pairs={{0,96},{32,0},{64,32},{96,64},{1,97},{33,1},{65,33},{97,65},{2,98}... | collective-permute-start | bytes 196616 | tf_op jit(solution)/shard_map/ppermute | solution.py:29
  35.2 142.4 %copy-start.5 = (s32[4,2,17]{2,1,0:T(2,128)}, s32[4,2,17]{2,1,0:T(2,128)S(1)}, u32[]{:S(2)}) copy-start(s32[4,2,17]{2,1,0:T(2,128)S(1)} %fusion.7.table) | copy-start | bytes 1636
  42.9 22.3 %all-to-all-start.1 = ((bf16[32,2,16,128]{3,2,1,0:T(8,128)(2,1)}), bf16[32,2,16,128]{3,2,1,0:T(8,128)(2,1)S(1)}, u32[]{:S(2)}, u32[]{:S(2)}) async-start(bf16[32,2,16,128]{3,2,1,0:T(8,128)(2,1)} %leaf_spread.1), calls=%async_computation.1 | async-start | bytes 524288 | tf_op jit(solution)/shard_map/all_to_all | solution.py:41
  66.0 15.5 %all-to-all-start.2 = ((bf16[32,2,16,128]{3,2,1,0:T(8,128)(2,1)}), bf16[32,2,16,128]{3,2,1,0:T(8,128)(2,1)S(1)}, u32[]{:S(2)}, u32[]{:S(2)}) async-start(bf16[32,2,16,128]{3,2,1,0:T(8,128)(2,1)} %broadcast_in_dim.26), calls=%async_computation.2 | async-start | bytes 524288 | tf_op jit(solution)/shard_map/all_to_all | solution.py:41
  70.5 7.7 %collective-permute-start.3 = (bf16[8,16,512]{2,1,0:T(8,128)(2,1)S(1)}, bf16[8,16,512]{2,1,0:T(8,128)(2,1)S(1)}, u32[]{:S(2)}, u32[]{:S(2)}) collective-permute-start(bf16[8,16,512]{2,1,0:T(8,128)(2,1)S(1)} %copy-done.14), channel_id=1, source_target_pairs={{0,32},{32,64},{64,96},{96,0},{1,33},{33,65},{65,97},{97,1},{2,34}... | collective-permute-start | bytes 393224 | tf_op jit(solution)/shard_map/ppermute | solution.py:29
  70.6 7.6 %collective-permute-start.4 = (bf16[8,16,512]{2,1,0:T(8,128)(2,1)S(1)}, bf16[8,16,512]{2,1,0:T(8,128)(2,1)S(1)}, u32[]{:S(2)}, u32[]{:S(2)}) collective-permute-start(bf16[8,16,512]{2,1,0:T(8,128)(2,1)S(1)} %copy-done.13), channel_id=1, source_target_pairs={{0,64},{32,96},{64,0},{96,32},{1,65},{33,97},{65,1},{97,33},{2,66}... | collective-permute-start | bytes 393224 | tf_op jit(solution)/shard_map/ppermute | solution.py:29
  72.7 6.4 %collective-permute-start.5 = (bf16[8,16,512]{2,1,0:T(8,128)(2,1)S(1)}, bf16[8,16,512]{2,1,0:T(8,128)(2,1)S(1)}, u32[]{:S(2)}, u32[]{:S(2)}) collective-permute-start(bf16[8,16,512]{2,1,0:T(8,128)(2,1)S(1)} %copy-done.12), channel_id=1, source_target_pairs={{0,96},{32,0},{64,32},{96,64},{1,97},{33,1},{65,33},{97,65},{2,98}... | collective-permute-start | bytes 393224 | tf_op jit(solution)/shard_map/ppermute | solution.py:29
  85.5 16.5 %copy-start.8 = (f32[2,16,128]{2,1,0:T(8,128)}, f32[2,16,128]{2,1,0:T(8,128)S(1)}, u32[]{:S(2)}) copy-start(f32[2,16,128]{2,1,0:T(8,128)S(1)} %get-tuple-element.36.fwd) | copy-start | bytes 49156
  102.8 14.2 %all-to-all-start.4 = ((bf16[32,16,128]{2,1,0:T(8,128)(2,1)}), bf16[32,16,128]{2,1,0:T(8,128)(2,1)S(1)}, u32[]{:S(2)}, u32[]{:S(2)}) async-start(bf16[32,16,128]{2,1,0:T(8,128)(2,1)} %broadcast_in_dim.28), calls=%async_computation.4 | async-start | bytes 262144 | tf_op jit(solution)/shard_map/all_to_all | solution.py:41
  118.7 30.5 %copy-start.1 = (bf16[80,128,128]{2,1,0:T(8,128)(2,1)S(1)}, bf16[80,128,128]{2,1,0:T(8,128)(2,1)}, u32[]{:S(2)}) copy-start(bf16[80,128,128]{2,1,0:T(8,128)(2,1)} %all-gather.9.cloned.1.call-done) | copy-start | bytes 7864324
  133.6 1.3 collective-permute-start.6
  228.2 15.5 %all-to-all-start.12 = ((bf16[32,2,16,128]{3,2,1,0:T(8,128)(2,1)}), bf16[32,2,16,128]{3,2,1,0:T(8,128)(2,1)S(1)}, u32[]{:S(2)}, u32[]{:S(2)}) async-start(bf16[32,2,16,128]{3,2,1,0:T(8,128)(2,1)} %broadcast_in_dim.66), calls=%async_computation.12 | async-start | bytes 524288 | tf_op jit(solution)/shard_map/all_to_all | solution.py:41
  237.4 17.9 %copy-start.4 = (bf16[32,16,128]{2,1,0:T(8,128)(2,1)S(1)}, bf16[32,16,128]{2,1,0:T(8,128)(2,1)}, u32[]{:S(2)}) copy-start(bf16[32,16,128]{2,1,0:T(8,128)(2,1)} %copy-done.3) | copy-start | bytes 393220
  237.4 17.9 %copy-start.10 = (bf16[32,16,128]{2,1,0:T(8,128)(2,1)S(1)}, bf16[32,16,128]{2,1,0:T(8,128)(2,1)}, u32[]{:S(2)}) copy-start(bf16[32,16,128]{2,1,0:T(8,128)(2,1)} %all_to_all.81.top) | copy-start | bytes 393220
  250.8 17.9 %all-to-all-start.13 = ((bf16[32,4,16,128]{3,2,1,0:T(8,128)(2,1)}), bf16[32,4,16,128]{3,2,1,0:T(8,128)(2,1)S(1)}, u32[]{:S(2)}, u32[]{:S(2)}) async-start(bf16[32,4,16,128]{3,2,1,0:T(8,128)(2,1)} %leaf_backward.1), calls=%async_computation.13 | async-start | bytes 1048576 | tf_op jit(solution)/shard_map/all_to_all | solution.py:41
  256.4 21.4 %collective-permute-start.7 = (bf16[8,4,16,128]{3,2,1,0:T(8,128)(2,1)S(1)}, bf16[8,4,16,128]{3,2,1,0:T(8,128)(2,1)S(1)}, u32[]{:S(2)}, u32[]{:S(2)}) collective-permute-start(bf16[8,4,16,128]{3,2,1,0:T(8,128)(2,1)S(1)} %get-tuple-element.42), channel_id=1, source_target_pairs={{0,32},{32,64},{64,96},{96,0},{1,33},{33,65},{65,97},{97,1},{2,34}... | collective-permute-start | bytes 393224 | tf_op jit(solution)/shard_map/ppermute | solution.py:29
  257.0 20.8 %collective-permute-start.8 = (bf16[8,4,16,128]{3,2,1,0:T(8,128)(2,1)S(1)}, bf16[8,4,16,128]{3,2,1,0:T(8,128)(2,1)S(1)}, u32[]{:S(2)}, u32[]{:S(2)}) collective-permute-start(bf16[8,4,16,128]{3,2,1,0:T(8,128)(2,1)S(1)} %get-tuple-element.41), channel_id=1, source_target_pairs={{0,64},{32,96},{64,0},{96,32},{1,65},{33,97},{65,1},{97,33},{2,66}... | collective-permute-start | bytes 393224 | tf_op jit(solution)/shard_map/ppermute | solution.py:29
  260.4 17.4 %collective-permute-start.9 = (bf16[8,4,16,128]{3,2,1,0:T(8,128)(2,1)S(1)}, bf16[8,4,16,128]{3,2,1,0:T(8,128)(2,1)S(1)}, u32[]{:S(2)}, u32[]{:S(2)}) collective-permute-start(bf16[8,4,16,128]{3,2,1,0:T(8,128)(2,1)S(1)} %get-tuple-element.40), channel_id=1, source_target_pairs={{0,96},{32,0},{64,32},{96,64},{1,97},{33,1},{65,33},{97,65},{2,98}... | collective-permute-start | bytes 393224 | tf_op jit(solution)/shard_map/ppermute | solution.py:29
  268.8 3.9 %collective-permute-start.12 = (bf16[16,128]{1,0:T(8,128)(2,1)S(1)}, bf16[16,128]{1,0:T(8,128)(2,1)S(1)}, u32[]{:S(2)}, u32[]{:S(2)}) collective-permute-start(bf16[16,128]{1,0:T(8,128)(2,1)S(1)} %get-tuple-element.45), channel_id=1, source_target_pairs={{0,96},{32,0},{64,32},{96,64},{1,97},{33,1},{65,33},{97,65},{2,98}... | collective-permute-start | bytes 12296 | tf_op jit(solution)/shard_map/ppermute | solution.py:29
  271.4 5.1 %collective-permute-start.11 = (bf16[16,128]{1,0:T(8,128)(2,1)S(1)}, bf16[16,128]{1,0:T(8,128)(2,1)S(1)}, u32[]{:S(2)}, u32[]{:S(2)}) collective-permute-start(bf16[16,128]{1,0:T(8,128)(2,1)S(1)} %get-tuple-element.46), channel_id=1, source_target_pairs={{0,64},{32,96},{64,0},{96,32},{1,65},{33,97},{65,1},{97,33},{2,66}... | collective-permute-start | bytes 12296 | tf_op jit(solution)/shard_map/ppermute | solution.py:29
  272.7 5.1 %collective-permute-start.10 = (bf16[16,128]{1,0:T(8,128)(2,1)S(1)}, bf16[16,128]{1,0:T(8,128)(2,1)S(1)}, u32[]{:S(2)}, u32[]{:S(2)}) collective-permute-start(bf16[16,128]{1,0:T(8,128)(2,1)S(1)} %get-tuple-element.47), channel_id=1, source_target_pairs={{0,32},{32,64},{64,96},{96,0},{1,33},{33,65},{65,97},{97,1},{2,34}... | collective-permute-start | bytes 12296 | tf_op jit(solution)/shard_map/ppermute | solution.py:29
  (8 other events, 12.7 us)
Sparse Core Ops, SparseCore 0:
  11.5 56.1 all-gather.6
  69.5 38.0 all-gather.8
  109.5 103.5 all-gather.10

commit v5 on v4

--- a/solution.py
+++ b/solution.py
@@ -15,6 +15,7 @@
 
 SMEM = pl.BlockSpec(memory_space=pltpu.SMEM)
 VMEM = pl.BlockSpec(memory_space=pltpu.VMEM)
+HBM = pl.BlockSpec(memory_space=pltpu.HBM)
 
 
 def whole(*shape):
@@ -219,6 +220,22 @@
     )(x, table, *crit)
 
 
+def fetch(weights, near, sems, nodes, tiles):
+    moves = [
+        [
+            pltpu.make_async_copy(
+                weights.at[r, n, 0:tiles], near.at[r, n], sems.at[NX * n + r]
+            )
+            for r in range(NX)
+        ]
+        for n in range(nodes)
+    ]
+    for node in moves:
+        for move in node:
+            move.start()
+    return moves
+
+
 def inverse_share(tiles):
     return tiles.reshape(1024, 128)
 
@@ -274,8 +291,9 @@
     return lambda r: factor_share(weights[r, m, 8 + 4 * i : 12 + 4 * i])
 
 
-def middle_forward_kernel(x_ref, table, values, weights, o0, o1, o2, o3, fwd, out, acc_root, acc):
+def middle_forward_kernel(x_ref, table, values, far, o0, o1, o2, o3, fwd, out, acc_root, acc, weights, sems):
     x = x_ref[0]
+    moves = fetch(far, weights, sems, 2, 16)
     acc[...] = jnp.zeros(acc.shape, F32)
     acc_root[...] = jnp.zeros(acc_root.shape, F32)
     for d, other in enumerate((o0, o1, o2, o3)):
@@ -284,6 +302,8 @@
             add_update(acc_root, table, r, 5 + 3 * n, other[2 * n])
             add_update(acc, table, r, 5 + 3 * n + 1, other[2 * n + 1])
     for m in range(2):
+        for move in moves[m]:
+            move.wait()
         solved = solve_columns(values, middle_inverse(weights, m), m)
         fwd[m] = solved
         rounded = solved.astype(BF)
@@ -300,9 +320,13 @@
             jax.ShapeDtypeStruct((NP, RX, 128), BF),
             jax.ShapeDtypeStruct((NP, RX, 128), F32),
         ],
-        in_specs=[SMEM] * 2 + [VMEM] * 6,
-        scratch_shapes=[pltpu.VMEM((NP, RX, 128), F32)],
-        compiler_params=params(),
+        in_specs=[SMEM] * 2 + [VMEM, HBM] + [VMEM] * 4,
+        scratch_shapes=[
+            pltpu.VMEM((NP, RX, 128), F32),
+            pltpu.VMEM((NX, 2, 16, 128, 128), BF),
+            pltpu.SemaphoreType.DMA((2 * NX,)),
+        ],
+        compiler_params=params(LARGE),
         name="middle_forward",
     )(x, table, values, weights, *other)
 
@@ -376,9 +400,12 @@
     )(x, table, root, fwd, weights, weights)
 
 
-def middle_backward_kernel(x_ref, table, root, top, fwd, weights, out):
+def middle_backward_kernel(x_ref, table, root, top, fwd, far, out, weights, sems):
     x = x_ref[0]
+    moves = fetch(far, weights, sems, 2, 16)
     for m in range(2):
+        for move in moves[m]:
+            move.wait()
         down = pick_product(x, table, 1 + 2 * m, root, middle_factor(weights, m, 0))
         down = down + pick_product(x, table, 2 + 2 * m, top, middle_factor(weights, m, 1))
 
@@ -392,7 +419,11 @@
     return pl.pallas_call(
         middle_backward_kernel,
         out_shape=jax.ShapeDtypeStruct((NP, 2, RX, 128), BF),
-        in_specs=[SMEM] * 2 + [VMEM] * 4,
+        in_specs=[SMEM] * 2 + [VMEM] * 3 + [HBM],
+        scratch_shapes=[
+            pltpu.VMEM((NX, 2, 16, 128, 128), BF),
+            pltpu.SemaphoreType.DMA((2 * NX,)),
+        ],
         compiler_params=params(LARGE),
         name="middle_backward",
     )(x, table, root, top, fwd, weights)
@@ -420,31 +451,32 @@
     )(x, table, root, top, fwd, weights, weights)
 
 
-def leaf_backward_kernel(x_ref, table, middle, fwd, weights, out):
-    x, n = x_ref[0], pl.program_id(0)
-    down = pick_product(
-        x, table, 7 + 3 * n, middle, lambda r: factor_share(weights[r, 0, 8:12]), n // 2
-    )
-
-    def store(r, k, tile):
-        out[k, lax.rem(r + NX - x, NX)] = tile
-
-    inverse = lambda r: inverse_share(weights[r, 0, 0:8])
-    solve_rows((fwd[0] - down).astype(BF), inverse, store)
+def leaf_backward_kernel(x_ref, table, middle, fwd, far, out, near, sems):
+    x = x_ref[0]
+    moves = fetch(far, near, sems, 4, 12)
+    for n in range(4):
+        for move in moves[n]:
+            move.wait()
+        down = pick_product(
+            x, table, 7 + 3 * n, middle, lambda r: factor_share(near[r, n, 8:12]), n // 2
+        )
+
+        def store(r, k, tile, n=n):
+            out[8 * n + k, lax.rem(r + NX - x, NX)] = tile
+
+        target = (fwd[n] - down).astype(BF)
+        solve_rows(target, lambda r: inverse_share(near[r, n, 0:8]), store)
 
 
 def leaf_backward(x, table, middle, fwd, weights):
     return pl.pallas_call(
         leaf_backward_kernel,
-        grid=(4,),
         out_shape=jax.ShapeDtypeStruct((NP, NX, RX, 128), BF),
-        in_specs=[SMEM] * 2
-        + [
-            whole(NP, 2, RX, 128),
-            pl.BlockSpec((1, RX, 128), lambda n: (n, 0, 0)),
-            pl.BlockSpec((NX, 1, 12, 128, 128), lambda n: (0, n, 0, 0, 0)),
-        ],
-        out_specs=pl.BlockSpec((8, NX, RX, 128), lambda n: (n, 0, 0, 0)),
+        in_specs=[SMEM] * 2 + [VMEM] * 2 + [HBM],
+        scratch_shapes=[
+            pltpu.VMEM((NX, 4, 12, 128, 128), BF),
+            pltpu.SemaphoreType.DMA((4 * NX,)),
+        ],
         compiler_params=params(LARGE),
         name="leaf_backward",
     )(x, table, middle, fwd, weights)

time: 305 us -> 311 us (1.020)
  Pallas kernels: 32.5 us -> 37.1 us
    pallas_call x1, Pallas kernels: 1.54 us -> 4.74 us  [middle_forward(): pl.pallas_call(middle_forward_kernel, out_shape=[jax.ShapeDtypeStruct((2,...]
    unnamed x36 -> x44, local copies, waits for them, and re-layouts: 6.43 us -> 6.37 us
  transfers between devices with their start and end apart: 22 -> 22, of which waited for: 16 -> 15; matrix products, arithmetic and copies ran while one was open for 2% -> 2% of each run, Pallas kernels for 7% -> 8%
where the time goes in v5:
time: 311 us; the launch traced here: 309 us
  blocking collectives  134 us (43%)
  waiting for transfers between devices  64.8 us (21%)
  starting transfers between devices  47.2 us (15%)
  Pallas kernels  37.1 us (12%)
  between operations  14.2 us (5%)
  local copies, waits for them, and re-layouts  8.74 us (3%)
    all_to_all x9, blocking collectives, exchange(): return lax.all_to_all(value, 'pcol', 0, 0, tiled=True)  134 us
    all_to_all x5, waiting for transfers between devices, exchange(): return lax.all_to_all(value, 'pcol', 0, 0, tiled=True)  37.1 us
    all_to_all x5, starting transfers between devices, exchange(): return lax.all_to_all(value, 'pcol', 0, 0, tiled=True)  29.2 us
    ppermute x12, waiting for transfers between devices, shift(): lax.ppermute(value, 'prow', [(i, (i + distance) % NX) for i in range(NX)])  17.5 us
    ppermute x12, starting transfers between devices, shift(): lax.ppermute(value, 'prow', [(i, (i + distance) % NX) for i in range(NX)])  13.5 us
    all_to_all x1, waiting for transfers between devices, per_device(): got = lax.all_to_all(sent, 'prow', 0, 0, tiled=True)  8.25 us
    pallas_call x1, Pallas kernels, leaf_backward(): pl.pallas_call(leaf_backward_kernel, out_shape=jax.ShapeDtypeStruct((NP,...  6.77 us
    unnamed x44, local copies, waits for them, and re-layouts  6.37 us
  transfers between devices with their start and end apart: 22, of which 15 were waited for; matrix products, arithmetic and copies ran while one was open for 2% of the time, Pallas kernels for 8%

profile of v5, /device:TPU:32, one launch (start us, length us, event | category | flops | bytes accessed | tf_op | source)
XLA Modules:
  0.0 309.2 jit_solution(16764669922376936628)
XLA Ops:
  7.2 4.1 %start.1 = (bf16[4,25,16,128]{3,2,1,0:T(8,128)(2,1)}, bf16[2,16,128,128]{3,2,1,0:T(8,128)(2,1)}, bf16[20,128,128]{2,1,0:T(8,128)(2,1)}) custom-call(s32[1]{0:T(128)} %bitcast.1.place, f32[7,64,1024]{2,1,0:T(8,128)} %right_sub.1, f32[64,1024]{1,0:T(8,128)} %right_root.1, bf16[7,8,128,128]{3,2,1,0:T(8,128)(2,1)} %bitcast.63, bf16[8,128,128]{2,1,0:T(8,128)(2,1)} %bitcast.66, ...), custom_call_target="tpu_custom_call" | custom-call | tf_op jit(solution)/shard_map/start/pallas_call | solution.py:120
  12.1 4.3 %all-to-all-start = ((bf16[4,25,16,128]{3,2,1,0:T(8,128)(2,1)}), bf16[4,25,16,128]{3,2,1,0:T(8,128)(2,1)S(1)}, u32[]{:S(2)}, u32[]{:S(2)}) async-start(bf16[4,25,16,128]{3,2,1,0:T(8,128)(2,1)} %get-tuple-element.21), calls=%async_computation | async-start | bytes 819200 | tf_op jit(solution)/shard_map/all_to_all | solution.py:532
  16.4 8.2 %all-to-all-done.got = bf16[4,25,16,128]{3,2,1,0:T(8,128)(2,1)S(1)} async-done(((bf16[4,25,16,128]{3,2,1,0:T(8,128)(2,1)}), bf16[4,25,16,128]{3,2,1,0:T(8,128)(2,1)S(1)}, u32[]{:S(2)}, u32[]{:S(2)}) %all-to-all-start) | async-done | bytes 409632 | tf_op jit(solution)/shard_map/all_to_all | solution.py:532
  25.4 4.9 %leaf_update.1 = (f32[4,16,128]{2,1,0:T(8,128)}, bf16[4,16,512]{2,1,0:T(8,128)(2,1)}, bf16[4,16,512]{2,1,0:T(8,128)(2,1)}, bf16[4,16,512]{2,1,0:T(8,128)(2,1)}, ...) custom-call(s32[1]{0:T(128)} %bitcast.x_ref, ...), custom_call_target="tpu_custom_call" | custom-call | tf_op jit(solution)/shard_map/leaf_update/pallas_call | solution.py:167
  35.2 3.4 %collective-permute-done.c1 = bf16[4,16,512]{2,1,0:T(8,128)(2,1)S(1)} collective-permute-done((bf16[4,16,512]{2,1,0:T(8,128)(2,1)S(1)}, bf16[4,16,512]{2,1,0:T(8,128)(2,1)S(1)}, u32[]{:S(2)}, u32[]{:S(2)}) %collective-permute-start) | collective-permute-done | bytes 65568 | tf_op jit(solution)/shard_map/ppermute | solution.py:30
  42.9 11.3 %all-to-all-start.1 = ((bf16[32,2,16,128]{3,2,1,0:T(8,128)(2,1)}), bf16[32,2,16,128]{3,2,1,0:T(8,128)(2,1)S(1)}, u32[]{:S(2)}, u32[]{:S(2)}) async-start(bf16[32,2,16,128]{3,2,1,0:T(8,128)(2,1)} %leaf_spread.1), calls=%async_computation.1 | async-start | bytes 524288 | tf_op jit(solution)/shard_map/all_to_all | solution.py:42
  55.0 10.2 %all-to-all-done.1 = bf16[32,2,16,128]{3,2,1,0:T(8,128)(2,1)S(1)} async-done(((bf16[32,2,16,128]{3,2,1,0:T(8,128)(2,1)}), bf16[32,2,16,128]{3,2,1,0:T(8,128)(2,1)S(1)}, u32[]{:S(2)}, u32[]{:S(2)}) %all-to-all-start.1) | async-done | bytes 262176 | tf_op jit(solution)/shard_map/all_to_all | solution.py:42
  66.0 4.5 %all-to-all-start.2 = ((bf16[32,2,16,128]{3,2,1,0:T(8,128)(2,1)}), bf16[32,2,16,128]{3,2,1,0:T(8,128)(2,1)S(1)}, u32[]{:S(2)}, u32[]{:S(2)}) async-start(bf16[32,2,16,128]{3,2,1,0:T(8,128)(2,1)} %broadcast_in_dim.26), calls=%async_computation.2 | async-start | bytes 524288 | tf_op jit(solution)/shard_map/all_to_all | solution.py:42
  74.0 4.2 %collective-permute-done.3.o1 = bf16[8,16,512]{2,1,0:T(8,128)(2,1)S(1)} collective-permute-done((bf16[8,16,512]{2,1,0:T(8,128)(2,1)S(1)}, bf16[8,16,512]{2,1,0:T(8,128)(2,1)S(1)}, u32[]{:S(2)}, u32[]{:S(2)}) %collective-permute-start.3) | collective-permute-done | bytes 131104 | tf_op jit(solution)/shard_map/ppermute | solution.py:30
  79.1 2.5 all-to-all-done.2.values
  82.3 4.7 %middle_forward.1 = (f32[2,16,128]{2,1,0:T(8,128)}, bf16[32,16,128]{2,1,0:T(8,128)(2,1)}, f32[32,16,128]{2,1,0:T(8,128)}) custom-call(s32[1]{0:T(128)} %bitcast.x_ref, s32[4,2,17]{2,1,0:T(2,128)} %copy-done.5, bf16[32,2,16,128]{3,2,1,0:T(8,128)(2,1)} %copy-done.12, bf16[4,2,16,128,128]{4,3,2,1,0:T(8,128)(2,1)} %bitcast.61, ...), custom_call_target="tpu_custom_call" | custom-call | tf_op jit(solution)/shard_map/middle_forward/pallas_call | solution.py:316
  87.0 17.2 %all_to_all.75 = bf16[32,16,128]{2,1,0:T(8,128)(2,1)S(1)} all-to-all(bf16[32,16,128]{2,1,0:T(8,128)(2,1)} %get-tuple-element.31), channel_id=1, replica_groups=mesh['layer'=2,'prow'=4,'pcol'=32] {'pcol'}, dimensions={0} | all-to-all | bytes 262144 | tf_op jit(solution)/shard_map/all_to_all | solution.py:42
  105.0 4.4 %all-to-all-start.4 = ((bf16[32,16,128]{2,1,0:T(8,128)(2,1)}), bf16[32,16,128]{2,1,0:T(8,128)(2,1)S(1)}, u32[]{:S(2)}, u32[]{:S(2)}) async-start(bf16[32,16,128]{2,1,0:T(8,128)(2,1)} %broadcast_in_dim.28), calls=%async_computation.4 | async-start | bytes 262144 | tf_op jit(solution)/shard_map/all_to_all | solution.py:42
  109.4 9.7 %all-to-all-done.4.values = bf16[32,16,128]{2,1,0:T(8,128)(2,1)S(1)} async-done(((bf16[32,16,128]{2,1,0:T(8,128)(2,1)}), bf16[32,16,128]{2,1,0:T(8,128)(2,1)S(1)}, u32[]{:S(2)}, u32[]{:S(2)}) %all-to-all-start.4) | async-done | bytes 131104 | tf_op jit(solution)/shard_map/all_to_all | solution.py:42
  123.6 13.9 %all_to_all.76 = bf16[32,16,128]{2,1,0:T(8,128)(2,1)S(1)} all-to-all(bf16[32,16,128]{2,1,0:T(8,128)(2,1)S(1)} %get-tuple-element.34), channel_id=1, replica_groups=mesh['layer'=2,'prow'=4,'pcol'=32] {'pcol'}, dimensions={0} | all-to-all | bytes 262144 | tf_op jit(solution)/shard_map/all_to_all | solution.py:42
  138.9 14.2 %all_to_all.77.values = bf16[32,16,128]{2,1,0:T(8,128)(2,1)S(1)} all-to-all(bf16[32,16,128]{2,1,0:T(8,128)(2,1)S(1)} %broadcast_in_dim.29), channel_id=1, replica_groups=mesh['layer'=2,'prow'=4,'pcol'=32] {'pcol'}, dimensions={0} | all-to-all | bytes 262144 | tf_op jit(solution)/shard_map/all_to_all | solution.py:42
  153.8 13.9 %all_to_all.78 = bf16[32,16,128]{2,1,0:T(8,128)(2,1)S(1)} all-to-all(bf16[32,16,128]{2,1,0:T(8,128)(2,1)S(1)} %root_solve.1), channel_id=1, replica_groups=mesh['layer'=2,'prow'=4,'pcol'=32] {'pcol'}, dimensions={0} | all-to-all | bytes 262144 | tf_op jit(solution)/shard_map/all_to_all | solution.py:42
  167.7 13.8 %all_to_all.79.root = bf16[32,16,128]{2,1,0:T(8,128)(2,1)S(1)} all-to-all(bf16[32,16,128]{2,1,0:T(8,128)(2,1)S(1)} %broadcast_in_dim.30), channel_id=1, replica_groups=mesh['layer'=2,'prow'=4,'pcol'=32] {'pcol'}, dimensions={0} | all-to-all | bytes 262144 | tf_op jit(solution)/shard_map/all_to_all | solution.py:42
  183.0 13.8 %all_to_all.80 = bf16[32,16,128]{2,1,0:T(8,128)(2,1)S(1)} all-to-all(bf16[32,16,128]{2,1,0:T(8,128)(2,1)S(1)} %top_backward.1), channel_id=1, replica_groups=mesh['layer'=2,'prow'=4,'pcol'=32] {'pcol'}, dimensions={0} | all-to-all | bytes 262144 | tf_op jit(solution)/shard_map/all_to_all | solution.py:42
  196.9 14.0 %all_to_all.81.top = bf16[32,16,128]{2,1,0:T(8,128)(2,1)} all-to-all(bf16[32,16,128]{2,1,0:T(8,128)(2,1)S(1)} %broadcast_in_dim.64), channel_id=1, replica_groups=mesh['layer'=2,'prow'=4,'pcol'=32] {'pcol'}, dimensions={0} | all-to-all | bytes 262144 | tf_op jit(solution)/shard_map/all_to_all | solution.py:42
  210.9 5.8 %middle_backward.1 = bf16[32,2,16,128]{3,2,1,0:T(8,128)(2,1)} custom-call(s32[1]{0:T(128)} %bitcast.x_ref, s32[4,2,17]{2,1,0:T(2,128)} %copy-done.5, bf16[32,16,128]{2,1,0:T(8,128)(2,1)} %copy-done.2, bf16[32,16,128]{2,1,0:T(8,128)(2,1)} %all_to_all.81.top, f32[2,16,128]{2,1,0:T(8,128)} %get-tuple-element.36.fwd, bf16[4,2,16,128,128]{4,3,2,1,0:T(8,128)(2,1)} %bitcast.62), custom_call_target="tpu_custom_call" | custom-call | tf_op jit(solution)/shard_map/middle_backward/pallas_call | solution.py:419
  216.7 15.5 %all_to_all.82 = bf16[32,2,16,128]{3,2,1,0:T(8,128)(2,1)S(1)} all-to-all(bf16[32,2,16,128]{3,2,1,0:T(8,128)(2,1)} %middle_backward.1), channel_id=1, replica_groups=mesh['layer'=2,'prow'=4,'pcol'=32] {'pcol'}, dimensions={0} | all-to-all | bytes 524288 | tf_op jit(solution)/shard_map/all_to_all | solution.py:42
  233.0 4.5 %all-to-all-start.12 = ((bf16[32,2,16,128]{3,2,1,0:T(8,128)(2,1)}), bf16[32,2,16,128]{3,2,1,0:T(8,128)(2,1)S(1)}, u32[]{:S(2)}, u32[]{:S(2)}) async-start(bf16[32,2,16,128]{3,2,1,0:T(8,128)(2,1)} %broadcast_in_dim.66), calls=%async_computation.12 | async-start | bytes 524288 | tf_op jit(solution)/shard_map/all_to_all | solution.py:42
  237.5 4.6 %leaf_down.1.fwd = f32[4,16,128]{2,1,0:T(8,128)} custom-call(s32[1]{0:T(128)} %bitcast.x_ref, s32[4,2,17]{2,1,0:T(2,128)} %copy-done.5, bf16[32,16,128]{2,1,0:T(8,128)(2,1)} %copy-done.2, bf16[32,16,128]{2,1,0:T(8,128)(2,1)} %all_to_all.81.top, f32[4,16,128]{2,1,0:T(8,128)} %get-tuple-element.37.fwd, bf16[4,4,20,128,128]{4,3,2,1,0:T(8,128)(2,1)} %bitcast.58, ...), custom_call_target="tpu_custom_call" | custom-call | tf_op jit(solution)/shard_map/leaf_down/pallas_call | solution.py:442
  242.1 6.4 %all-to-all-done.12.middle = bf16[32,2,16,128]{3,2,1,0:T(8,128)(2,1)S(1)} async-done(((bf16[32,2,16,128]{3,2,1,0:T(8,128)(2,1)}), bf16[32,2,16,128]{3,2,1,0:T(8,128)(2,1)S(1)}, u32[]{:S(2)}, u32[]{:S(2)}) %all-to-all-start.12) | async-done | bytes 262176 | tf_op jit(solution)/shard_map/all_to_all | solution.py:42
  249.2 6.8 %leaf_backward.1 = bf16[32,4,16,128]{3,2,1,0:T(8,128)(2,1)} custom-call(s32[1]{0:T(128)} %bitcast.x_ref, s32[4,2,17]{2,1,0:T(2,128)} %copy-done.5, bf16[32,2,16,128]{3,2,1,0:T(8,128)(2,1)} %copy-done.9, f32[4,16,128]{2,1,0:T(8,128)} %leaf_down.1.fwd, bf16[4,4,20,128,128]{4,3,2,1,0:T(8,128)(2,1)} %bitcast.60), custom_call_target="tpu_custom_call" | custom-call | tf_op jit(solution)/shard_map/leaf_backward/pallas_call | solution.py:472
  255.9 4.5 %all-to-all-start.13 = ((bf16[32,4,16,128]{3,2,1,0:T(8,128)(2,1)}), bf16[32,4,16,128]{3,2,1,0:T(8,128)(2,1)S(1)}, u32[]{:S(2)}, u32[]{:S(2)}) async-start(bf16[32,4,16,128]{3,2,1,0:T(8,128)(2,1)} %leaf_backward.1), calls=%async_computation.13 | async-start | bytes 1048576 | tf_op jit(solution)/shard_map/all_to_all | solution.py:42
  262.0 3.6 %collective-permute-start.8 = (bf16[8,4,16,128]{3,2,1,0:T(8,128)(2,1)S(1)}, bf16[8,4,16,128]{3,2,1,0:T(8,128)(2,1)S(1)}, u32[]{:S(2)}, u32[]{:S(2)}) collective-permute-start(bf16[8,4,16,128]{3,2,1,0:T(8,128)(2,1)S(1)} %get-tuple-element.41), channel_id=1, source_target_pairs={{0,64},{32,96},{64,0},{96,32},{1,65},{33,97},{65,1},{97,33},{2,66}... | collective-permute-start | bytes 393224 | tf_op jit(solution)/shard_map/ppermute | solution.py:30
  265.6 8.3 %all-to-all-done.13 = bf16[32,4,16,128]{3,2,1,0:T(8,128)(2,1)S(1)} async-done(((bf16[32,4,16,128]{3,2,1,0:T(8,128)(2,1)}), bf16[32,4,16,128]{3,2,1,0:T(8,128)(2,1)S(1)}, u32[]{:S(2)}, u32[]{:S(2)}) %all-to-all-start.13) | async-done | bytes 524320 | tf_op jit(solution)/shard_map/all_to_all | solution.py:42
  274.0 2.6 collective-permute-start.12
  278.0 3.7 %collective-permute-done.11 = bf16[16,128]{1,0:T(8,128)(2,1)S(1)} collective-permute-done((bf16[16,128]{1,0:T(8,128)(2,1)S(1)}, bf16[16,128]{1,0:T(8,128)(2,1)S(1)}, u32[]{:S(2)}, u32[]{:S(2)}) %collective-permute-start.11) | collective-permute-done | bytes 4128 | tf_op jit(solution)/shard_map/ppermute | solution.py:30
  283.1 18.1 %all_to_all.83.leaves = bf16[32,4,16,128]{3,2,1,0:T(8,128)(2,1)S(1)} all-to-all(bf16[32,4,16,128]{3,2,1,0:T(8,128)(2,1)S(1)} %broadcast_in_dim.67), channel_id=1, replica_groups=mesh['layer'=2,'prow'=4,'pcol'=32] {'pcol'}, dimensions={0} | all-to-all | bytes 1048576 | tf_op jit(solution)/shard_map/all_to_all | solution.py:42
  (102 shorter events, 33.4 us)
Async XLA Ops:
  7.2 74.4 %all-gather.7.cloned.1.call-start = ((), (), s32[]{:S(2)}) async-start(), calls=%async_computation.15 | async-start | bytes 5242880 | tf_op jit(solution)/shard_map/all_gather | solution.py:512
  11.4 98.0 %all-gather.9.cloned.1.call-start = ((), (), s32[]{:S(2)}) async-start(), calls=%async_computation.16 | async-start | bytes 3276800 | tf_op jit(solution)/shard_map/all_gather | solution.py:512
  12.1 12.6 %all-to-all-start = ((bf16[4,25,16,128]{3,2,1,0:T(8,128)(2,1)}), bf16[4,25,16,128]{3,2,1,0:T(8,128)(2,1)S(1)}, u32[]{:S(2)}, u32[]{:S(2)}) async-start(bf16[4,25,16,128]{3,2,1,0:T(8,128)(2,1)} %get-tuple-element.21), calls=%async_computation | async-start | bytes 819200 | tf_op jit(solution)/shard_map/all_to_all | solution.py:532
  16.4 221.1 %all-gather.11.cloned.1.call-start = ((), (), s32[]{:S(2)}) async-start(), calls=%async_computation.17 | async-start | bytes 13107200 | tf_op jit(solution)/shard_map/all_gather | solution.py:512
  30.4 11.0 %copy-start.8 = (bf16[4,16,512]{2,1,0:T(8,128)(2,1)S(1)}, bf16[4,16,512]{2,1,0:T(8,128)(2,1)}, u32[]{:S(2)}) copy-start(bf16[4,16,512]{2,1,0:T(8,128)(2,1)} %get-tuple-element.22.c0) | copy-start | bytes 196612
  30.4 40.1 %copy-start.18 = (bf16[8,16,512]{2,1,0:T(8,128)(2,1)S(1)}, bf16[8,16,512]{2,1,0:T(8,128)(2,1)}, u32[]{:S(2)}) copy-start(bf16[8,16,512]{2,1,0:T(8,128)(2,1)} %get-tuple-element.28) | copy-start | bytes 393220
  30.4 40.2 %copy-start.17 = (bf16[8,16,512]{2,1,0:T(8,128)(2,1)S(1)}, bf16[8,16,512]{2,1,0:T(8,128)(2,1)}, u32[]{:S(2)}) copy-start(bf16[8,16,512]{2,1,0:T(8,128)(2,1)} %get-tuple-element.29) | copy-start | bytes 393220
  30.4 42.3 %copy-start.16 = (bf16[8,16,512]{2,1,0:T(8,128)(2,1)S(1)}, bf16[8,16,512]{2,1,0:T(8,128)(2,1)}, u32[]{:S(2)}) copy-start(bf16[8,16,512]{2,1,0:T(8,128)(2,1)} %get-tuple-element.30) | copy-start | bytes 393220
  31.2 7.4 %collective-permute-start = (bf16[4,16,512]{2,1,0:T(8,128)(2,1)S(1)}, bf16[4,16,512]{2,1,0:T(8,128)(2,1)S(1)}, u32[]{:S(2)}, u32[]{:S(2)}) collective-permute-start(bf16[4,16,512]{2,1,0:T(8,128)(2,1)S(1)} %copy-done.21), channel_id=1, source_target_pairs={{0,32},{32,64},{64,96},{96,0},{1,33},{33,65},{65,97},{97,1},{2,34}... | collective-permute-start | bytes 196616 | tf_op jit(solution)/shard_map/ppermute | solution.py:30
  31.8 8.2 %collective-permute-start.1 = (bf16[4,16,512]{2,1,0:T(8,128)(2,1)S(1)}, bf16[4,16,512]{2,1,0:T(8,128)(2,1)S(1)}, u32[]{:S(2)}, u32[]{:S(2)}) collective-permute-start(bf16[4,16,512]{2,1,0:T(8,128)(2,1)S(1)} %copy-done.20), channel_id=1, source_target_pairs={{0,64},{32,96},{64,0},{96,32},{1,65},{33,97},{65,1},{97,33},{2,66}... | collective-permute-start | bytes 196616 | tf_op jit(solution)/shard_map/ppermute | solution.py:30
  33.7 7.7 %collective-permute-start.2 = (bf16[4,16,512]{2,1,0:T(8,128)(2,1)S(1)}, bf16[4,16,512]{2,1,0:T(8,128)(2,1)S(1)}, u32[]{:S(2)}, u32[]{:S(2)}) collective-permute-start(bf16[4,16,512]{2,1,0:T(8,128)(2,1)S(1)} %copy-done.19), channel_id=1, source_target_pairs={{0,96},{32,0},{64,32},{96,64},{1,97},{33,1},{65,33},{97,65},{2,98}... | collective-permute-start | bytes 196616 | tf_op jit(solution)/shard_map/ppermute | solution.py:30
  35.2 46.3 %copy-start.5 = (s32[4,2,17]{2,1,0:T(2,128)}, s32[4,2,17]{2,1,0:T(2,128)S(1)}, u32[]{:S(2)}) copy-start(s32[4,2,17]{2,1,0:T(2,128)S(1)} %fusion.7.table) | copy-start | bytes 1636
  42.9 22.3 %all-to-all-start.1 = ((bf16[32,2,16,128]{3,2,1,0:T(8,128)(2,1)}), bf16[32,2,16,128]{3,2,1,0:T(8,128)(2,1)S(1)}, u32[]{:S(2)}, u32[]{:S(2)}) async-start(bf16[32,2,16,128]{3,2,1,0:T(8,128)(2,1)} %leaf_spread.1), calls=%async_computation.1 | async-start | bytes 524288 | tf_op jit(solution)/shard_map/all_to_all | solution.py:42
  66.0 15.5 %all-to-all-start.2 = ((bf16[32,2,16,128]{3,2,1,0:T(8,128)(2,1)}), bf16[32,2,16,128]{3,2,1,0:T(8,128)(2,1)S(1)}, u32[]{:S(2)}, u32[]{:S(2)}) async-start(bf16[32,2,16,128]{3,2,1,0:T(8,128)(2,1)} %broadcast_in_dim.26), calls=%async_computation.2 | async-start | bytes 524288 | tf_op jit(solution)/shard_map/all_to_all | solution.py:42
  70.5 7.7 %collective-permute-start.3 = (bf16[8,16,512]{2,1,0:T(8,128)(2,1)S(1)}, bf16[8,16,512]{2,1,0:T(8,128)(2,1)S(1)}, u32[]{:S(2)}, u32[]{:S(2)}) collective-permute-start(bf16[8,16,512]{2,1,0:T(8,128)(2,1)S(1)} %copy-done.18), channel_id=1, source_target_pairs={{0,32},{32,64},{64,96},{96,0},{1,33},{33,65},{65,97},{97,1},{2,34}... | collective-permute-start | bytes 393224 | tf_op jit(solution)/shard_map/ppermute | solution.py:30
  70.6 7.6 %collective-permute-start.4 = (bf16[8,16,512]{2,1,0:T(8,128)(2,1)S(1)}, bf16[8,16,512]{2,1,0:T(8,128)(2,1)S(1)}, u32[]{:S(2)}, u32[]{:S(2)}) collective-permute-start(bf16[8,16,512]{2,1,0:T(8,128)(2,1)S(1)} %copy-done.17), channel_id=1, source_target_pairs={{0,64},{32,96},{64,0},{96,32},{1,65},{33,97},{65,1},{97,33},{2,66}... | collective-permute-start | bytes 393224 | tf_op jit(solution)/shard_map/ppermute | solution.py:30
  72.7 6.4 %collective-permute-start.5 = (bf16[8,16,512]{2,1,0:T(8,128)(2,1)S(1)}, bf16[8,16,512]{2,1,0:T(8,128)(2,1)S(1)}, u32[]{:S(2)}, u32[]{:S(2)}) collective-permute-start(bf16[8,16,512]{2,1,0:T(8,128)(2,1)S(1)} %copy-done.16), channel_id=1, source_target_pairs={{0,96},{32,0},{64,32},{96,64},{1,97},{33,1},{65,33},{97,65},{2,98}... | collective-permute-start | bytes 393224 | tf_op jit(solution)/shard_map/ppermute | solution.py:30
  78.2 3.4 %copy-start.14 = (bf16[8,16,512]{2,1,0:T(8,128)(2,1)}, bf16[8,16,512]{2,1,0:T(8,128)(2,1)S(1)}, u32[]{:S(2)}) copy-start(bf16[8,16,512]{2,1,0:T(8,128)(2,1)S(1)} %collective-permute-done.4.o2) | copy-start | bytes 393220
  105.0 14.2 %all-to-all-start.4 = ((bf16[32,16,128]{2,1,0:T(8,128)(2,1)}), bf16[32,16,128]{2,1,0:T(8,128)(2,1)S(1)}, u32[]{:S(2)}, u32[]{:S(2)}) async-start(bf16[32,16,128]{2,1,0:T(8,128)(2,1)} %broadcast_in_dim.28), calls=%async_computation.4 | async-start | bytes 262144 | tf_op jit(solution)/shard_map/all_to_all | solution.py:42
  122.6 30.5 %copy-start.1 = (bf16[80,128,128]{2,1,0:T(8,128)(2,1)S(1)}, bf16[80,128,128]{2,1,0:T(8,128)(2,1)}, u32[]{:S(2)}) copy-start(bf16[80,128,128]{2,1,0:T(8,128)(2,1)} %all-gather.9.cloned.1.call-done) | copy-start | bytes 7864324
  123.6 57.9 %copy-start.7 = (s32[4,2,17]{2,1,0:T(2,128)S(1)}, s32[4,2,17]{2,1,0:T(2,128)}, u32[]{:S(2)}) copy-start(s32[4,2,17]{2,1,0:T(2,128)} %copy-done.5) | copy-start | bytes 1636
  137.6 1.3 collective-permute-start.6
  233.0 15.5 %all-to-all-start.12 = ((bf16[32,2,16,128]{3,2,1,0:T(8,128)(2,1)}), bf16[32,2,16,128]{3,2,1,0:T(8,128)(2,1)S(1)}, u32[]{:S(2)}, u32[]{:S(2)}) async-start(bf16[32,2,16,128]{3,2,1,0:T(8,128)(2,1)} %broadcast_in_dim.66), calls=%async_computation.12 | async-start | bytes 524288 | tf_op jit(solution)/shard_map/all_to_all | solution.py:42
  242.1 18.4 %copy-start.3 = (bf16[32,16,128]{2,1,0:T(8,128)(2,1)S(1)}, bf16[32,16,128]{2,1,0:T(8,128)(2,1)}, u32[]{:S(2)}) copy-start(bf16[32,16,128]{2,1,0:T(8,128)(2,1)} %copy-done.2) | copy-start | bytes 393220
  242.1 18.4 %copy-start.10 = (bf16[32,16,128]{2,1,0:T(8,128)(2,1)S(1)}, bf16[32,16,128]{2,1,0:T(8,128)(2,1)}, u32[]{:S(2)}) copy-start(bf16[32,16,128]{2,1,0:T(8,128)(2,1)} %all_to_all.81.top) | copy-start | bytes 393220
  255.9 17.9 %all-to-all-start.13 = ((bf16[32,4,16,128]{3,2,1,0:T(8,128)(2,1)}), bf16[32,4,16,128]{3,2,1,0:T(8,128)(2,1)S(1)}, u32[]{:S(2)}, u32[]{:S(2)}) async-start(bf16[32,4,16,128]{3,2,1,0:T(8,128)(2,1)} %leaf_backward.1), calls=%async_computation.13 | async-start | bytes 1048576 | tf_op jit(solution)/shard_map/all_to_all | solution.py:42
  261.5 21.4 %collective-permute-start.7 = (bf16[8,4,16,128]{3,2,1,0:T(8,128)(2,1)S(1)}, bf16[8,4,16,128]{3,2,1,0:T(8,128)(2,1)S(1)}, u32[]{:S(2)}, u32[]{:S(2)}) collective-permute-start(bf16[8,4,16,128]{3,2,1,0:T(8,128)(2,1)S(1)} %get-tuple-element.42), channel_id=1, source_target_pairs={{0,32},{32,64},{64,96},{96,0},{1,33},{33,65},{65,97},{97,1},{2,34}... | collective-permute-start | bytes 393224 | tf_op jit(solution)/shard_map/ppermute | solution.py:30
  262.0 21.0 %collective-permute-start.8 = (bf16[8,4,16,128]{3,2,1,0:T(8,128)(2,1)S(1)}, bf16[8,4,16,128]{3,2,1,0:T(8,128)(2,1)S(1)}, u32[]{:S(2)}, u32[]{:S(2)}) collective-permute-start(bf16[8,4,16,128]{3,2,1,0:T(8,128)(2,1)S(1)} %get-tuple-element.41), channel_id=1, source_target_pairs={{0,64},{32,96},{64,0},{96,32},{1,65},{33,97},{65,1},{97,33},{2,66}... | collective-permute-start | bytes 393224 | tf_op jit(solution)/shard_map/ppermute | solution.py:30
  265.6 17.4 %collective-permute-start.9 = (bf16[8,4,16,128]{3,2,1,0:T(8,128)(2,1)S(1)}, bf16[8,4,16,128]{3,2,1,0:T(8,128)(2,1)S(1)}, u32[]{:S(2)}, u32[]{:S(2)}) collective-permute-start(bf16[8,4,16,128]{3,2,1,0:T(8,128)(2,1)S(1)} %get-tuple-element.40), channel_id=1, source_target_pairs={{0,96},{32,0},{64,32},{96,64},{1,97},{33,1},{65,33},{97,65},{2,98}... | collective-permute-start | bytes 393224 | tf_op jit(solution)/shard_map/ppermute | solution.py:30
  274.0 3.9 %collective-permute-start.12 = (bf16[16,128]{1,0:T(8,128)(2,1)S(1)}, bf16[16,128]{1,0:T(8,128)(2,1)S(1)}, u32[]{:S(2)}, u32[]{:S(2)}) collective-permute-start(bf16[16,128]{1,0:T(8,128)(2,1)S(1)} %get-tuple-element.45), channel_id=1, source_target_pairs={{0,96},{32,0},{64,32},{96,64},{1,97},{33,1},{65,33},{97,65},{2,98}... | collective-permute-start | bytes 12296 | tf_op jit(solution)/shard_map/ppermute | solution.py:30
  276.6 5.1 %collective-permute-start.11 = (bf16[16,128]{1,0:T(8,128)(2,1)S(1)}, bf16[16,128]{1,0:T(8,128)(2,1)S(1)}, u32[]{:S(2)}, u32[]{:S(2)}) collective-permute-start(bf16[16,128]{1,0:T(8,128)(2,1)S(1)} %get-tuple-element.46), channel_id=1, source_target_pairs={{0,64},{32,96},{64,0},{96,32},{1,65},{33,97},{65,1},{97,33},{2,66}... | collective-permute-start | bytes 12296 | tf_op jit(solution)/shard_map/ppermute | solution.py:30
  277.9 5.1 %collective-permute-start.10 = (bf16[16,128]{1,0:T(8,128)(2,1)S(1)}, bf16[16,128]{1,0:T(8,128)(2,1)S(1)}, u32[]{:S(2)}, u32[]{:S(2)}) collective-permute-start(bf16[16,128]{1,0:T(8,128)(2,1)S(1)} %get-tuple-element.47), channel_id=1, source_target_pairs={{0,32},{32,64},{64,96},{96,0},{1,33},{33,65},{65,97},{97,1},{2,34}... | collective-permute-start | bytes 12296 | tf_op jit(solution)/shard_map/ppermute | solution.py:30
  (12 other events, 18.5 us)
Sparse Core Ops, SparseCore 0:
  11.5 56.1 all-gather.6
  69.5 38.0 all-gather.8
  109.5 103.5 all-gather.10

commit v6 on v4

--- a/solution.py
+++ b/solution.py
@@ -193,10 +193,9 @@
 def add_update(acc, table, r, pair, update, *lead):
     for j in range(2):
         block = listed(table, r, pair, j)
-        for h in range(2):
-            index = (2 * block + h, *lead)
-            tile = update[:, 256 * j + 128 * h : 256 * j + 128 * (h + 1)]
-            acc[index] = acc[index] + tile.astype(F32)
+        index = (pl.ds(2 * block, 2), *lead)
+        tiles = [update[:, 256 * j + 128 * h : 256 * j + 128 * (h + 1)] for h in range(2)]
+        acc[index] = acc[index] + jnp.stack(tiles).astype(F32)
 
 
 def leaf_spread_kernel(x_ref, table, c0, c1, c2, c3, out, acc):
@@ -255,7 +254,8 @@
         tiles = []
         for j in range(2):
             block = listed(table, r, pair, j)
-            tiles += [values[(2 * block, *lead)], values[(2 * block + 1, *lead)]]
+            pair_of_tiles = values[(pl.ds(2 * block, 2), *lead)]
+            tiles += [pair_of_tiles[0], pair_of_tiles[1]]
         term = dot_t(jnp.concatenate(tiles, axis=1), factor(r))
         total = term if total is None else total + term
     return total
@@ -427,7 +427,7 @@
     )
 
     def store(r, k, tile):
-        out[k, lax.rem(r + NX - x, NX)] = tile
+        out[r, k] = tile
 
     inverse = lambda r: inverse_share(weights[r, 0, 0:8])
     solve_rows((fwd[0] - down).astype(BF), inverse, store)
@@ -437,14 +437,14 @@
     return pl.pallas_call(
         leaf_backward_kernel,
         grid=(4,),
-        out_shape=jax.ShapeDtypeStruct((NP, NX, RX, 128), BF),
+        out_shape=jax.ShapeDtypeStruct((NX, NP, RX, 128), BF),
         in_specs=[SMEM] * 2
         + [
             whole(NP, 2, RX, 128),
             pl.BlockSpec((1, RX, 128), lambda n: (n, 0, 0)),
             pl.BlockSpec((NX, 1, 12, 128, 128), lambda n: (0, n, 0, 0, 0)),
         ],
-        out_specs=pl.BlockSpec((8, NX, RX, 128), lambda n: (n, 0, 0, 0)),
+        out_specs=pl.BlockSpec((NX, 8, RX, 128), lambda n: (0, n, 0, 0)),
         compiler_params=params(LARGE),
         name="leaf_backward",
     )(x, table, middle, fwd, weights)
@@ -460,7 +460,8 @@
             for t in range(3):
                 out_sub[t, rows, columns] = early[k, 1 + t].astype(F32)
             for t in range(4):
-                out_sub[3 + t, rows, columns] = leaves[8 * t + k, d].astype(F32)
+                tile = leaves[8 * t + k, d].astype(F32)
+                out_sub[3 + t, RX * d : RX * (d + 1), columns] = tile
 
 
 def finish(x, early, leaves):
@@ -528,8 +529,10 @@
         pieces.append(shift(piece, d) if d else piece)
 
     parts = leaf_backward(x, table, middle, fwd_leaf, leaf_weights)
-    chunk = reduce_columns(parts).astype(BF)
-    chunk = jnp.stack([chunk[0]] + [shift(chunk[d], d) for d in range(1, NX)])
+    parts = lax.all_to_all(
+        parts.reshape(NX * NP, RX, 128), ("prow", "pcol"), 0, 0, tiled=True
+    ).reshape(NX, NP, RX, 128)
+    chunk = jnp.sum(parts.astype(F32), axis=1).astype(BF)
     leaves = gather_columns(after(chunk, *pieces))
     return tuple(finish(x, pieces, leaves))
 

time: 305 us -> 302 us (level)
  waiting for transfers between devices: 64.4 us -> 59 us
    all_to_all x0 -> x1, waiting for transfers between devices: none -> 8.81 us  [per_device(): lax.all_to_all(parts.reshape(NX * NP, RX, 128), ('prow', 'pcol'), 0, 0, t...]
    all_to_all x5 -> x4, waiting for transfers between devices: 36.6 us -> 28.4 us  [exchange(): return lax.all_to_all(value, 'pcol', 0, 0, tiled=True)]
    all_to_all x0 -> x1, starting transfers between devices: none -> 7.61 us  [per_device(): lax.all_to_all(parts.reshape(NX * NP, RX, 128), ('prow', 'pcol'), 0, 0, t...]
    ppermute x12 -> x9, waiting for transfers between devices: 17.2 us -> 11.3 us  [shift(): lax.ppermute(value, 'prow', [(i, (i + distance) % NX) for i in range(NX)])]
    all_to_all x5 -> x4, starting transfers between devices: 29.2 us -> 24.7 us  [exchange(): return lax.all_to_all(value, 'pcol', 0, 0, tiled=True)]
    ppermute x12 -> x9, starting transfers between devices: 13.9 us -> 12.8 us  [shift(): lax.ppermute(value, 'prow', [(i, (i + distance) % NX) for i in range(NX)])]
  transfers between devices with their start and end apart: 22 -> 19, of which waited for: 16 -> 13; matrix products, arithmetic and copies ran while one was open for 2% -> 2% of each run, Pallas kernels for 7% -> 7%
where the time goes in v6:
time: 302 us; the launch traced here: 301 us
  blocking collectives  134 us (44%)
  waiting for transfers between devices  59 us (20%)
  starting transfers between devices  49.6 us (16%)
  Pallas kernels  32.5 us (11%)
  between operations  14.1 us (5%)
  local copies, waits for them, and re-layouts  8.79 us (3%)
    all_to_all x9, blocking collectives, exchange(): return lax.all_to_all(value, 'pcol', 0, 0, tiled=True)  134 us
    all_to_all x4, waiting for transfers between devices, exchange(): return lax.all_to_all(value, 'pcol', 0, 0, tiled=True)  28.4 us
    all_to_all x4, starting transfers between devices, exchange(): return lax.all_to_all(value, 'pcol', 0, 0, tiled=True)  24.7 us
    ppermute x9, starting transfers between devices, shift(): lax.ppermute(value, 'prow', [(i, (i + distance) % NX) for i in range(NX)])  12.8 us
    ppermute x9, waiting for transfers between devices, shift(): lax.ppermute(value, 'prow', [(i, (i + distance) % NX) for i in range(NX)])  11.3 us
    all_to_all x1, waiting for transfers between devices, per_device(): lax.all_to_all(parts.reshape(NX * NP, RX, 128), ('prow', 'pcol'), 0, 0, t...  8.81 us
    all_to_all x1, waiting for transfers between devices, per_device(): got = lax.all_to_all(sent, 'prow', 0, 0, tiled=True)  8.25 us
    all_to_all x1, starting transfers between devices, per_device(): lax.all_to_all(parts.reshape(NX * NP, RX, 128), ('prow', 'pcol'), 0, 0, t...  7.61 us
  transfers between devices with their start and end apart: 19, of which 13 were waited for; matrix products, arithmetic and copies ran while one was open for 2% of the time, Pallas kernels for 7%

profile of v6, /device:TPU:32, one launch (start us, length us, event | category | flops | bytes accessed | tf_op | source)
XLA Modules:
  0.0 300.8 jit_solution(5664424637863303758)
XLA Ops:
  7.2 4.1 %start.1 = (bf16[4,25,16,128]{3,2,1,0:T(8,128)(2,1)}, bf16[2,16,128,128]{3,2,1,0:T(8,128)(2,1)}, bf16[20,128,128]{2,1,0:T(8,128)(2,1)}) custom-call(s32[1]{0:T(128)} %bitcast.1.place, f32[7,64,1024]{2,1,0:T(8,128)} %right_sub.1, f32[64,1024]{1,0:T(8,128)} %right_root.1, bf16[7,8,128,128]{3,2,1,0:T(8,128)(2,1)} %bitcast.57, bf16[8,128,128]{2,1,0:T(8,128)(2,1)} %bitcast.61, ...), custom_call_target="tpu_custom_call" | custom-call | tf_op jit(solution)/shard_map/start/pallas_call | solution.py:119
  12.1 4.3 %all-to-all-start = ((bf16[4,25,16,128]{3,2,1,0:T(8,128)(2,1)}), bf16[4,25,16,128]{3,2,1,0:T(8,128)(2,1)S(1)}, u32[]{:S(2)}, u32[]{:S(2)}) async-start(bf16[4,25,16,128]{3,2,1,0:T(8,128)(2,1)} %get-tuple-element.21), calls=%async_computation | async-start | bytes 819200 | tf_op jit(solution)/shard_map/all_to_all | solution.py:501
  16.4 8.2 %all-to-all-done.got = bf16[4,25,16,128]{3,2,1,0:T(8,128)(2,1)S(1)} async-done(((bf16[4,25,16,128]{3,2,1,0:T(8,128)(2,1)}), bf16[4,25,16,128]{3,2,1,0:T(8,128)(2,1)S(1)}, u32[]{:S(2)}, u32[]{:S(2)}) %all-to-all-start) | async-done | bytes 409632 | tf_op jit(solution)/shard_map/all_to_all | solution.py:501
  25.4 4.9 %leaf_update.1 = (f32[4,16,128]{2,1,0:T(8,128)}, bf16[4,16,512]{2,1,0:T(8,128)(2,1)}, bf16[4,16,512]{2,1,0:T(8,128)(2,1)}, bf16[4,16,512]{2,1,0:T(8,128)(2,1)}, ...) custom-call(s32[1]{0:T(128)} %bitcast.x_ref, ...), custom_call_target="tpu_custom_call" | custom-call | tf_op jit(solution)/shard_map/leaf_update/pallas_call | solution.py:166
  31.7 2.0 collective-permute-start.1
  35.2 3.4 %collective-permute-done.c1 = bf16[4,16,512]{2,1,0:T(8,128)(2,1)S(1)} collective-permute-done((bf16[4,16,512]{2,1,0:T(8,128)(2,1)S(1)}, bf16[4,16,512]{2,1,0:T(8,128)(2,1)S(1)}, u32[]{:S(2)}, u32[]{:S(2)}) %collective-permute-start) | collective-permute-done | bytes 65568 | tf_op jit(solution)/shard_map/ppermute | solution.py:29
  42.9 11.3 %all-to-all-start.1 = ((bf16[32,2,16,128]{3,2,1,0:T(8,128)(2,1)}), bf16[32,2,16,128]{3,2,1,0:T(8,128)(2,1)S(1)}, u32[]{:S(2)}, u32[]{:S(2)}) async-start(bf16[32,2,16,128]{3,2,1,0:T(8,128)(2,1)} %leaf_spread.1), calls=%async_computation.1 | async-start | bytes 524288 | tf_op jit(solution)/shard_map/all_to_all | solution.py:41
  55.0 10.2 %all-to-all-done.1 = bf16[32,2,16,128]{3,2,1,0:T(8,128)(2,1)S(1)} async-done(((bf16[32,2,16,128]{3,2,1,0:T(8,128)(2,1)}), bf16[32,2,16,128]{3,2,1,0:T(8,128)(2,1)S(1)}, u32[]{:S(2)}, u32[]{:S(2)}) %all-to-all-start.1) | async-done | bytes 262176 | tf_op jit(solution)/shard_map/all_to_all | solution.py:41
  66.0 4.5 %all-to-all-start.2 = ((bf16[32,2,16,128]{3,2,1,0:T(8,128)(2,1)}), bf16[32,2,16,128]{3,2,1,0:T(8,128)(2,1)S(1)}, u32[]{:S(2)}, u32[]{:S(2)}) async-start(bf16[32,2,16,128]{3,2,1,0:T(8,128)(2,1)} %broadcast_in_dim.26), calls=%async_computation.2 | async-start | bytes 524288 | tf_op jit(solution)/shard_map/all_to_all | solution.py:41
  70.6 2.1 collective-permute-start.4
  74.0 4.2 %collective-permute-done.3.o1 = bf16[8,16,512]{2,1,0:T(8,128)(2,1)S(1)} collective-permute-done((bf16[8,16,512]{2,1,0:T(8,128)(2,1)S(1)}, bf16[8,16,512]{2,1,0:T(8,128)(2,1)S(1)}, u32[]{:S(2)}, u32[]{:S(2)}) %collective-permute-start.3) | collective-permute-done | bytes 131104 | tf_op jit(solution)/shard_map/ppermute | solution.py:29
  79.0 2.5 all-to-all-done.2.values
  81.5 2.4 copy-done.2
  85.5 16.5 %all_to_all.75 = bf16[32,16,128]{2,1,0:T(8,128)(2,1)S(1)} all-to-all(bf16[32,16,128]{2,1,0:T(8,128)(2,1)S(1)} %get-tuple-element.31), channel_id=1, replica_groups=mesh['layer'=2,'prow'=4,'pcol'=32] {'pcol'}, dimensions={0} | all-to-all | bytes 262144 | tf_op jit(solution)/shard_map/all_to_all | solution.py:41
  102.8 4.4 %all-to-all-start.4 = ((bf16[32,16,128]{2,1,0:T(8,128)(2,1)}), bf16[32,16,128]{2,1,0:T(8,128)(2,1)S(1)}, u32[]{:S(2)}, u32[]{:S(2)}) async-start(bf16[32,16,128]{2,1,0:T(8,128)(2,1)} %broadcast_in_dim.28), calls=%async_computation.4 | async-start | bytes 262144 | tf_op jit(solution)/shard_map/all_to_all | solution.py:41
  107.6 9.3 %all-to-all-done.4.values = bf16[32,16,128]{2,1,0:T(8,128)(2,1)S(1)} async-done(((bf16[32,16,128]{2,1,0:T(8,128)(2,1)}), bf16[32,16,128]{2,1,0:T(8,128)(2,1)S(1)}, u32[]{:S(2)}, u32[]{:S(2)}) %all-to-all-start.4) | async-done | bytes 131104 | tf_op jit(solution)/shard_map/all_to_all | solution.py:41
  119.7 13.9 %all_to_all.76 = bf16[32,16,128]{2,1,0:T(8,128)(2,1)S(1)} all-to-all(bf16[32,16,128]{2,1,0:T(8,128)(2,1)S(1)} %get-tuple-element.34), channel_id=1, replica_groups=mesh['layer'=2,'prow'=4,'pcol'=32] {'pcol'}, dimensions={0} | all-to-all | bytes 262144 | tf_op jit(solution)/shard_map/all_to_all | solution.py:41
  134.9 14.2 %all_to_all.77.values = bf16[32,16,128]{2,1,0:T(8,128)(2,1)S(1)} all-to-all(bf16[32,16,128]{2,1,0:T(8,128)(2,1)S(1)} %broadcast_in_dim.29), channel_id=1, replica_groups=mesh['layer'=2,'prow'=4,'pcol'=32] {'pcol'}, dimensions={0} | all-to-all | bytes 262144 | tf_op jit(solution)/shard_map/all_to_all | solution.py:41
  149.8 13.9 %all_to_all.78 = bf16[32,16,128]{2,1,0:T(8,128)(2,1)S(1)} all-to-all(bf16[32,16,128]{2,1,0:T(8,128)(2,1)S(1)} %root_solve.1), channel_id=1, replica_groups=mesh['layer'=2,'prow'=4,'pcol'=32] {'pcol'}, dimensions={0} | all-to-all | bytes 262144 | tf_op jit(solution)/shard_map/all_to_all | solution.py:41
  163.8 13.8 %all_to_all.79.root = bf16[32,16,128]{2,1,0:T(8,128)(2,1)S(1)} all-to-all(bf16[32,16,128]{2,1,0:T(8,128)(2,1)S(1)} %broadcast_in_dim.30), channel_id=1, replica_groups=mesh['layer'=2,'prow'=4,'pcol'=32] {'pcol'}, dimensions={0} | all-to-all | bytes 262144 | tf_op jit(solution)/shard_map/all_to_all | solution.py:41
  179.0 14.0 %all_to_all.80 = bf16[32,16,128]{2,1,0:T(8,128)(2,1)S(1)} all-to-all(bf16[32,16,128]{2,1,0:T(8,128)(2,1)S(1)} %top_backward.1), channel_id=1, replica_groups=mesh['layer'=2,'prow'=4,'pcol'=32] {'pcol'}, dimensions={0} | all-to-all | bytes 262144 | tf_op jit(solution)/shard_map/all_to_all | solution.py:41
  193.1 14.0 %all_to_all.81.top = bf16[32,16,128]{2,1,0:T(8,128)(2,1)} all-to-all(bf16[32,16,128]{2,1,0:T(8,128)(2,1)S(1)} %broadcast_in_dim.64), channel_id=1, replica_groups=mesh['layer'=2,'prow'=4,'pcol'=32] {'pcol'}, dimensions={0} | all-to-all | bytes 262144 | tf_op jit(solution)/shard_map/all_to_all | solution.py:41
  207.1 4.9 %middle_backward.1 = bf16[32,2,16,128]{3,2,1,0:T(8,128)(2,1)} custom-call(s32[1]{0:T(128)} %bitcast.x_ref, s32[4,2,17]{2,1,0:T(2,128)} %copy-done.5, bf16[32,16,128]{2,1,0:T(8,128)(2,1)} %copy-done.3, bf16[32,16,128]{2,1,0:T(8,128)(2,1)} %all_to_all.81.top, f32[2,16,128]{2,1,0:T(8,128)} %copy-done.8, bf16[4,2,16,128,128]{4,3,2,1,0:T(8,128)(2,1)} %bitcast.51), custom_call_target="tpu_custom_call" | custom-call | tf_op jit(solution)/shard_map/middle_backward/pallas_call | solution.py:392
  212.0 15.4 %all_to_all.82 = bf16[32,2,16,128]{3,2,1,0:T(8,128)(2,1)S(1)} all-to-all(bf16[32,2,16,128]{3,2,1,0:T(8,128)(2,1)} %middle_backward.1), channel_id=1, replica_groups=mesh['layer'=2,'prow'=4,'pcol'=32] {'pcol'}, dimensions={0} | all-to-all | bytes 524288 | tf_op jit(solution)/shard_map/all_to_all | solution.py:41
  228.2 4.5 %all-to-all-start.12 = ((bf16[32,2,16,128]{3,2,1,0:T(8,128)(2,1)}), bf16[32,2,16,128]{3,2,1,0:T(8,128)(2,1)S(1)}, u32[]{:S(2)}, u32[]{:S(2)}) async-start(bf16[32,2,16,128]{3,2,1,0:T(8,128)(2,1)} %broadcast_in_dim.66), calls=%async_computation.12 | async-start | bytes 524288 | tf_op jit(solution)/shard_map/all_to_all | solution.py:41
  232.8 4.6 %leaf_down.1.fwd = f32[4,16,128]{2,1,0:T(8,128)} custom-call(s32[1]{0:T(128)} %bitcast.x_ref, s32[4,2,17]{2,1,0:T(2,128)} %copy-done.5, bf16[32,16,128]{2,1,0:T(8,128)(2,1)} %copy-done.3, bf16[32,16,128]{2,1,0:T(8,128)(2,1)} %all_to_all.81.top, f32[4,16,128]{2,1,0:T(8,128)} %get-tuple-element.37.fwd, bf16[4,4,20,128,128]{4,3,2,1,0:T(8,128)(2,1)} %bitcast.54, ...), custom_call_target="tpu_custom_call" | custom-call | tf_op jit(solution)/shard_map/leaf_down/pallas_call | solution.py:411
  237.3 6.4 %all-to-all-done.12.middle = bf16[32,2,16,128]{3,2,1,0:T(8,128)(2,1)S(1)} async-done(((bf16[32,2,16,128]{3,2,1,0:T(8,128)(2,1)}), bf16[32,2,16,128]{3,2,1,0:T(8,128)(2,1)S(1)}, u32[]{:S(2)}, u32[]{:S(2)}) %all-to-all-start.12) | async-done | bytes 262176 | tf_op jit(solution)/shard_map/all_to_all | solution.py:41
  244.4 6.3 %leaf_backward.1 = bf16[4,32,16,128]{3,2,1,0:T(8,128)(2,1)} custom-call(s32[1]{0:T(128)} %bitcast.x_ref, s32[4,2,17]{2,1,0:T(2,128)} %copy-done.5, bf16[32,2,16,128]{3,2,1,0:T(8,128)(2,1)} %copy-done.9, f32[4,16,128]{2,1,0:T(8,128)} %leaf_down.1.fwd, bf16[4,4,20,128,128]{4,3,2,1,0:T(8,128)(2,1)} %bitcast.56), custom_call_target="tpu_custom_call" | custom-call | tf_op jit(solution)/shard_map/leaf_backward/pallas_call | solution.py:437
  250.8 7.6 %all-to-all-start.13 = ((bf16[128,16,128]{2,1,0:T(8,128)(2,1)}), bf16[128,16,128]{2,1,0:T(8,128)(2,1)S(1)}, u32[]{:S(2)}, u32[]{:S(2)}) async-start(bf16[128,16,128]{2,1,0:T(8,128)(2,1)} %bitcast.60), calls=%async_computation.13 | async-start | bytes 1048576 | tf_op jit(solution)/shard_map/all_to_all | solution.py:532
  261.1 3.1 %collective-permute-start.8 = (bf16[8,4,16,128]{3,2,1,0:T(8,128)(2,1)S(1)}, bf16[8,4,16,128]{3,2,1,0:T(8,128)(2,1)S(1)}, u32[]{:S(2)}, u32[]{:S(2)}) collective-permute-start(bf16[8,4,16,128]{3,2,1,0:T(8,128)(2,1)S(1)} %get-tuple-element.41), channel_id=1, source_target_pairs={{0,64},{32,96},{64,0},{96,32},{1,65},{33,97},{65,1},{97,33},{2,66}... | collective-permute-start | bytes 393224 | tf_op jit(solution)/shard_map/ppermute | solution.py:29
  265.5 8.8 %all-to-all-done.13 = bf16[128,16,128]{2,1,0:T(8,128)(2,1)S(1)} async-done(((bf16[128,16,128]{2,1,0:T(8,128)(2,1)}), bf16[128,16,128]{2,1,0:T(8,128)(2,1)S(1)}, u32[]{:S(2)}, u32[]{:S(2)}) %all-to-all-start.13) | async-done | bytes 524320 | tf_op jit(solution)/shard_map/all_to_all | solution.py:532
  274.5 18.3 %all_to_all.83.leaves = bf16[32,4,16,128]{3,2,1,0:T(8,128)(2,1)S(1)} all-to-all(bf16[32,4,16,128]{3,2,1,0:T(8,128)(2,1)S(1)} %broadcast_in_dim.67), channel_id=1, replica_groups=mesh['layer'=2,'prow'=4,'pcol'=32] {'pcol'}, dimensions={0} | all-to-all | bytes 1048576 | tf_op jit(solution)/shard_map/all_to_all | solution.py:41
  (86 shorter events, 28.7 us)
Async XLA Ops:
  7.2 74.4 %all-gather.7.cloned.1.call-start = ((), (), s32[]{:S(2)}) async-start(), calls=%async_computation.15 | async-start | bytes 5242880 | tf_op jit(solution)/shard_map/all_gather | solution.py:481
  11.3 96.3 %all-gather.9.cloned.1.call-start = ((), (), s32[]{:S(2)}) async-start(), calls=%async_computation.16 | async-start | bytes 3276800 | tf_op jit(solution)/shard_map/all_gather | solution.py:481
  12.1 12.6 %all-to-all-start = ((bf16[4,25,16,128]{3,2,1,0:T(8,128)(2,1)}), bf16[4,25,16,128]{3,2,1,0:T(8,128)(2,1)S(1)}, u32[]{:S(2)}, u32[]{:S(2)}) async-start(bf16[4,25,16,128]{3,2,1,0:T(8,128)(2,1)} %get-tuple-element.21), calls=%async_computation | async-start | bytes 819200 | tf_op jit(solution)/shard_map/all_to_all | solution.py:501
  16.4 216.3 %all-gather.11.cloned.1.call-start = ((), (), s32[]{:S(2)}) async-start(), calls=%async_computation.17 | async-start | bytes 13107200 | tf_op jit(solution)/shard_map/all_gather | solution.py:481
  30.3 3.4 %copy-start.15 = (bf16[4,16,512]{2,1,0:T(8,128)(2,1)S(1)}, bf16[4,16,512]{2,1,0:T(8,128)(2,1)}, u32[]{:S(2)}) copy-start(bf16[4,16,512]{2,1,0:T(8,128)(2,1)} %get-tuple-element.25) | copy-start | bytes 196612
  30.3 11.0 %copy-start.7 = (bf16[4,16,512]{2,1,0:T(8,128)(2,1)S(1)}, bf16[4,16,512]{2,1,0:T(8,128)(2,1)}, u32[]{:S(2)}) copy-start(bf16[4,16,512]{2,1,0:T(8,128)(2,1)} %get-tuple-element.22.c0) | copy-start | bytes 196612
  30.4 40.1 %copy-start.14 = (bf16[8,16,512]{2,1,0:T(8,128)(2,1)S(1)}, bf16[8,16,512]{2,1,0:T(8,128)(2,1)}, u32[]{:S(2)}) copy-start(bf16[8,16,512]{2,1,0:T(8,128)(2,1)} %get-tuple-element.28) | copy-start | bytes 393220
  30.4 40.2 %copy-start.13 = (bf16[8,16,512]{2,1,0:T(8,128)(2,1)S(1)}, bf16[8,16,512]{2,1,0:T(8,128)(2,1)}, u32[]{:S(2)}) copy-start(bf16[8,16,512]{2,1,0:T(8,128)(2,1)} %get-tuple-element.29) | copy-start | bytes 393220
  30.4 42.3 %copy-start.12 = (bf16[8,16,512]{2,1,0:T(8,128)(2,1)S(1)}, bf16[8,16,512]{2,1,0:T(8,128)(2,1)}, u32[]{:S(2)}) copy-start(bf16[8,16,512]{2,1,0:T(8,128)(2,1)} %get-tuple-element.30) | copy-start | bytes 393220
  30.4 51.1 %copy-start.6 = (bf16[8,16,512]{2,1,0:T(8,128)(2,1)S(1)}, bf16[8,16,512]{2,1,0:T(8,128)(2,1)}, u32[]{:S(2)}) copy-start(bf16[8,16,512]{2,1,0:T(8,128)(2,1)} %get-tuple-element.27.o0) | copy-start | bytes 393220
  31.2 7.4 %collective-permute-start = (bf16[4,16,512]{2,1,0:T(8,128)(2,1)S(1)}, bf16[4,16,512]{2,1,0:T(8,128)(2,1)S(1)}, u32[]{:S(2)}, u32[]{:S(2)}) collective-permute-start(bf16[4,16,512]{2,1,0:T(8,128)(2,1)S(1)} %copy-done.17), channel_id=1, source_target_pairs={{0,32},{32,64},{64,96},{96,0},{1,33},{33,65},{65,97},{97,1},{2,34}... | collective-permute-start | bytes 196616 | tf_op jit(solution)/shard_map/ppermute | solution.py:29
  31.7 8.2 %collective-permute-start.1 = (bf16[4,16,512]{2,1,0:T(8,128)(2,1)S(1)}, bf16[4,16,512]{2,1,0:T(8,128)(2,1)S(1)}, u32[]{:S(2)}, u32[]{:S(2)}) collective-permute-start(bf16[4,16,512]{2,1,0:T(8,128)(2,1)S(1)} %copy-done.16), channel_id=1, source_target_pairs={{0,64},{32,96},{64,0},{96,32},{1,65},{33,97},{65,1},{97,33},{2,66}... | collective-permute-start | bytes 196616 | tf_op jit(solution)/shard_map/ppermute | solution.py:29
  33.7 7.7 %collective-permute-start.2 = (bf16[4,16,512]{2,1,0:T(8,128)(2,1)S(1)}, bf16[4,16,512]{2,1,0:T(8,128)(2,1)S(1)}, u32[]{:S(2)}, u32[]{:S(2)}) collective-permute-start(bf16[4,16,512]{2,1,0:T(8,128)(2,1)S(1)} %copy-done.15), channel_id=1, source_target_pairs={{0,96},{32,0},{64,32},{96,64},{1,97},{33,1},{65,33},{97,65},{2,98}... | collective-permute-start | bytes 196616 | tf_op jit(solution)/shard_map/ppermute | solution.py:29
  35.2 142.4 %copy-start.5 = (s32[4,2,17]{2,1,0:T(2,128)}, s32[4,2,17]{2,1,0:T(2,128)S(1)}, u32[]{:S(2)}) copy-start(s32[4,2,17]{2,1,0:T(2,128)S(1)} %fusion.7.table) | copy-start | bytes 1636
  42.9 22.3 %all-to-all-start.1 = ((bf16[32,2,16,128]{3,2,1,0:T(8,128)(2,1)}), bf16[32,2,16,128]{3,2,1,0:T(8,128)(2,1)S(1)}, u32[]{:S(2)}, u32[]{:S(2)}) async-start(bf16[32,2,16,128]{3,2,1,0:T(8,128)(2,1)} %leaf_spread.1), calls=%async_computation.1 | async-start | bytes 524288 | tf_op jit(solution)/shard_map/all_to_all | solution.py:41
  66.0 15.5 %all-to-all-start.2 = ((bf16[32,2,16,128]{3,2,1,0:T(8,128)(2,1)}), bf16[32,2,16,128]{3,2,1,0:T(8,128)(2,1)S(1)}, u32[]{:S(2)}, u32[]{:S(2)}) async-start(bf16[32,2,16,128]{3,2,1,0:T(8,128)(2,1)} %broadcast_in_dim.26), calls=%async_computation.2 | async-start | bytes 524288 | tf_op jit(solution)/shard_map/all_to_all | solution.py:41
  70.5 7.7 %collective-permute-start.3 = (bf16[8,16,512]{2,1,0:T(8,128)(2,1)S(1)}, bf16[8,16,512]{2,1,0:T(8,128)(2,1)S(1)}, u32[]{:S(2)}, u32[]{:S(2)}) collective-permute-start(bf16[8,16,512]{2,1,0:T(8,128)(2,1)S(1)} %copy-done.14), channel_id=1, source_target_pairs={{0,32},{32,64},{64,96},{96,0},{1,33},{33,65},{65,97},{97,1},{2,34}... | collective-permute-start | bytes 393224 | tf_op jit(solution)/shard_map/ppermute | solution.py:29
  70.6 7.6 %collective-permute-start.4 = (bf16[8,16,512]{2,1,0:T(8,128)(2,1)S(1)}, bf16[8,16,512]{2,1,0:T(8,128)(2,1)S(1)}, u32[]{:S(2)}, u32[]{:S(2)}) collective-permute-start(bf16[8,16,512]{2,1,0:T(8,128)(2,1)S(1)} %copy-done.13), channel_id=1, source_target_pairs={{0,64},{32,96},{64,0},{96,32},{1,65},{33,97},{65,1},{97,33},{2,66}... | collective-permute-start | bytes 393224 | tf_op jit(solution)/shard_map/ppermute | solution.py:29
  72.7 6.4 %collective-permute-start.5 = (bf16[8,16,512]{2,1,0:T(8,128)(2,1)S(1)}, bf16[8,16,512]{2,1,0:T(8,128)(2,1)S(1)}, u32[]{:S(2)}, u32[]{:S(2)}) collective-permute-start(bf16[8,16,512]{2,1,0:T(8,128)(2,1)S(1)} %copy-done.12), channel_id=1, source_target_pairs={{0,96},{32,0},{64,32},{96,64},{1,97},{33,1},{65,33},{97,65},{2,98}... | collective-permute-start | bytes 393224 | tf_op jit(solution)/shard_map/ppermute | solution.py:29
  81.5 2.4 copy-start.2
  85.5 16.5 %copy-start.8 = (f32[2,16,128]{2,1,0:T(8,128)}, f32[2,16,128]{2,1,0:T(8,128)S(1)}, u32[]{:S(2)}) copy-start(f32[2,16,128]{2,1,0:T(8,128)S(1)} %get-tuple-element.36.fwd) | copy-start | bytes 49156
  102.8 14.2 %all-to-all-start.4 = ((bf16[32,16,128]{2,1,0:T(8,128)(2,1)}), bf16[32,16,128]{2,1,0:T(8,128)(2,1)S(1)}, u32[]{:S(2)}, u32[]{:S(2)}) async-start(bf16[32,16,128]{2,1,0:T(8,128)(2,1)} %broadcast_in_dim.28), calls=%async_computation.4 | async-start | bytes 262144 | tf_op jit(solution)/shard_map/all_to_all | solution.py:41
  116.9 1.7 copy-start
  118.7 30.5 %copy-start.1 = (bf16[80,128,128]{2,1,0:T(8,128)(2,1)S(1)}, bf16[80,128,128]{2,1,0:T(8,128)(2,1)}, u32[]{:S(2)}) copy-start(bf16[80,128,128]{2,1,0:T(8,128)(2,1)} %all-gather.9.cloned.1.call-done) | copy-start | bytes 7864324
  133.6 1.3 collective-permute-start.6
  228.2 15.5 %all-to-all-start.12 = ((bf16[32,2,16,128]{3,2,1,0:T(8,128)(2,1)}), bf16[32,2,16,128]{3,2,1,0:T(8,128)(2,1)S(1)}, u32[]{:S(2)}, u32[]{:S(2)}) async-start(bf16[32,2,16,128]{3,2,1,0:T(8,128)(2,1)} %broadcast_in_dim.66), calls=%async_computation.12 | async-start | bytes 524288 | tf_op jit(solution)/shard_map/all_to_all | solution.py:41
  237.3 21.1 %copy-start.4 = (bf16[32,16,128]{2,1,0:T(8,128)(2,1)S(1)}, bf16[32,16,128]{2,1,0:T(8,128)(2,1)}, u32[]{:S(2)}) copy-start(bf16[32,16,128]{2,1,0:T(8,128)(2,1)} %copy-done.3) | copy-start | bytes 393220
  237.3 21.1 %copy-start.10 = (bf16[32,16,128]{2,1,0:T(8,128)(2,1)S(1)}, bf16[32,16,128]{2,1,0:T(8,128)(2,1)}, u32[]{:S(2)}) copy-start(bf16[32,16,128]{2,1,0:T(8,128)(2,1)} %all_to_all.81.top) | copy-start | bytes 393220
  250.8 23.5 %all-to-all-start.13 = ((bf16[128,16,128]{2,1,0:T(8,128)(2,1)}), bf16[128,16,128]{2,1,0:T(8,128)(2,1)S(1)}, u32[]{:S(2)}, u32[]{:S(2)}) async-start(bf16[128,16,128]{2,1,0:T(8,128)(2,1)} %bitcast.60), calls=%async_computation.13 | async-start | bytes 1048576 | tf_op jit(solution)/shard_map/all_to_all | solution.py:532
  259.5 14.9 %collective-permute-start.7 = (bf16[8,4,16,128]{3,2,1,0:T(8,128)(2,1)S(1)}, bf16[8,4,16,128]{3,2,1,0:T(8,128)(2,1)S(1)}, u32[]{:S(2)}, u32[]{:S(2)}) collective-permute-start(bf16[8,4,16,128]{3,2,1,0:T(8,128)(2,1)S(1)} %get-tuple-element.42), channel_id=1, source_target_pairs={{0,32},{32,64},{64,96},{96,0},{1,33},{33,65},{65,97},{97,1},{2,34}... | collective-permute-start | bytes 393224 | tf_op jit(solution)/shard_map/ppermute | solution.py:29
  261.1 13.2 %collective-permute-start.8 = (bf16[8,4,16,128]{3,2,1,0:T(8,128)(2,1)S(1)}, bf16[8,4,16,128]{3,2,1,0:T(8,128)(2,1)S(1)}, u32[]{:S(2)}, u32[]{:S(2)}) collective-permute-start(bf16[8,4,16,128]{3,2,1,0:T(8,128)(2,1)S(1)} %get-tuple-element.41), channel_id=1, source_target_pairs={{0,64},{32,96},{64,0},{96,32},{1,65},{33,97},{65,1},{97,33},{2,66}... | collective-permute-start | bytes 393224 | tf_op jit(solution)/shard_map/ppermute | solution.py:29
  264.3 10.1 %collective-permute-start.9 = (bf16[8,4,16,128]{3,2,1,0:T(8,128)(2,1)S(1)}, bf16[8,4,16,128]{3,2,1,0:T(8,128)(2,1)S(1)}, u32[]{:S(2)}, u32[]{:S(2)}) collective-permute-start(bf16[8,4,16,128]{3,2,1,0:T(8,128)(2,1)S(1)} %get-tuple-element.40), channel_id=1, source_target_pairs={{0,96},{32,0},{64,32},{96,64},{1,97},{33,1},{65,33},{97,65},{2,98}... | collective-permute-start | bytes 393224 | tf_op jit(solution)/shard_map/ppermute | solution.py:29
  (5 other events, 5.1 us)
Sparse Core Ops, SparseCore 0:
  11.5 56.1 all-gather.6
  69.5 38.0 all-gather.8
  109.5 103.5 all-gather.10

commit v7 on v6

--- a/solution.py
+++ b/solution.py
@@ -496,16 +496,18 @@
         block_lists.T,
     )
     middle_weights = gather_rows(middle_weights)
-    top_weights = gather_rows(top_weights)
 
     got = lax.all_to_all(sent, "prow", 0, 0, tiled=True)
     fwd_leaf, crit, other, leaf_weights = leaf_update(x, got, inverse_sub, factor_blocks)
-    leaf_weights = gather_rows(leaf_weights)
     crit = [crit[0]] + [shift(crit[d], d) for d in range(1, NX)]
     other = [other[0]] + [shift(other[d], d) for d in range(1, NX)]
     table = got[:, 24, 0:2, 0:17].astype(jnp.int32)
     right = lax.dynamic_index_in_dim(got, column // 8, 0, keepdims=False)
     right = right[16:20].astype(F32) + right[20:24].astype(F32)
+    crit[0], right = lax.optimization_barrier((crit[0], right))
+    top_weights, leaf_weights, right = lax.optimization_barrier((top_weights, leaf_weights, right))
+    top_weights = gather_rows(top_weights)
+    leaf_weights = gather_rows(leaf_weights)
     parts = leaf_spread(x, table, crit)
 
     values = gather_columns(right[1:3] - reduce_columns(parts))

time: 302 us -> 301 us (level)
  blocking collectives: 134 us -> 156 us
  starting transfers between devices: 49.6 us -> 38.2 us
  waiting for transfers between devices: 59 us -> 48.9 us
    all_to_all x9 -> x10, blocking collectives: 134 us -> 156 us  [exchange(): return lax.all_to_all(value, 'pcol', 0, 0, tiled=True)]
    all_to_all x4 -> x3, starting transfers between devices: 24.7 us -> 13.4 us  [exchange(): return lax.all_to_all(value, 'pcol', 0, 0, tiled=True)]
    all_to_all x4 -> x3, waiting for transfers between devices: 28.4 us -> 17.4 us  [exchange(): return lax.all_to_all(value, 'pcol', 0, 0, tiled=True)]
  transfers between devices with their start and end apart: 19 -> 18, of which waited for: 13 -> 12; matrix products, arithmetic and copies ran while one was open for 2% -> 2% of each run, Pallas kernels for 7% -> 7%
where the time goes in v7:
time: 301 us; the launch traced here: 300 us
  blocking collectives  156 us (52%)
  waiting for transfers between devices  48.9 us (16%)
  starting transfers between devices  38.2 us (13%)
  Pallas kernels  31.7 us (11%)
  between operations  14.1 us (5%)
  local copies, waits for them, and re-layouts  8.12 us (3%)
    all_to_all x10, blocking collectives, exchange(): return lax.all_to_all(value, 'pcol', 0, 0, tiled=True)  156 us
    all_to_all x3, waiting for transfers between devices, exchange(): return lax.all_to_all(value, 'pcol', 0, 0, tiled=True)  17.4 us
    all_to_all x3, starting transfers between devices, exchange(): return lax.all_to_all(value, 'pcol', 0, 0, tiled=True)  13.4 us
    ppermute x9, starting transfers between devices, shift(): lax.ppermute(value, 'prow', [(i, (i + distance) % NX) for i in range(NX)])  12.8 us
    ppermute x9, waiting for transfers between devices, shift(): lax.ppermute(value, 'prow', [(i, (i + distance) % NX) for i in range(NX)])  11.3 us
    all_to_all x1, waiting for transfers between devices, per_device(): lax.all_to_all(parts.reshape(NX * NP, RX, 128), ('prow', 'pcol'), 0, 0, t...  8.81 us
    all_to_all x1, waiting for transfers between devices, per_device(): got = lax.all_to_all(sent, 'prow', 0, 0, tiled=True)  8.25 us
    all_to_all x1, starting transfers between devices, per_device(): lax.all_to_all(parts.reshape(NX * NP, RX, 128), ('prow', 'pcol'), 0, 0, t...  7.56 us
  transfers between devices with their start and end apart: 18, of which 12 were waited for; matrix products, arithmetic and copies ran while one was open for 2% of the time, Pallas kernels for 7%

profile of v7, /device:TPU:32, one launch (start us, length us, event | category | flops | bytes accessed | tf_op | source)
XLA Modules:
  0.0 300.1 jit_solution(14357344000938703204)
XLA Ops:
  7.2 4.1 %start.1 = (bf16[4,25,16,128]{3,2,1,0:T(8,128)(2,1)}, bf16[2,16,128,128]{3,2,1,0:T(8,128)(2,1)}, bf16[20,128,128]{2,1,0:T(8,128)(2,1)}) custom-call(s32[1]{0:T(128)} %bitcast.1.place, f32[7,64,1024]{2,1,0:T(8,128)} %right_sub.1, f32[64,1024]{1,0:T(8,128)} %right_root.1, bf16[7,8,128,128]{3,2,1,0:T(8,128)(2,1)} %bitcast.45, bf16[8,128,128]{2,1,0:T(8,128)(2,1)} %bitcast.49, ...), custom_call_target="tpu_custom_call" | custom-call | tf_op jit(solution)/shard_map/start/pallas_call | solution.py:119
  11.3 4.3 %all-to-all-start = ((bf16[4,25,16,128]{3,2,1,0:T(8,128)(2,1)}), bf16[4,25,16,128]{3,2,1,0:T(8,128)(2,1)S(1)}, u32[]{:S(2)}, u32[]{:S(2)}) async-start(bf16[4,25,16,128]{3,2,1,0:T(8,128)(2,1)} %get-tuple-element.27), calls=%async_computation | async-start | bytes 819200 | tf_op jit(solution)/shard_map/all_to_all | solution.py:500
  15.6 8.2 %all-to-all-done.got = bf16[4,25,16,128]{3,2,1,0:T(8,128)(2,1)S(1)} async-done(((bf16[4,25,16,128]{3,2,1,0:T(8,128)(2,1)}), bf16[4,25,16,128]{3,2,1,0:T(8,128)(2,1)S(1)}, u32[]{:S(2)}, u32[]{:S(2)}) %all-to-all-start) | async-done | bytes 409632 | tf_op jit(solution)/shard_map/all_to_all | solution.py:500
  24.6 4.9 %leaf_update.1 = (f32[4,16,128]{2,1,0:T(8,128)}, bf16[4,16,512]{2,1,0:T(8,128)(2,1)}, bf16[4,16,512]{2,1,0:T(8,128)(2,1)}, bf16[4,16,512]{2,1,0:T(8,128)(2,1)}, ...) custom-call(s32[1]{0:T(128)} %bitcast.x_ref, ...), custom_call_target="tpu_custom_call" | custom-call | tf_op jit(solution)/shard_map/leaf_update/pallas_call | solution.py:166
  31.8 2.1 collective-permute-start.1
  35.3 3.4 %collective-permute-done.c1 = bf16[4,16,512]{2,1,0:T(8,128)(2,1)S(1)} collective-permute-done((bf16[4,16,512]{2,1,0:T(8,128)(2,1)S(1)}, bf16[4,16,512]{2,1,0:T(8,128)(2,1)S(1)}, u32[]{:S(2)}, u32[]{:S(2)}) %collective-permute-start) | collective-permute-done | bytes 65568 | tf_op jit(solution)/shard_map/ppermute | solution.py:29
  42.3 22.2 %all_to_all.75 = bf16[32,2,16,128]{3,2,1,0:T(8,128)(2,1)S(1)} all-to-all(bf16[32,2,16,128]{3,2,1,0:T(8,128)(2,1)S(1)} %leaf_spread.1), channel_id=1, replica_groups=mesh['layer'=2,'prow'=4,'pcol'=32] {'pcol'}, dimensions={0} | all-to-all | bytes 524288 | tf_op jit(solution)/shard_map/all_to_all | solution.py:41
  65.3 4.5 %all-to-all-start.2 = ((bf16[32,2,16,128]{3,2,1,0:T(8,128)(2,1)}), bf16[32,2,16,128]{3,2,1,0:T(8,128)(2,1)S(1)}, u32[]{:S(2)}, u32[]{:S(2)}) async-start(bf16[32,2,16,128]{3,2,1,0:T(8,128)(2,1)} %broadcast_in_dim.26), calls=%async_computation.2 | async-start | bytes 524288 | tf_op jit(solution)/shard_map/all_to_all | solution.py:41
  69.9 2.1 collective-permute-start.4
  73.2 4.2 %collective-permute-done.3.o1 = bf16[8,16,512]{2,1,0:T(8,128)(2,1)S(1)} collective-permute-done((bf16[8,16,512]{2,1,0:T(8,128)(2,1)S(1)}, bf16[8,16,512]{2,1,0:T(8,128)(2,1)S(1)}, u32[]{:S(2)}, u32[]{:S(2)}) %collective-permute-start.3) | collective-permute-done | bytes 131104 | tf_op jit(solution)/shard_map/ppermute | solution.py:29
  78.3 2.5 all-to-all-done.2.values
  80.8 2.5 copy-done.2
  84.9 16.5 %all_to_all.76 = bf16[32,16,128]{2,1,0:T(8,128)(2,1)S(1)} all-to-all(bf16[32,16,128]{2,1,0:T(8,128)(2,1)S(1)} %get-tuple-element.41), channel_id=1, replica_groups=mesh['layer'=2,'prow'=4,'pcol'=32] {'pcol'}, dimensions={0} | all-to-all | bytes 262144 | tf_op jit(solution)/shard_map/all_to_all | solution.py:41
  102.1 4.4 %all-to-all-start.4 = ((bf16[32,16,128]{2,1,0:T(8,128)(2,1)}), bf16[32,16,128]{2,1,0:T(8,128)(2,1)S(1)}, u32[]{:S(2)}, u32[]{:S(2)}) async-start(bf16[32,16,128]{2,1,0:T(8,128)(2,1)} %broadcast_in_dim.28), calls=%async_computation.4 | async-start | bytes 262144 | tf_op jit(solution)/shard_map/all_to_all | solution.py:41
  107.6 8.6 %all-to-all-done.4.values = bf16[32,16,128]{2,1,0:T(8,128)(2,1)S(1)} async-done(((bf16[32,16,128]{2,1,0:T(8,128)(2,1)}), bf16[32,16,128]{2,1,0:T(8,128)(2,1)S(1)}, u32[]{:S(2)}, u32[]{:S(2)}) %all-to-all-start.4) | async-done | bytes 131104 | tf_op jit(solution)/shard_map/all_to_all | solution.py:41
  116.2 1.7 copy-done
  119.0 13.9 %all_to_all.77 = bf16[32,16,128]{2,1,0:T(8,128)(2,1)S(1)} all-to-all(bf16[32,16,128]{2,1,0:T(8,128)(2,1)S(1)} %get-tuple-element.44), channel_id=1, replica_groups=mesh['layer'=2,'prow'=4,'pcol'=32] {'pcol'}, dimensions={0} | all-to-all | bytes 262144 | tf_op jit(solution)/shard_map/all_to_all | solution.py:41
  134.2 14.2 %all_to_all.78.values = bf16[32,16,128]{2,1,0:T(8,128)(2,1)S(1)} all-to-all(bf16[32,16,128]{2,1,0:T(8,128)(2,1)S(1)} %broadcast_in_dim.29), channel_id=1, replica_groups=mesh['layer'=2,'prow'=4,'pcol'=32] {'pcol'}, dimensions={0} | all-to-all | bytes 262144 | tf_op jit(solution)/shard_map/all_to_all | solution.py:41
  149.1 13.9 %all_to_all.79 = bf16[32,16,128]{2,1,0:T(8,128)(2,1)S(1)} all-to-all(bf16[32,16,128]{2,1,0:T(8,128)(2,1)S(1)} %root_solve.1), channel_id=1, replica_groups=mesh['layer'=2,'prow'=4,'pcol'=32] {'pcol'}, dimensions={0} | all-to-all | bytes 262144 | tf_op jit(solution)/shard_map/all_to_all | solution.py:41
  163.1 13.8 %all_to_all.80.root = bf16[32,16,128]{2,1,0:T(8,128)(2,1)S(1)} all-to-all(bf16[32,16,128]{2,1,0:T(8,128)(2,1)S(1)} %broadcast_in_dim.30), channel_id=1, replica_groups=mesh['layer'=2,'prow'=4,'pcol'=32] {'pcol'}, dimensions={0} | all-to-all | bytes 262144 | tf_op jit(solution)/shard_map/all_to_all | solution.py:41
  178.3 14.0 %all_to_all.81 = bf16[32,16,128]{2,1,0:T(8,128)(2,1)S(1)} all-to-all(bf16[32,16,128]{2,1,0:T(8,128)(2,1)S(1)} %top_backward.1), channel_id=1, replica_groups=mesh['layer'=2,'prow'=4,'pcol'=32] {'pcol'}, dimensions={0} | all-to-all | bytes 262144 | tf_op jit(solution)/shard_map/all_to_all | solution.py:41
  192.4 14.0 %all_to_all.82.top = bf16[32,16,128]{2,1,0:T(8,128)(2,1)} all-to-all(bf16[32,16,128]{2,1,0:T(8,128)(2,1)S(1)} %broadcast_in_dim.64), channel_id=1, replica_groups=mesh['layer'=2,'prow'=4,'pcol'=32] {'pcol'}, dimensions={0} | all-to-all | bytes 262144 | tf_op jit(solution)/shard_map/all_to_all | solution.py:41
  206.4 4.9 %middle_backward.1 = bf16[32,2,16,128]{3,2,1,0:T(8,128)(2,1)} custom-call(s32[1]{0:T(128)} %bitcast.x_ref, s32[4,2,17]{2,1,0:T(2,128)} %copy-done.5, bf16[32,16,128]{2,1,0:T(8,128)(2,1)} %copy-done.3, bf16[32,16,128]{2,1,0:T(8,128)(2,1)} %all_to_all.82.top, f32[2,16,128]{2,1,0:T(8,128)} %copy-done.8, bf16[4,2,16,128,128]{4,3,2,1,0:T(8,128)(2,1)} %bitcast.39), custom_call_target="tpu_custom_call" | custom-call | tf_op jit(solution)/shard_map/middle_backward/pallas_call | solution.py:392
  211.3 15.4 %all_to_all.83 = bf16[32,2,16,128]{3,2,1,0:T(8,128)(2,1)S(1)} all-to-all(bf16[32,2,16,128]{3,2,1,0:T(8,128)(2,1)} %middle_backward.1), channel_id=1, replica_groups=mesh['layer'=2,'prow'=4,'pcol'=32] {'pcol'}, dimensions={0} | all-to-all | bytes 524288 | tf_op jit(solution)/shard_map/all_to_all | solution.py:41
  227.5 4.5 %all-to-all-start.12 = ((bf16[32,2,16,128]{3,2,1,0:T(8,128)(2,1)}), bf16[32,2,16,128]{3,2,1,0:T(8,128)(2,1)S(1)}, u32[]{:S(2)}, u32[]{:S(2)}) async-start(bf16[32,2,16,128]{3,2,1,0:T(8,128)(2,1)} %broadcast_in_dim.66), calls=%async_computation.12 | async-start | bytes 524288 | tf_op jit(solution)/shard_map/all_to_all | solution.py:41
  232.0 4.6 %leaf_down.1.fwd = f32[4,16,128]{2,1,0:T(8,128)} custom-call(s32[1]{0:T(128)} %bitcast.x_ref, s32[4,2,17]{2,1,0:T(2,128)} %copy-done.5, bf16[32,16,128]{2,1,0:T(8,128)(2,1)} %copy-done.3, bf16[32,16,128]{2,1,0:T(8,128)(2,1)} %all_to_all.82.top, f32[4,16,128]{2,1,0:T(8,128)} %get-tuple-element.47.fwd, bf16[4,4,20,128,128]{4,3,2,1,0:T(8,128)(2,1)} %bitcast.42, ...), custom_call_target="tpu_custom_call" | custom-call | tf_op jit(solution)/shard_map/leaf_down/pallas_call | solution.py:411
  236.6 6.4 %all-to-all-done.12.middle = bf16[32,2,16,128]{3,2,1,0:T(8,128)(2,1)S(1)} async-done(((bf16[32,2,16,128]{3,2,1,0:T(8,128)(2,1)}), bf16[32,2,16,128]{3,2,1,0:T(8,128)(2,1)S(1)}, u32[]{:S(2)}, u32[]{:S(2)}) %all-to-all-start.12) | async-done | bytes 262176 | tf_op jit(solution)/shard_map/all_to_all | solution.py:41
  243.7 6.3 %leaf_backward.1 = bf16[4,32,16,128]{3,2,1,0:T(8,128)(2,1)} custom-call(s32[1]{0:T(128)} %bitcast.x_ref, s32[4,2,17]{2,1,0:T(2,128)} %copy-done.5, bf16[32,2,16,128]{3,2,1,0:T(8,128)(2,1)} %copy-done.9, f32[4,16,128]{2,1,0:T(8,128)} %leaf_down.1.fwd, bf16[4,4,20,128,128]{4,3,2,1,0:T(8,128)(2,1)} %bitcast.44), custom_call_target="tpu_custom_call" | custom-call | tf_op jit(solution)/shard_map/leaf_backward/pallas_call | solution.py:437
  250.1 7.6 %all-to-all-start.13 = ((bf16[128,16,128]{2,1,0:T(8,128)(2,1)}), bf16[128,16,128]{2,1,0:T(8,128)(2,1)S(1)}, u32[]{:S(2)}, u32[]{:S(2)}) async-start(bf16[128,16,128]{2,1,0:T(8,128)(2,1)} %bitcast.48), calls=%async_computation.13 | async-start | bytes 1048576 | tf_op jit(solution)/shard_map/all_to_all | solution.py:534
  260.4 3.1 %collective-permute-start.8 = (bf16[8,4,16,128]{3,2,1,0:T(8,128)(2,1)S(1)}, bf16[8,4,16,128]{3,2,1,0:T(8,128)(2,1)S(1)}, u32[]{:S(2)}, u32[]{:S(2)}) collective-permute-start(bf16[8,4,16,128]{3,2,1,0:T(8,128)(2,1)S(1)} %get-tuple-element.51), channel_id=1, source_target_pairs={{0,64},{32,96},{64,0},{96,32},{1,65},{33,97},{65,1},{97,33},{2,66}... | collective-permute-start | bytes 393224 | tf_op jit(solution)/shard_map/ppermute | solution.py:29
  264.7 8.8 %all-to-all-done.13 = bf16[128,16,128]{2,1,0:T(8,128)(2,1)S(1)} async-done(((bf16[128,16,128]{2,1,0:T(8,128)(2,1)}), bf16[128,16,128]{2,1,0:T(8,128)(2,1)S(1)}, u32[]{:S(2)}, u32[]{:S(2)}) %all-to-all-start.13) | async-done | bytes 524320 | tf_op jit(solution)/shard_map/all_to_all | solution.py:534
  273.8 18.3 %all_to_all.84.leaves = bf16[32,4,16,128]{3,2,1,0:T(8,128)(2,1)S(1)} all-to-all(bf16[32,4,16,128]{3,2,1,0:T(8,128)(2,1)S(1)} %broadcast_in_dim.67), channel_id=1, replica_groups=mesh['layer'=2,'prow'=4,'pcol'=32] {'pcol'}, dimensions={0} | all-to-all | bytes 1048576 | tf_op jit(solution)/shard_map/all_to_all | solution.py:41
  (85 shorter events, 26.2 us)
Async XLA Ops:
  7.2 73.7 %all-gather.7.cloned.1.call-start = ((), (), s32[]{:S(2)}) async-start(), calls=%async_computation.15 | async-start | bytes 5242880 | tf_op jit(solution)/shard_map/all_gather | solution.py:481
  11.3 12.6 %all-to-all-start = ((bf16[4,25,16,128]{3,2,1,0:T(8,128)(2,1)}), bf16[4,25,16,128]{3,2,1,0:T(8,128)(2,1)S(1)}, u32[]{:S(2)}, u32[]{:S(2)}) async-start(bf16[4,25,16,128]{3,2,1,0:T(8,128)(2,1)} %get-tuple-element.27), calls=%async_computation | async-start | bytes 819200 | tf_op jit(solution)/shard_map/all_to_all | solution.py:500
  15.6 92.0 %all-gather.9.cloned.1.call-start = ((), (), s32[]{:S(2)}) async-start(), calls=%async_computation.16 | async-start | bytes 3276800 | tf_op jit(solution)/shard_map/all_gather | solution.py:481
  29.5 2.2 copy-start.16
  29.5 4.3 %copy-start.15 = (bf16[4,16,512]{2,1,0:T(8,128)(2,1)S(1)}, bf16[4,16,512]{2,1,0:T(8,128)(2,1)}, u32[]{:S(2)}) copy-start(bf16[4,16,512]{2,1,0:T(8,128)(2,1)} %get-tuple-element.35) | copy-start | bytes 196612
  29.6 11.9 %copy-start.7 = (bf16[4,16,512]{2,1,0:T(8,128)(2,1)S(1)}, bf16[4,16,512]{2,1,0:T(8,128)(2,1)}, u32[]{:S(2)}) copy-start(bf16[4,16,512]{2,1,0:T(8,128)(2,1)} %get-tuple-element.32.c0) | copy-start | bytes 196612
  30.4 39.4 %copy-start.14 = (bf16[8,16,512]{2,1,0:T(8,128)(2,1)S(1)}, bf16[8,16,512]{2,1,0:T(8,128)(2,1)}, u32[]{:S(2)}) copy-start(bf16[8,16,512]{2,1,0:T(8,128)(2,1)} %get-tuple-element.38) | copy-start | bytes 393220
  30.4 39.5 %copy-start.13 = (bf16[8,16,512]{2,1,0:T(8,128)(2,1)S(1)}, bf16[8,16,512]{2,1,0:T(8,128)(2,1)}, u32[]{:S(2)}) copy-start(bf16[8,16,512]{2,1,0:T(8,128)(2,1)} %get-tuple-element.39) | copy-start | bytes 393220
  30.4 41.6 %copy-start.12 = (bf16[8,16,512]{2,1,0:T(8,128)(2,1)S(1)}, bf16[8,16,512]{2,1,0:T(8,128)(2,1)}, u32[]{:S(2)}) copy-start(bf16[8,16,512]{2,1,0:T(8,128)(2,1)} %get-tuple-element.40) | copy-start | bytes 393220
  30.4 50.4 %copy-start.6 = (bf16[8,16,512]{2,1,0:T(8,128)(2,1)S(1)}, bf16[8,16,512]{2,1,0:T(8,128)(2,1)}, u32[]{:S(2)}) copy-start(bf16[8,16,512]{2,1,0:T(8,128)(2,1)} %get-tuple-element.37.o0) | copy-start | bytes 393220
  30.4 201.6 %all-gather.11.cloned.1.call-start = ((), (), s32[]{:S(2)}) async-start(), calls=%async_computation.17 | async-start | bytes 13107200 | tf_op jit(solution)/shard_map/all_gather | solution.py:481
  31.2 7.5 %collective-permute-start = (bf16[4,16,512]{2,1,0:T(8,128)(2,1)S(1)}, bf16[4,16,512]{2,1,0:T(8,128)(2,1)S(1)}, u32[]{:S(2)}, u32[]{:S(2)}) collective-permute-start(bf16[4,16,512]{2,1,0:T(8,128)(2,1)S(1)} %copy-done.17), channel_id=1, source_target_pairs={{0,32},{32,64},{64,96},{96,0},{1,33},{33,65},{65,97},{97,1},{2,34}... | collective-permute-start | bytes 196616 | tf_op jit(solution)/shard_map/ppermute | solution.py:29
  31.8 8.2 %collective-permute-start.1 = (bf16[4,16,512]{2,1,0:T(8,128)(2,1)S(1)}, bf16[4,16,512]{2,1,0:T(8,128)(2,1)S(1)}, u32[]{:S(2)}, u32[]{:S(2)}) collective-permute-start(bf16[4,16,512]{2,1,0:T(8,128)(2,1)S(1)} %copy-done.16), channel_id=1, source_target_pairs={{0,64},{32,96},{64,0},{96,32},{1,65},{33,97},{65,1},{97,33},{2,66}... | collective-permute-start | bytes 196616 | tf_op jit(solution)/shard_map/ppermute | solution.py:29
  33.8 7.6 %collective-permute-start.2 = (bf16[4,16,512]{2,1,0:T(8,128)(2,1)S(1)}, bf16[4,16,512]{2,1,0:T(8,128)(2,1)S(1)}, u32[]{:S(2)}, u32[]{:S(2)}) collective-permute-start(bf16[4,16,512]{2,1,0:T(8,128)(2,1)S(1)} %copy-done.15), channel_id=1, source_target_pairs={{0,96},{32,0},{64,32},{96,64},{1,97},{33,1},{65,33},{97,65},{2,98}... | collective-permute-start | bytes 196616 | tf_op jit(solution)/shard_map/ppermute | solution.py:29
  35.3 141.6 %copy-start.5 = (s32[4,2,17]{2,1,0:T(2,128)}, s32[4,2,17]{2,1,0:T(2,128)S(1)}, u32[]{:S(2)}) copy-start(s32[4,2,17]{2,1,0:T(2,128)S(1)} %fusion.3.table) | copy-start | bytes 1636
  65.3 15.5 %all-to-all-start.2 = ((bf16[32,2,16,128]{3,2,1,0:T(8,128)(2,1)}), bf16[32,2,16,128]{3,2,1,0:T(8,128)(2,1)S(1)}, u32[]{:S(2)}, u32[]{:S(2)}) async-start(bf16[32,2,16,128]{3,2,1,0:T(8,128)(2,1)} %broadcast_in_dim.26), calls=%async_computation.2 | async-start | bytes 524288 | tf_op jit(solution)/shard_map/all_to_all | solution.py:41
  69.8 7.7 %collective-permute-start.3 = (bf16[8,16,512]{2,1,0:T(8,128)(2,1)S(1)}, bf16[8,16,512]{2,1,0:T(8,128)(2,1)S(1)}, u32[]{:S(2)}, u32[]{:S(2)}) collective-permute-start(bf16[8,16,512]{2,1,0:T(8,128)(2,1)S(1)} %copy-done.14), channel_id=1, source_target_pairs={{0,32},{32,64},{64,96},{96,0},{1,33},{33,65},{65,97},{97,1},{2,34}... | collective-permute-start | bytes 393224 | tf_op jit(solution)/shard_map/ppermute | solution.py:29
  69.9 7.6 %collective-permute-start.4 = (bf16[8,16,512]{2,1,0:T(8,128)(2,1)S(1)}, bf16[8,16,512]{2,1,0:T(8,128)(2,1)S(1)}, u32[]{:S(2)}, u32[]{:S(2)}) collective-permute-start(bf16[8,16,512]{2,1,0:T(8,128)(2,1)S(1)} %copy-done.13), channel_id=1, source_target_pairs={{0,64},{32,96},{64,0},{96,32},{1,65},{33,97},{65,1},{97,33},{2,66}... | collective-permute-start | bytes 393224 | tf_op jit(solution)/shard_map/ppermute | solution.py:29
  72.0 6.4 %collective-permute-start.5 = (bf16[8,16,512]{2,1,0:T(8,128)(2,1)S(1)}, bf16[8,16,512]{2,1,0:T(8,128)(2,1)S(1)}, u32[]{:S(2)}, u32[]{:S(2)}) collective-permute-start(bf16[8,16,512]{2,1,0:T(8,128)(2,1)S(1)} %copy-done.12), channel_id=1, source_target_pairs={{0,96},{32,0},{64,32},{96,64},{1,97},{33,1},{65,33},{97,65},{2,98}... | collective-permute-start | bytes 393224 | tf_op jit(solution)/shard_map/ppermute | solution.py:29
  80.8 2.5 copy-start.2
  84.9 16.5 %copy-start.8 = (f32[2,16,128]{2,1,0:T(8,128)}, f32[2,16,128]{2,1,0:T(8,128)S(1)}, u32[]{:S(2)}) copy-start(f32[2,16,128]{2,1,0:T(8,128)S(1)} %get-tuple-element.46.fwd) | copy-start | bytes 49156
  102.1 14.2 %all-to-all-start.4 = ((bf16[32,16,128]{2,1,0:T(8,128)(2,1)}), bf16[32,16,128]{2,1,0:T(8,128)(2,1)S(1)}, u32[]{:S(2)}, u32[]{:S(2)}) async-start(bf16[32,16,128]{2,1,0:T(8,128)(2,1)} %broadcast_in_dim.28), calls=%async_computation.4 | async-start | bytes 262144 | tf_op jit(solution)/shard_map/all_to_all | solution.py:41
  116.2 1.7 copy-start
  118.0 30.5 %copy-start.1 = (bf16[80,128,128]{2,1,0:T(8,128)(2,1)S(1)}, bf16[80,128,128]{2,1,0:T(8,128)(2,1)}, u32[]{:S(2)}) copy-start(bf16[80,128,128]{2,1,0:T(8,128)(2,1)} %all-gather.9.cloned.1.call-done) | copy-start | bytes 7864324
  132.9 1.3 collective-permute-start.6
  227.5 15.5 %all-to-all-start.12 = ((bf16[32,2,16,128]{3,2,1,0:T(8,128)(2,1)}), bf16[32,2,16,128]{3,2,1,0:T(8,128)(2,1)S(1)}, u32[]{:S(2)}, u32[]{:S(2)}) async-start(bf16[32,2,16,128]{3,2,1,0:T(8,128)(2,1)} %broadcast_in_dim.66), calls=%async_computation.12 | async-start | bytes 524288 | tf_op jit(solution)/shard_map/all_to_all | solution.py:41
  236.6 21.0 %copy-start.4 = (bf16[32,16,128]{2,1,0:T(8,128)(2,1)S(1)}, bf16[32,16,128]{2,1,0:T(8,128)(2,1)}, u32[]{:S(2)}) copy-start(bf16[32,16,128]{2,1,0:T(8,128)(2,1)} %copy-done.3) | copy-start | bytes 393220
  236.6 21.1 %copy-start.10 = (bf16[32,16,128]{2,1,0:T(8,128)(2,1)S(1)}, bf16[32,16,128]{2,1,0:T(8,128)(2,1)}, u32[]{:S(2)}) copy-start(bf16[32,16,128]{2,1,0:T(8,128)(2,1)} %all_to_all.82.top) | copy-start | bytes 393220
  250.1 23.5 %all-to-all-start.13 = ((bf16[128,16,128]{2,1,0:T(8,128)(2,1)}), bf16[128,16,128]{2,1,0:T(8,128)(2,1)S(1)}, u32[]{:S(2)}, u32[]{:S(2)}) async-start(bf16[128,16,128]{2,1,0:T(8,128)(2,1)} %bitcast.48), calls=%async_computation.13 | async-start | bytes 1048576 | tf_op jit(solution)/shard_map/all_to_all | solution.py:534
  258.7 14.9 %collective-permute-start.7 = (bf16[8,4,16,128]{3,2,1,0:T(8,128)(2,1)S(1)}, bf16[8,4,16,128]{3,2,1,0:T(8,128)(2,1)S(1)}, u32[]{:S(2)}, u32[]{:S(2)}) collective-permute-start(bf16[8,4,16,128]{3,2,1,0:T(8,128)(2,1)S(1)} %get-tuple-element.52), channel_id=1, source_target_pairs={{0,32},{32,64},{64,96},{96,0},{1,33},{33,65},{65,97},{97,1},{2,34}... | collective-permute-start | bytes 393224 | tf_op jit(solution)/shard_map/ppermute | solution.py:29
  260.4 13.2 %collective-permute-start.8 = (bf16[8,4,16,128]{3,2,1,0:T(8,128)(2,1)S(1)}, bf16[8,4,16,128]{3,2,1,0:T(8,128)(2,1)S(1)}, u32[]{:S(2)}, u32[]{:S(2)}) collective-permute-start(bf16[8,4,16,128]{3,2,1,0:T(8,128)(2,1)S(1)} %get-tuple-element.51), channel_id=1, source_target_pairs={{0,64},{32,96},{64,0},{96,32},{1,65},{33,97},{65,1},{97,33},{2,66}... | collective-permute-start | bytes 393224 | tf_op jit(solution)/shard_map/ppermute | solution.py:29
  263.5 10.1 %collective-permute-start.9 = (bf16[8,4,16,128]{3,2,1,0:T(8,128)(2,1)S(1)}, bf16[8,4,16,128]{3,2,1,0:T(8,128)(2,1)S(1)}, u32[]{:S(2)}, u32[]{:S(2)}) collective-permute-start(bf16[8,4,16,128]{3,2,1,0:T(8,128)(2,1)S(1)} %get-tuple-element.50), channel_id=1, source_target_pairs={{0,96},{32,0},{64,32},{96,64},{1,97},{33,1},{65,33},{97,65},{2,98}... | collective-permute-start | bytes 393224 | tf_op jit(solution)/shard_map/ppermute | solution.py:29
  (4 other events, 4.6 us)
Sparse Core Ops, SparseCore 0:
  11.5 56.1 all-gather.6
  69.5 38.0 all-gather.8
  109.5 103.5 all-gather.10

commit v8 on v7

--- a/solution.py
+++ b/solution.py
@@ -450,31 +450,33 @@
     )(x, table, middle, fwd, weights)
 
 
-def finish_kernel(x_ref, e0, e1, e2, e3, leaves, out_sub, out_root):
+def finish_kernel(x_ref, *refs):
+    upper, middle, (leaves, out_sub, out_root) = refs[0:4], refs[4:8], refs[8:]
     x = x_ref[0]
-    for d, early in enumerate((e0, e1, e2, e3)):
+    for d in range(NX):
         rows = pl.ds(pl.multiple_of(RX * source(x, d), RX), RX)
         for k in range(8):
             columns = slice(128 * k, 128 * (k + 1))
-            out_root[rows, columns] = early[k, 0].astype(F32)
-            for t in range(3):
-                out_sub[t, rows, columns] = early[k, 1 + t].astype(F32)
+            out_root[rows, columns] = upper[d][k, 0].astype(F32)
+            out_sub[0, rows, columns] = upper[d][k, 1].astype(F32)
+            for t in range(2):
+                out_sub[1 + t, rows, columns] = middle[d][k, t].astype(F32)
             for t in range(4):
                 tile = leaves[8 * t + k, d].astype(F32)
                 out_sub[3 + t, RX * d : RX * (d + 1), columns] = tile
 
 
-def finish(x, early, leaves):
+def finish(x, upper, middle, leaves):
     return pl.pallas_call(
         finish_kernel,
         out_shape=[
             jax.ShapeDtypeStruct((7, 64, 1024), F32),
             jax.ShapeDtypeStruct((64, 1024), F32),
         ],
-        in_specs=[SMEM] + [pl.BlockSpec(memory_space=pltpu.VMEM)] * 5,
+        in_specs=[SMEM] + [VMEM] * 9,
         compiler_params=params(),
         name="finish",
-    )(x, *early, leaves)
+    )(x, *upper, *middle, leaves)
 
 
 def gather_rows(value):
@@ -524,19 +526,23 @@
     fwd_leaf = leaf_down(x, table, root, top, fwd_leaf, leaf_weights)
     middle = gather_columns(reduce_columns(parts))
 
-    early = jnp.concatenate([root[:, None], top[:, None], middle], 1)
-    pieces = []
-    for d in range(NX):
-        piece = lax.dynamic_slice_in_dim(early, 8 * lax.rem(position + d, NX), 8, 0)
-        pieces.append(shift(piece, d) if d else piece)
-
+    def own_columns(values):
+        found = []
+        for d in range(NX):
+            piece = lax.dynamic_slice_in_dim(values, 8 * lax.rem(position + d, NX), 8, 0)
+            found.append(shift(piece, d) if d else piece)
+        return found
+
+    upper = own_columns(jnp.stack([root, top], 1))
+    fwd_leaf, *upper = lax.optimization_barrier((fwd_leaf, *upper))
+    pieces = own_columns(middle)
     parts = leaf_backward(x, table, middle, fwd_leaf, leaf_weights)
     parts = lax.all_to_all(
         parts.reshape(NX * NP, RX, 128), ("prow", "pcol"), 0, 0, tiled=True
     ).reshape(NX, NP, RX, 128)
     chunk = jnp.sum(parts.astype(F32), axis=1).astype(BF)
     leaves = gather_columns(after(chunk, *pieces))
-    return tuple(finish(x, pieces, leaves))
+    return tuple(finish(x, upper, pieces, leaves))
 
 
 def solution(mesh):

time: 301 us -> 304 us (level)
  starting transfers between devices: 38.2 us -> 45 us
  waiting for transfers between devices: 48.9 us -> 44.9 us
    all_to_all x3, waiting for transfers between devices: 17.4 us -> 13.4 us  [exchange(): return lax.all_to_all(value, 'pcol', 0, 0, tiled=True)]
    ppermute x9 -> x12, starting transfers between devices: 12.8 us -> 16.8 us  [shift(): lax.ppermute(value, 'prow', [(i, (i + distance) % NX) for i in range(NX)])]
    ppermute x9 -> x12, waiting for transfers between devices: 11.3 us -> 11.3 us  [shift(): lax.ppermute(value, 'prow', [(i, (i + distance) % NX) for i in range(NX)])]
  transfers between devices with their start and end apart: 18 -> 21, of which waited for: 12 -> 12; matrix products, arithmetic and copies ran while one was open for 2% -> 2% of each run, Pallas kernels for 7% -> 7%
where the time goes in v8:
time: 304 us; the launch traced here: 302 us
  blocking collectives  156 us (51%)
  starting transfers between devices  45 us (15%)
  waiting for transfers between devices  44.9 us (15%)
  Pallas kernels  31.7 us (10%)
  between operations  14.1 us (5%)
  local copies, waits for them, and re-layouts  9.05 us (3%)
    all_to_all x10, blocking collectives, exchange(): return lax.all_to_all(value, 'pcol', 0, 0, tiled=True)  156 us
    ppermute x12, starting transfers between devices, shift(): lax.ppermute(value, 'prow', [(i, (i + distance) % NX) for i in range(NX)])  16.8 us
    all_to_all x3, waiting for transfers between devices, exchange(): return lax.all_to_all(value, 'pcol', 0, 0, tiled=True)  13.4 us
    all_to_all x3, starting transfers between devices, exchange(): return lax.all_to_all(value, 'pcol', 0, 0, tiled=True)  13.4 us
    ppermute x12, waiting for transfers between devices, shift(): lax.ppermute(value, 'prow', [(i, (i + distance) % NX) for i in range(NX)])  11.3 us
    all_to_all x1, starting transfers between devices, per_device(): lax.all_to_all(parts.reshape(NX * NP, RX, 128), ('prow', 'pcol'), 0, 0, t...  10.3 us
    all_to_all x1, waiting for transfers between devices, per_device(): lax.all_to_all(parts.reshape(NX * NP, RX, 128), ('prow', 'pcol'), 0, 0, t...  8.95 us
    all_to_all x1, waiting for transfers between devices, per_device(): got = lax.all_to_all(sent, 'prow', 0, 0, tiled=True)  8.25 us
  transfers between devices with their start and end apart: 21, of which 12 were waited for; matrix products, arithmetic and copies ran while one was open for 2% of the time, Pallas kernels for 7%

profile of v8, /device:TPU:32, one launch (start us, length us, event | category | flops | bytes accessed | tf_op | source)
XLA Modules:
  0.0 302.4 jit_solution(3582281261927731968)
XLA Ops:
  7.2 4.1 %start.1 = (bf16[4,25,16,128]{3,2,1,0:T(8,128)(2,1)}, bf16[2,16,128,128]{3,2,1,0:T(8,128)(2,1)}, bf16[20,128,128]{2,1,0:T(8,128)(2,1)}) custom-call(s32[1]{0:T(128)} %bitcast.1.place, f32[7,64,1024]{2,1,0:T(8,128)} %right_sub.1, f32[64,1024]{1,0:T(8,128)} %right_root.1, bf16[7,8,128,128]{3,2,1,0:T(8,128)(2,1)} %bitcast.45, bf16[8,128,128]{2,1,0:T(8,128)(2,1)} %bitcast.49, ...), custom_call_target="tpu_custom_call" | custom-call | tf_op jit(solution)/shard_map/start/pallas_call | solution.py:119
  11.4 4.3 %all-to-all-start = ((bf16[4,25,16,128]{3,2,1,0:T(8,128)(2,1)}), bf16[4,25,16,128]{3,2,1,0:T(8,128)(2,1)S(1)}, u32[]{:S(2)}, u32[]{:S(2)}) async-start(bf16[4,25,16,128]{3,2,1,0:T(8,128)(2,1)} %get-tuple-element.31), calls=%async_computation | async-start | bytes 819200 | tf_op jit(solution)/shard_map/all_to_all | solution.py:502
  15.7 8.2 %all-to-all-done.got = bf16[4,25,16,128]{3,2,1,0:T(8,128)(2,1)S(1)} async-done(((bf16[4,25,16,128]{3,2,1,0:T(8,128)(2,1)}), bf16[4,25,16,128]{3,2,1,0:T(8,128)(2,1)S(1)}, u32[]{:S(2)}, u32[]{:S(2)}) %all-to-all-start) | async-done | bytes 409632 | tf_op jit(solution)/shard_map/all_to_all | solution.py:502
  24.7 4.9 %leaf_update.1 = (f32[4,16,128]{2,1,0:T(8,128)}, bf16[4,16,512]{2,1,0:T(8,128)(2,1)}, bf16[4,16,512]{2,1,0:T(8,128)(2,1)}, bf16[4,16,512]{2,1,0:T(8,128)(2,1)}, ...) custom-call(s32[1]{0:T(128)} %bitcast.x_ref, ...), custom_call_target="tpu_custom_call" | custom-call | tf_op jit(solution)/shard_map/leaf_update/pallas_call | solution.py:166
  31.8 2.1 collective-permute-start.1
  35.3 3.4 %collective-permute-done.c1 = bf16[4,16,512]{2,1,0:T(8,128)(2,1)S(1)} collective-permute-done((bf16[4,16,512]{2,1,0:T(8,128)(2,1)S(1)}, bf16[4,16,512]{2,1,0:T(8,128)(2,1)S(1)}, u32[]{:S(2)}, u32[]{:S(2)}) %collective-permute-start) | collective-permute-done | bytes 65568 | tf_op jit(solution)/shard_map/ppermute | solution.py:29
  42.3 22.2 %all_to_all.75 = bf16[32,2,16,128]{3,2,1,0:T(8,128)(2,1)S(1)} all-to-all(bf16[32,2,16,128]{3,2,1,0:T(8,128)(2,1)S(1)} %leaf_spread.1), channel_id=1, replica_groups=mesh['layer'=2,'prow'=4,'pcol'=32] {'pcol'}, dimensions={0} | all-to-all | bytes 524288 | tf_op jit(solution)/shard_map/all_to_all | solution.py:41
  65.3 4.5 %all-to-all-start.2 = ((bf16[32,2,16,128]{3,2,1,0:T(8,128)(2,1)}), bf16[32,2,16,128]{3,2,1,0:T(8,128)(2,1)S(1)}, u32[]{:S(2)}, u32[]{:S(2)}) async-start(bf16[32,2,16,128]{3,2,1,0:T(8,128)(2,1)} %broadcast_in_dim.22), calls=%async_computation.2 | async-start | bytes 524288 | tf_op jit(solution)/shard_map/all_to_all | solution.py:41
  69.9 2.1 collective-permute-start.4
  73.2 4.2 %collective-permute-done.3.o1 = bf16[8,16,512]{2,1,0:T(8,128)(2,1)S(1)} collective-permute-done((bf16[8,16,512]{2,1,0:T(8,128)(2,1)S(1)}, bf16[8,16,512]{2,1,0:T(8,128)(2,1)S(1)}, u32[]{:S(2)}, u32[]{:S(2)}) %collective-permute-start.3) | collective-permute-done | bytes 131104 | tf_op jit(solution)/shard_map/ppermute | solution.py:29
  78.4 2.5 all-to-all-done.2.values
  80.9 2.5 copy-done.2
  84.9 16.5 %all_to_all.76 = bf16[32,16,128]{2,1,0:T(8,128)(2,1)S(1)} all-to-all(bf16[32,16,128]{2,1,0:T(8,128)(2,1)S(1)} %get-tuple-element.46), channel_id=1, replica_groups=mesh['layer'=2,'prow'=4,'pcol'=32] {'pcol'}, dimensions={0} | all-to-all | bytes 262144 | tf_op jit(solution)/shard_map/all_to_all | solution.py:41
  102.1 4.4 %all-to-all-start.4 = ((bf16[32,16,128]{2,1,0:T(8,128)(2,1)}), bf16[32,16,128]{2,1,0:T(8,128)(2,1)S(1)}, u32[]{:S(2)}, u32[]{:S(2)}) async-start(bf16[32,16,128]{2,1,0:T(8,128)(2,1)} %broadcast_in_dim.24), calls=%async_computation.4 | async-start | bytes 262144 | tf_op jit(solution)/shard_map/all_to_all | solution.py:41
  107.7 8.6 %all-to-all-done.4.values = bf16[32,16,128]{2,1,0:T(8,128)(2,1)S(1)} async-done(((bf16[32,16,128]{2,1,0:T(8,128)(2,1)}), bf16[32,16,128]{2,1,0:T(8,128)(2,1)S(1)}, u32[]{:S(2)}, u32[]{:S(2)}) %all-to-all-start.4) | async-done | bytes 131104 | tf_op jit(solution)/shard_map/all_to_all | solution.py:41
  119.0 13.9 %all_to_all.77 = bf16[32,16,128]{2,1,0:T(8,128)(2,1)S(1)} all-to-all(bf16[32,16,128]{2,1,0:T(8,128)(2,1)S(1)} %get-tuple-element.49), channel_id=1, replica_groups=mesh['layer'=2,'prow'=4,'pcol'=32] {'pcol'}, dimensions={0} | all-to-all | bytes 262144 | tf_op jit(solution)/shard_map/all_to_all | solution.py:41
  134.2 14.2 %all_to_all.78.values = bf16[32,16,128]{2,1,0:T(8,128)(2,1)S(1)} all-to-all(bf16[32,16,128]{2,1,0:T(8,128)(2,1)S(1)} %broadcast_in_dim.25), channel_id=1, replica_groups=mesh['layer'=2,'prow'=4,'pcol'=32] {'pcol'}, dimensions={0} | all-to-all | bytes 262144 | tf_op jit(solution)/shard_map/all_to_all | solution.py:41
  149.1 13.9 %all_to_all.79 = bf16[32,16,128]{2,1,0:T(8,128)(2,1)S(1)} all-to-all(bf16[32,16,128]{2,1,0:T(8,128)(2,1)S(1)} %root_solve.1), channel_id=1, replica_groups=mesh['layer'=2,'prow'=4,'pcol'=32] {'pcol'}, dimensions={0} | all-to-all | bytes 262144 | tf_op jit(solution)/shard_map/all_to_all | solution.py:41
  163.1 13.8 %all_to_all.80.root = bf16[32,16,128]{2,1,0:T(8,128)(2,1)S(1)} all-to-all(bf16[32,16,128]{2,1,0:T(8,128)(2,1)S(1)} %broadcast_in_dim.26), channel_id=1, replica_groups=mesh['layer'=2,'prow'=4,'pcol'=32] {'pcol'}, dimensions={0} | all-to-all | bytes 262144 | tf_op jit(solution)/shard_map/all_to_all | solution.py:41
  178.4 14.0 %all_to_all.81 = bf16[32,16,128]{2,1,0:T(8,128)(2,1)S(1)} all-to-all(bf16[32,16,128]{2,1,0:T(8,128)(2,1)S(1)} %top_backward.1), channel_id=1, replica_groups=mesh['layer'=2,'prow'=4,'pcol'=32] {'pcol'}, dimensions={0} | all-to-all | bytes 262144 | tf_op jit(solution)/shard_map/all_to_all | solution.py:41
  192.4 14.0 %all_to_all.82.top = bf16[32,16,128]{2,1,0:T(8,128)(2,1)} all-to-all(bf16[32,16,128]{2,1,0:T(8,128)(2,1)S(1)} %broadcast_in_dim.27), channel_id=1, replica_groups=mesh['layer'=2,'prow'=4,'pcol'=32] {'pcol'}, dimensions={0} | all-to-all | bytes 262144 | tf_op jit(solution)/shard_map/all_to_all | solution.py:41
  206.4 4.9 %middle_backward.1 = bf16[32,2,16,128]{3,2,1,0:T(8,128)(2,1)} custom-call(s32[1]{0:T(128)} %bitcast.x_ref, s32[4,2,17]{2,1,0:T(2,128)} %copy-done.5, bf16[32,16,128]{2,1,0:T(8,128)(2,1)} %copy-done.3, bf16[32,16,128]{2,1,0:T(8,128)(2,1)} %all_to_all.82.top, f32[2,16,128]{2,1,0:T(8,128)} %copy-done.8, bf16[4,2,16,128,128]{4,3,2,1,0:T(8,128)(2,1)} %bitcast.39), custom_call_target="tpu_custom_call" | custom-call | tf_op jit(solution)/shard_map/middle_backward/pallas_call | solution.py:392
  211.3 15.4 %all_to_all.83 = bf16[32,2,16,128]{3,2,1,0:T(8,128)(2,1)S(1)} all-to-all(bf16[32,2,16,128]{3,2,1,0:T(8,128)(2,1)} %middle_backward.1), channel_id=1, replica_groups=mesh['layer'=2,'prow'=4,'pcol'=32] {'pcol'}, dimensions={0} | all-to-all | bytes 524288 | tf_op jit(solution)/shard_map/all_to_all | solution.py:41
  227.6 4.5 %all-to-all-start.12 = ((bf16[32,2,16,128]{3,2,1,0:T(8,128)(2,1)}), bf16[32,2,16,128]{3,2,1,0:T(8,128)(2,1)S(1)}, u32[]{:S(2)}, u32[]{:S(2)}) async-start(bf16[32,2,16,128]{3,2,1,0:T(8,128)(2,1)} %broadcast_in_dim.28), calls=%async_computation.12 | async-start | bytes 524288 | tf_op jit(solution)/shard_map/all_to_all | solution.py:41
  232.8 3.3 %collective-permute-start.8 = (bf16[8,2,16,128]{3,2,1,0:T(8,128)(2,1)S(1)}, bf16[8,2,16,128]{3,2,1,0:T(8,128)(2,1)S(1)}, u32[]{:S(2)}, u32[]{:S(2)}) collective-permute-start(bf16[8,2,16,128]{3,2,1,0:T(8,128)(2,1)S(1)} %get-tuple-element.67), channel_id=1, source_target_pairs={{0,64},{32,96},{64,0},{96,32},{1,65},{33,97},{65,1},{97,33},{2,66}... | collective-permute-start | bytes 196616 | tf_op jit(solution)/shard_map/ppermute | solution.py:29
  236.2 4.6 %leaf_down.1.fwd = f32[4,16,128]{2,1,0:T(8,128)} custom-call(s32[1]{0:T(128)} %bitcast.x_ref, s32[4,2,17]{2,1,0:T(2,128)} %copy-done.5, bf16[32,16,128]{2,1,0:T(8,128)(2,1)} %copy-done.3, bf16[32,16,128]{2,1,0:T(8,128)(2,1)} %all_to_all.82.top, f32[4,16,128]{2,1,0:T(8,128)} %get-tuple-element.51.fwd, bf16[4,4,20,128,128]{4,3,2,1,0:T(8,128)(2,1)} %bitcast.42, ...), custom_call_target="tpu_custom_call" | custom-call | tf_op jit(solution)/shard_map/leaf_down/pallas_call | solution.py:411
  240.8 2.3 all-to-all-done.12.middle
  243.8 6.3 %leaf_backward.1 = bf16[4,32,16,128]{3,2,1,0:T(8,128)(2,1)} custom-call(s32[1]{0:T(128)} %bitcast.x_ref, s32[4,2,17]{2,1,0:T(2,128)} %copy-done.5, bf16[32,2,16,128]{3,2,1,0:T(8,128)(2,1)} %copy-done.9, f32[4,16,128]{2,1,0:T(8,128)} %leaf_down.1.fwd, bf16[4,4,20,128,128]{4,3,2,1,0:T(8,128)(2,1)} %bitcast.44), custom_call_target="tpu_custom_call" | custom-call | tf_op jit(solution)/shard_map/leaf_backward/pallas_call | solution.py:437
  250.1 10.3 %all-to-all-start.13 = ((bf16[128,16,128]{2,1,0:T(8,128)(2,1)}), bf16[128,16,128]{2,1,0:T(8,128)(2,1)S(1)}, u32[]{:S(2)}, u32[]{:S(2)}) async-start(bf16[128,16,128]{2,1,0:T(8,128)(2,1)} %bitcast.48), calls=%async_computation.13 | async-start | bytes 1048576 | tf_op jit(solution)/shard_map/all_to_all | solution.py:540
  263.1 3.1 %collective-permute-start.11 = (bf16[8,2,16,128]{3,2,1,0:T(8,128)(2,1)S(1)}, bf16[8,2,16,128]{3,2,1,0:T(8,128)(2,1)S(1)}, u32[]{:S(2)}, u32[]{:S(2)}) collective-permute-start(bf16[8,2,16,128]{3,2,1,0:T(8,128)(2,1)S(1)} %get-tuple-element.61), channel_id=1, source_target_pairs={{0,64},{32,96},{64,0},{96,32},{1,65},{33,97},{65,1},{97,33},{2,66}... | collective-permute-start | bytes 196616 | tf_op jit(solution)/shard_map/ppermute | solution.py:29
  267.4 8.9 %all-to-all-done.13 = bf16[128,16,128]{2,1,0:T(8,128)(2,1)S(1)} async-done(((bf16[128,16,128]{2,1,0:T(8,128)(2,1)}), bf16[128,16,128]{2,1,0:T(8,128)(2,1)S(1)}, u32[]{:S(2)}, u32[]{:S(2)}) %all-to-all-start.13) | async-done | bytes 524320 | tf_op jit(solution)/shard_map/all_to_all | solution.py:540
  276.6 17.8 %all_to_all.84.refs_8_ = bf16[32,4,16,128]{3,2,1,0:T(8,128)(2,1)S(1)} all-to-all(bf16[32,4,16,128]{3,2,1,0:T(8,128)(2,1)S(1)} %broadcast_in_dim.29), channel_id=1, replica_groups=mesh['layer'=2,'prow'=4,'pcol'=32] {'pcol'}, dimensions={0} | all-to-all | bytes 1048576 | tf_op jit(solution)/shard_map/all_to_all | solution.py:41
  (91 shorter events, 28.6 us)
Async XLA Ops:
  7.2 73.7 %all-gather.7.cloned.1.call-start = ((), (), s32[]{:S(2)}) async-start(), calls=%async_computation.15 | async-start | bytes 5242880 | tf_op jit(solution)/shard_map/all_gather | solution.py:483
  11.4 12.6 %all-to-all-start = ((bf16[4,25,16,128]{3,2,1,0:T(8,128)(2,1)}), bf16[4,25,16,128]{3,2,1,0:T(8,128)(2,1)S(1)}, u32[]{:S(2)}, u32[]{:S(2)}) async-start(bf16[4,25,16,128]{3,2,1,0:T(8,128)(2,1)} %get-tuple-element.31), calls=%async_computation | async-start | bytes 819200 | tf_op jit(solution)/shard_map/all_to_all | solution.py:502
  15.7 92.0 %all-gather.9.cloned.1.call-start = ((), (), s32[]{:S(2)}) async-start(), calls=%async_computation.16 | async-start | bytes 3276800 | tf_op jit(solution)/shard_map/all_gather | solution.py:483
  29.6 4.3 %copy-start.15 = (bf16[4,16,512]{2,1,0:T(8,128)(2,1)S(1)}, bf16[4,16,512]{2,1,0:T(8,128)(2,1)}, u32[]{:S(2)}) copy-start(bf16[4,16,512]{2,1,0:T(8,128)(2,1)} %get-tuple-element.40) | copy-start | bytes 196612
  29.6 11.9 %copy-start.7 = (bf16[4,16,512]{2,1,0:T(8,128)(2,1)S(1)}, bf16[4,16,512]{2,1,0:T(8,128)(2,1)}, u32[]{:S(2)}) copy-start(bf16[4,16,512]{2,1,0:T(8,128)(2,1)} %get-tuple-element.37.c0) | copy-start | bytes 196612
  30.4 39.4 %copy-start.14 = (bf16[8,16,512]{2,1,0:T(8,128)(2,1)S(1)}, bf16[8,16,512]{2,1,0:T(8,128)(2,1)}, u32[]{:S(2)}) copy-start(bf16[8,16,512]{2,1,0:T(8,128)(2,1)} %get-tuple-element.43) | copy-start | bytes 393220
  30.4 39.5 %copy-start.13 = (bf16[8,16,512]{2,1,0:T(8,128)(2,1)S(1)}, bf16[8,16,512]{2,1,0:T(8,128)(2,1)}, u32[]{:S(2)}) copy-start(bf16[8,16,512]{2,1,0:T(8,128)(2,1)} %get-tuple-element.44) | copy-start | bytes 393220
  30.4 41.6 %copy-start.12 = (bf16[8,16,512]{2,1,0:T(8,128)(2,1)S(1)}, bf16[8,16,512]{2,1,0:T(8,128)(2,1)}, u32[]{:S(2)}) copy-start(bf16[8,16,512]{2,1,0:T(8,128)(2,1)} %get-tuple-element.45) | copy-start | bytes 393220
  30.4 50.4 %copy-start.6 = (bf16[8,16,512]{2,1,0:T(8,128)(2,1)S(1)}, bf16[8,16,512]{2,1,0:T(8,128)(2,1)}, u32[]{:S(2)}) copy-start(bf16[8,16,512]{2,1,0:T(8,128)(2,1)} %get-tuple-element.42.o0) | copy-start | bytes 393220
  30.5 205.7 %all-gather.11.cloned.1.call-start = ((), (), s32[]{:S(2)}) async-start(), calls=%async_computation.17 | async-start | bytes 13107200 | tf_op jit(solution)/shard_map/all_gather | solution.py:483
  31.2 7.5 %collective-permute-start = (bf16[4,16,512]{2,1,0:T(8,128)(2,1)S(1)}, bf16[4,16,512]{2,1,0:T(8,128)(2,1)S(1)}, u32[]{:S(2)}, u32[]{:S(2)}) collective-permute-start(bf16[4,16,512]{2,1,0:T(8,128)(2,1)S(1)} %copy-done.17), channel_id=1, source_target_pairs={{0,32},{32,64},{64,96},{96,0},{1,33},{33,65},{65,97},{97,1},{2,34}... | collective-permute-start | bytes 196616 | tf_op jit(solution)/shard_map/ppermute | solution.py:29
  31.8 8.3 %collective-permute-start.1 = (bf16[4,16,512]{2,1,0:T(8,128)(2,1)S(1)}, bf16[4,16,512]{2,1,0:T(8,128)(2,1)S(1)}, u32[]{:S(2)}, u32[]{:S(2)}) collective-permute-start(bf16[4,16,512]{2,1,0:T(8,128)(2,1)S(1)} %copy-done.16), channel_id=1, source_target_pairs={{0,64},{32,96},{64,0},{96,32},{1,65},{33,97},{65,1},{97,33},{2,66}... | collective-permute-start | bytes 196616 | tf_op jit(solution)/shard_map/ppermute | solution.py:29
  33.9 7.6 %collective-permute-start.2 = (bf16[4,16,512]{2,1,0:T(8,128)(2,1)S(1)}, bf16[4,16,512]{2,1,0:T(8,128)(2,1)S(1)}, u32[]{:S(2)}, u32[]{:S(2)}) collective-permute-start(bf16[4,16,512]{2,1,0:T(8,128)(2,1)S(1)} %copy-done.15), channel_id=1, source_target_pairs={{0,96},{32,0},{64,32},{96,64},{1,97},{33,1},{65,33},{97,65},{2,98}... | collective-permute-start | bytes 196616 | tf_op jit(solution)/shard_map/ppermute | solution.py:29
  35.3 141.6 %copy-start.5 = (s32[4,2,17]{2,1,0:T(2,128)}, s32[4,2,17]{2,1,0:T(2,128)S(1)}, u32[]{:S(2)}) copy-start(s32[4,2,17]{2,1,0:T(2,128)S(1)} %fusion.7.table) | copy-start | bytes 1636
  65.3 15.5 %all-to-all-start.2 = ((bf16[32,2,16,128]{3,2,1,0:T(8,128)(2,1)}), bf16[32,2,16,128]{3,2,1,0:T(8,128)(2,1)S(1)}, u32[]{:S(2)}, u32[]{:S(2)}) async-start(bf16[32,2,16,128]{3,2,1,0:T(8,128)(2,1)} %broadcast_in_dim.22), calls=%async_computation.2 | async-start | bytes 524288 | tf_op jit(solution)/shard_map/all_to_all | solution.py:41
  69.8 7.7 %collective-permute-start.3 = (bf16[8,16,512]{2,1,0:T(8,128)(2,1)S(1)}, bf16[8,16,512]{2,1,0:T(8,128)(2,1)S(1)}, u32[]{:S(2)}, u32[]{:S(2)}) collective-permute-start(bf16[8,16,512]{2,1,0:T(8,128)(2,1)S(1)} %copy-done.14), channel_id=1, source_target_pairs={{0,32},{32,64},{64,96},{96,0},{1,33},{33,65},{65,97},{97,1},{2,34}... | collective-permute-start | bytes 393224 | tf_op jit(solution)/shard_map/ppermute | solution.py:29
  69.9 7.6 %collective-permute-start.4 = (bf16[8,16,512]{2,1,0:T(8,128)(2,1)S(1)}, bf16[8,16,512]{2,1,0:T(8,128)(2,1)S(1)}, u32[]{:S(2)}, u32[]{:S(2)}) collective-permute-start(bf16[8,16,512]{2,1,0:T(8,128)(2,1)S(1)} %copy-done.13), channel_id=1, source_target_pairs={{0,64},{32,96},{64,0},{96,32},{1,65},{33,97},{65,1},{97,33},{2,66}... | collective-permute-start | bytes 393224 | tf_op jit(solution)/shard_map/ppermute | solution.py:29
  72.0 6.4 %collective-permute-start.5 = (bf16[8,16,512]{2,1,0:T(8,128)(2,1)S(1)}, bf16[8,16,512]{2,1,0:T(8,128)(2,1)S(1)}, u32[]{:S(2)}, u32[]{:S(2)}) collective-permute-start(bf16[8,16,512]{2,1,0:T(8,128)(2,1)S(1)} %copy-done.12), channel_id=1, source_target_pairs={{0,96},{32,0},{64,32},{96,64},{1,97},{33,1},{65,33},{97,65},{2,98}... | collective-permute-start | bytes 393224 | tf_op jit(solution)/shard_map/ppermute | solution.py:29
  84.9 16.5 %copy-start.8 = (f32[2,16,128]{2,1,0:T(8,128)}, f32[2,16,128]{2,1,0:T(8,128)S(1)}, u32[]{:S(2)}) copy-start(f32[2,16,128]{2,1,0:T(8,128)S(1)} %get-tuple-element.57.fwd) | copy-start | bytes 49156
  102.1 14.2 %all-to-all-start.4 = ((bf16[32,16,128]{2,1,0:T(8,128)(2,1)}), bf16[32,16,128]{2,1,0:T(8,128)(2,1)S(1)}, u32[]{:S(2)}, u32[]{:S(2)}) async-start(bf16[32,16,128]{2,1,0:T(8,128)(2,1)} %broadcast_in_dim.24), calls=%async_computation.4 | async-start | bytes 262144 | tf_op jit(solution)/shard_map/all_to_all | solution.py:41
  118.0 30.5 %copy-start.1 = (bf16[80,128,128]{2,1,0:T(8,128)(2,1)S(1)}, bf16[80,128,128]{2,1,0:T(8,128)(2,1)}, u32[]{:S(2)}) copy-start(bf16[80,128,128]{2,1,0:T(8,128)(2,1)} %all-gather.9.cloned.1.call-done) | copy-start | bytes 7864324
  132.9 1.3 collective-permute-start.6
  206.4 25.7 %copy-start.4 = (bf16[32,16,128]{2,1,0:T(8,128)(2,1)S(1)}, bf16[32,16,128]{2,1,0:T(8,128)(2,1)}, u32[]{:S(2)}) copy-start(bf16[32,16,128]{2,1,0:T(8,128)(2,1)} %copy-done.3) | copy-start | bytes 393220
  206.4 25.7 %copy-start.10 = (bf16[32,16,128]{2,1,0:T(8,128)(2,1)S(1)}, bf16[32,16,128]{2,1,0:T(8,128)(2,1)}, u32[]{:S(2)}) copy-start(bf16[32,16,128]{2,1,0:T(8,128)(2,1)} %all_to_all.82.top) | copy-start | bytes 393220
  227.6 15.5 %all-to-all-start.12 = ((bf16[32,2,16,128]{3,2,1,0:T(8,128)(2,1)}), bf16[32,2,16,128]{3,2,1,0:T(8,128)(2,1)S(1)}, u32[]{:S(2)}, u32[]{:S(2)}) async-start(bf16[32,2,16,128]{3,2,1,0:T(8,128)(2,1)} %broadcast_in_dim.28), calls=%async_computation.12 | async-start | bytes 524288 | tf_op jit(solution)/shard_map/all_to_all | solution.py:41
  232.2 8.6 %collective-permute-start.7 = (bf16[8,2,16,128]{3,2,1,0:T(8,128)(2,1)S(1)}, bf16[8,2,16,128]{3,2,1,0:T(8,128)(2,1)S(1)}, u32[]{:S(2)}, u32[]{:S(2)}) collective-permute-start(bf16[8,2,16,128]{3,2,1,0:T(8,128)(2,1)S(1)} %get-tuple-element.66), channel_id=1, source_target_pairs={{0,32},{32,64},{64,96},{96,0},{1,33},{33,65},{65,97},{97,1},{2,34}... | collective-permute-start | bytes 196616 | tf_op jit(solution)/shard_map/ppermute | solution.py:29
  232.8 7.9 %collective-permute-start.8 = (bf16[8,2,16,128]{3,2,1,0:T(8,128)(2,1)S(1)}, bf16[8,2,16,128]{3,2,1,0:T(8,128)(2,1)S(1)}, u32[]{:S(2)}, u32[]{:S(2)}) collective-permute-start(bf16[8,2,16,128]{3,2,1,0:T(8,128)(2,1)S(1)} %get-tuple-element.67), channel_id=1, source_target_pairs={{0,64},{32,96},{64,0},{96,32},{1,65},{33,97},{65,1},{97,33},{2,66}... | collective-permute-start | bytes 196616 | tf_op jit(solution)/shard_map/ppermute | solution.py:29
  236.2 4.6 %collective-permute-start.9 = (bf16[8,2,16,128]{3,2,1,0:T(8,128)(2,1)S(1)}, bf16[8,2,16,128]{3,2,1,0:T(8,128)(2,1)S(1)}, u32[]{:S(2)}, u32[]{:S(2)}) collective-permute-start(bf16[8,2,16,128]{3,2,1,0:T(8,128)(2,1)S(1)} %get-tuple-element.64), channel_id=1, source_target_pairs={{0,96},{32,0},{64,32},{96,64},{1,97},{33,1},{65,33},{97,65},{2,98}... | collective-permute-start | bytes 196616 | tf_op jit(solution)/shard_map/ppermute | solution.py:29
  250.1 26.3 %all-to-all-start.13 = ((bf16[128,16,128]{2,1,0:T(8,128)(2,1)}), bf16[128,16,128]{2,1,0:T(8,128)(2,1)S(1)}, u32[]{:S(2)}, u32[]{:S(2)}) async-start(bf16[128,16,128]{2,1,0:T(8,128)(2,1)} %bitcast.48), calls=%async_computation.13 | async-start | bytes 1048576 | tf_op jit(solution)/shard_map/all_to_all | solution.py:540
  261.4 15.0 %collective-permute-start.10 = (bf16[8,2,16,128]{3,2,1,0:T(8,128)(2,1)S(1)}, bf16[8,2,16,128]{3,2,1,0:T(8,128)(2,1)S(1)}, u32[]{:S(2)}, u32[]{:S(2)}) collective-permute-start(bf16[8,2,16,128]{3,2,1,0:T(8,128)(2,1)S(1)} %get-tuple-element.62), channel_id=1, source_target_pairs={{0,32},{32,64},{64,96},{96,0},{1,33},{33,65},{65,97},{97,1},{2,34}... | collective-permute-start | bytes 196616 | tf_op jit(solution)/shard_map/ppermute | solution.py:29
  263.1 13.4 %collective-permute-start.11 = (bf16[8,2,16,128]{3,2,1,0:T(8,128)(2,1)S(1)}, bf16[8,2,16,128]{3,2,1,0:T(8,128)(2,1)S(1)}, u32[]{:S(2)}, u32[]{:S(2)}) collective-permute-start(bf16[8,2,16,128]{3,2,1,0:T(8,128)(2,1)S(1)} %get-tuple-element.61), channel_id=1, source_target_pairs={{0,64},{32,96},{64,0},{96,32},{1,65},{33,97},{65,1},{97,33},{2,66}... | collective-permute-start | bytes 196616 | tf_op jit(solution)/shard_map/ppermute | solution.py:29
  266.2 10.3 %collective-permute-start.12 = (bf16[8,2,16,128]{3,2,1,0:T(8,128)(2,1)S(1)}, bf16[8,2,16,128]{3,2,1,0:T(8,128)(2,1)S(1)}, u32[]{:S(2)}, u32[]{:S(2)}) collective-permute-start(bf16[8,2,16,128]{3,2,1,0:T(8,128)(2,1)S(1)} %get-tuple-element.60), channel_id=1, source_target_pairs={{0,96},{32,0},{64,32},{96,64},{1,97},{33,1},{65,33},{97,65},{2,98}... | collective-permute-start | bytes 196616 | tf_op jit(solution)/shard_map/ppermute | solution.py:29
  (7 other events, 11.1 us)
Sparse Core Ops, SparseCore 0:
  11.5 56.1 all-gather.6
  69.5 38.0 all-gather.8
  109.5 103.5 all-gather.10
